TPU v7x, 512 devices: a whole 4x8x8 slice. The times are simulated.
512 devices in a mesh: ctx: 64 (over x, y_lo, z), tp: 8 (over y_hi, core).
Axes of the slice: x: 4, y: 8 (y_hi: 4, y_lo: 2; y = y_hi * 2 + y_lo), z: 8, core: 2. Of those that a mesh axis runs over, the one named last changes fastest.
Arguments:
- query_vectors: bfloat16 [8192, 3072], P(('ctx', 'tp')), may hold values from -20 to 20
- key_vectors: bfloat16 [8192, 3072], P(('ctx', 'tp')), may hold values from -20 to 20
- value_vectors: bfloat16 [8192, 3072], P(('ctx', 'tp')), may hold values from -6 to 6
- out_weight: bfloat16 [3072, 5120], P('tp'), may hold values from -0.109375 to 0.109375
Outputs:
- mixed: bfloat16 [8192, 5120], P(('ctx', 'tp'))
All inputs are finite; a program needn't handle non-finite values.
Results may differ from a plain program's by a relative error of at most 0.027.
Values may be sent and summed in bfloat16 or wider, within the bound.
A program may use at most 64 MiB of HBM per device.

v0:
```python
import math

import jax
import jax.numpy as jnp
from jax import lax
from jax.sharding import PartitionSpec as P

HD = 128


def fresh_state(row_count, head_count):
    row_peak = jnp.full((row_count, head_count), -1e30, jnp.float32)
    row_total = jnp.zeros((row_count, head_count), jnp.float32)
    weighted = jnp.zeros((row_count, head_count, HD), jnp.float32)
    return (row_peak, row_total, weighted)


def attend_piece(running, query_heads, key_rows, value_rows, score_scale):
    head_count = query_heads.shape[1]
    piece_rows = key_rows.shape[0]
    sub_rows = math.gcd(piece_rows, 256)
    sub_count = piece_rows // sub_rows
    key_parts = key_rows.reshape(sub_count, sub_rows, head_count, HD)
    value_parts = value_rows.reshape(sub_count, sub_rows, head_count, HD)

    def absorb(current, part_pair):
        row_peak, row_total, weighted = current
        key_part, value_part = part_pair
        scores = (
            jnp.einsum("ihd,jhd->ihj", query_heads, key_part, preferred_element_type=jnp.float32)
            * score_scale
        )
        new_peak = jnp.maximum(row_peak, jnp.max(scores, axis=-1))
        weights_low = jnp.exp(scores - new_peak[..., None]).astype(jnp.bfloat16)
        shrink = jnp.exp(row_peak - new_peak)
        row_total = row_total * shrink + jnp.sum(weights_low.astype(jnp.float32), axis=-1)
        weighted = weighted * shrink[..., None] + jnp.einsum(
            "ihj,jhd->ihd", weights_low, value_part, preferred_element_type=jnp.float32
        )
        return ((new_peak, row_total, weighted), None)

    finished, unused = lax.scan(absorb, running, (key_parts, value_parts))
    return finished


def local(query_vectors, key_vectors, value_vectors, out_weight):
    score_scale = 1.0 / math.sqrt(HD)
    tp_count = lax.axis_size("tp")
    all_queries = lax.all_gather(query_vectors, "tp", axis=0, tiled=True)
    row_count = all_queries.shape[0]
    head_count = all_queries.shape[1] // HD
    query_heads = all_queries.reshape(row_count, head_count, HD)
    row_peak, row_total, weighted = attend_piece(
        fresh_state(row_count, head_count),
        query_heads,
        lax.all_gather(key_vectors, "ctx", axis=0, tiled=True),
        lax.all_gather(value_vectors, "ctx", axis=0, tiled=True),
        score_scale,
    )
    top_peak = lax.pmax(row_peak, "tp")
    factor = jnp.exp(row_peak - top_peak)
    all_totals = lax.psum(row_total * factor, "tp")
    numerator = (weighted * factor[..., None]).reshape(row_count, head_count * HD)
    own_numerator = lax.psum_scatter(
        numerator.astype(jnp.bfloat16), "tp", scatter_dimension=1, tiled=True
    ).astype(jnp.float32)
    own_heads = head_count // tp_count
    own_totals = lax.dynamic_slice_in_dim(
        all_totals, lax.axis_index("tp") * own_heads, own_heads, 1
    )
    attended = (own_numerator.reshape(row_count, own_heads, HD) / own_totals[..., None]).astype(
        jnp.bfloat16
    )
    attended = attended.reshape(row_count, own_heads * HD)
    return lax.psum_scatter(
        jnp.dot(attended, out_weight, preferred_element_type=jnp.float32).astype(jnp.bfloat16),
        "tp",
        scatter_dimension=0,
        tiled=True,
    )


def solution(mesh):
    return jax.shard_map(
        local,
        mesh=mesh,
        in_specs=(
            P(("ctx", "tp"), None),
            P(("ctx", "tp"), None),
            P(("ctx", "tp"), None),
            P("tp", None),
        ),
        out_specs=P(("ctx", "tp"), None),
        check_vma=False,
    )
```

profile of v0, /device:TPU:1, one launch (start us, length us, event | category | flops | bytes accessed | tf_op | source)
XLA Modules:
  0.0 810.6 jit_solution(7666811695530442042)
XLA Ops:
  8.1 22.4 %all_gather.10 = bf16[128,3072]{1,0:T(8,128)(2,1)S(1)} all-gather(bf16[16,3072]{1,0:T(8,128)(2,1)} %param.6), channel_id=1, replica_groups=mesh['ctx'=64,'tp'=8] {'tp'}, dimensions={0}, use_global_device_ids=true | all-gather | bytes 884736 | tf_op jit(solution)/shard_map/all_gather | solution.py:49
  32.0 254.9 %all-gather.5.cloned.1.call-done = bf16[1024,3072]{1,0:T(8,128)(2,1)} async-done(((bf16[16,3072]{1,0:T(8,128)(2,1)}), bf16[1024,3072]{1,0:T(8,128)(2,1)}) %all-gather.5.cloned.1.call-update) | async-done | bytes 6291472 | tf_op jit(solution)/shard_map/all_gather | solution.py:57
  286.9 7.4 copy.20
  294.2 302.0 %all-gather.3.cloned.1.call-done = bf16[1024,3072]{1,0:T(8,128)(2,1)} async-done(((bf16[16,3072]{1,0:T(8,128)(2,1)}), bf16[1024,3072]{1,0:T(8,128)(2,1)}) %all-gather.3.cloned.1.call-update) | async-done | bytes 6291472 | tf_op jit(solution)/shard_map/all_gather | solution.py:56
  596.2 7.4 copy.19
  603.6 46.2 %while.15 = (s32[]{:T(128)}, f32[128,24]{0,1:T(8,128)S(1)}, f32[128,24]{0,1:T(8,128)S(1)}, f32[128,24,128]{0,2,1:T(8,128)}, bf16[4,256,24,128]{3,2,1,0:T(8,128)(...) while((s32[]{:T(128)}, f32[128,24]{0,1:T(8,128)S(1)}, ...), condition=%wide.region_3.4_spmd.clone, body=%wide.region_0.3_spmd.clone.sunk | while | flops 411712512 | bytes 29294728 | solution.py:42
  603.6 3.6 constant_dynamic-slice_fusion.4
  608.4 2.9 copy.28
  611.3 3.5 bitcast_add_fusion.2
  614.8 3.6 constant_dynamic-slice_fusion.4
  619.6 2.9 copy.28
  622.5 3.9 bitcast_add_fusion.2
  626.5 3.6 constant_dynamic-slice_fusion.4
  631.3 2.9 copy.28
  634.2 3.9 bitcast_add_fusion.2
  638.1 3.6 constant_dynamic-slice_fusion.4
  643.0 2.9 copy.28
  645.8 3.9 bitcast_add_fusion.2
  649.8 66.0 %pmax.7 = f32[128,24]{0,1:T(8,128)S(1)} all-reduce(f32[128,24]{0,1:T(8,128)S(1)} %get-tuple-element.45), channel_id=1, replica_groups=mesh['ctx'=64,'tp'=8] {'tp'}, use_global_device_ids=true, to_apply=%region_4.5 | all-reduce | flops 3072 | bytes 24576 | tf_op jit(solution)/shard_map/pmax | solution.py:60
  715.8 2.5 multiply_convert_fusion
  718.4 27.3 %psum.7 = f32[128,24]{0,1:T(8,128)S(1)} all-reduce(f32[128,24]{0,1:T(8,128)S(1)} %get-tuple-element.101), channel_id=1, replica_groups=mesh['ctx'=64,'tp'=8] {'tp'}, use_global_device_ids=true, to_apply=%region_6.7 | all-reduce | flops 3072 | bytes 24576 | tf_op jit(solution)/shard_map/psum | solution.py:62
  745.7 11.9 %reduce-scatter.3.cloned.1.call-done = bf16[128,384]{0,1:T(8,128)(2,1)} async-done(((bf16[128,3072]{0,1:T(8,128)(2,1)}), bf16[128,384]{0,1:T(8,128)(2,1)}) %reduce-scatter.3.cloned.1.call-update) | async-done | bytes 98320 | tf_op jit(solution)/shard_map/reduce_scatter | solution.py:64
  758.5 4.1 convolution_convert_fusion
  762.6 41.5 %reduce-scatter.5.cloned.1.call-done = bf16[16,5120]{1,0:T(8,128)(2,1)} async-done(((bf16[128,5120]{1,0:T(8,128)(2,1)}), bf16[16,5120]{1,0:T(8,128)(2,1)}) %reduce-scatter.5.cloned.1.call-update) | async-done | bytes 163856 | tf_op jit(solution)/shard_map/reduce_scatter | solution.py:75
  (44 shorter events, 8.7 us)
Async XLA Ops:
  6.5 280.3 %all-gather.5.cloned.1.call-start = ((), (), s32[]{:S(2)}) async-start(), calls=%async_computation.3 | async-start | bytes 6389760 | tf_op jit(solution)/shard_map/all_gather | solution.py:57
  7.3 588.9 %all-gather.3.cloned.1.call-start = ((), (), s32[]{:S(2)}) async-start(), calls=%async_computation.2 | async-start | bytes 6389760 | tf_op jit(solution)/shard_map/all_gather | solution.py:56
  8.0 749.6 %reduce-scatter.3.cloned.1.call-start = ((), (), s32[]{:S(2)}) async-start(), calls=%async_computation.4 | async-start | bytes 884736 | tf_op jit(solution)/shard_map/reduce_scatter | solution.py:64
  603.6 3.6 copy-start
  614.8 3.6 copy-start
  626.5 3.6 copy-start
  638.1 3.6 copy-start
  718.3 85.8 %reduce-scatter.5.cloned.1.call-start = ((), (), s32[]{:S(2)}) async-start(), calls=%async_computation.5 | async-start | bytes 1474560 | tf_op jit(solution)/shard_map/reduce_scatter | solution.py:75
Sparse Core Ops, SparseCore 0:
  9.4 277.3 all-gather.4
  288.9 307.2 all-gather.2
  718.4 39.1 reduce-scatter.2
  762.7 41.3 reduce-scatter.4
where the time goes:
time: 812 us; the launch traced here: 811 us
  waiting for transfers between devices  612 us (75%)
  blocking collectives  116 us (14%)
  local copies, waits for them, and re-layouts  42.5 us (5%)
  matrix products  21.7 us (3%)
  between operations  13.2 us (2%)
    all_gather x1, waiting for transfers between devices, local(): lax.all_gather(key_vectors, 'ctx', axis=0, tiled=True)  302 us
    all_gather x1, waiting for transfers between devices, local(): lax.all_gather(value_vectors, 'ctx', axis=0, tiled=True)  255 us
    pmax x1, blocking collectives, local(): top_peak = lax.pmax(row_peak, 'tp')  66 us
    reduce_scatter x1, waiting for transfers between devices, local(): lax.psum_scatter(jnp.dot(attended, out_weight, preferred_element_type=jnp...  41.5 us
    psum x1, blocking collectives, local(): all_totals = lax.psum(row_total * factor, 'tp')  27.3 us
    dynamic_slice x8, local copies, waits for them, and re-layouts, attend_piece(): finished, unused = lax.scan(absorb, running, (key_parts, value_parts))  26.1 us
    all_gather x1, blocking collectives, local(): all_queries = lax.all_gather(query_vectors, 'tp', axis=0, tiled=True)  22.4 us
  transfers between devices with their start and end apart: 4, of which 4 were waited for; matrix products, arithmetic and copies ran while one was open for 1% of the time, Pallas kernels for 0%

commit v1 on v0

v1 whole, which is shorter than its diff:
```python
import math

import jax
import jax.numpy as jnp
import numpy as np
from jax import lax
from jax.sharding import Mesh
from jax.sharding import PartitionSpec as P

HD = 128
KEY_SPLIT = 8


def attend_local(query_heads, key_heads, value_heads, score_scale):
    scores = (
        jnp.einsum("hid,hjd->hij", query_heads, key_heads, preferred_element_type=jnp.float32)
        * score_scale
    )
    row_peak = jnp.max(scores, axis=-1)
    weights_low = jnp.exp(scores - row_peak[..., None]).astype(jnp.bfloat16)
    row_total = jnp.sum(weights_low.astype(jnp.float32), axis=-1)
    weighted = jnp.einsum(
        "hij,hjd->hid", weights_low, value_heads, preferred_element_type=jnp.float32
    )
    return row_peak, row_total, weighted


def local(query_vectors, key_vectors, value_vectors, out_weight):
    score_scale = 1.0 / math.sqrt(HD)
    tp_count = lax.axis_size("tp")
    own_heads = query_vectors.shape[1] // HD // tp_count

    def own_group(rows):
        return lax.all_to_all(rows, "tp", 1, 0, tiled=True)

    def heads_major(rows):
        return rows.reshape(rows.shape[0], own_heads, HD).transpose(1, 0, 2)

    block_q = own_group(query_vectors)
    block_k = own_group(key_vectors)
    block_v = own_group(value_vectors)
    block_rows = block_q.shape[0]
    query_heads = heads_major(lax.all_gather(block_q, "ca", axis=0, tiled=True))
    key_heads = heads_major(lax.all_gather(block_k, "cz", axis=0, tiled=True))
    value_heads = heads_major(lax.all_gather(block_v, "cz", axis=0, tiled=True))

    row_peak, row_total, weighted = attend_local(query_heads, key_heads, value_heads, score_scale)
    top_peak = lax.pmax(row_peak, "ca")
    factor = jnp.exp(row_peak - top_peak)
    own_totals = lax.psum_scatter(row_total * factor, "ca", scatter_dimension=1, tiled=True)
    numerator = (weighted * factor[..., None]).astype(jnp.bfloat16)
    own_numerator = lax.psum_scatter(numerator, "ca", scatter_dimension=1, tiled=True)
    attended = (own_numerator.astype(jnp.float32) / own_totals[..., None]).astype(jnp.bfloat16)
    attended = attended.transpose(1, 0, 2).reshape(block_rows, own_heads * HD)
    return lax.psum_scatter(
        jnp.dot(attended, out_weight, preferred_element_type=jnp.float32).astype(jnp.bfloat16),
        "tp",
        scatter_dimension=0,
        tiled=True,
    )


def solution(mesh):
    ctx_count, tp_count = mesh.devices.shape
    split_mesh = Mesh(
        mesh.devices.reshape(ctx_count // KEY_SPLIT, KEY_SPLIT, tp_count), ("ca", "cz", "tp")
    )
    rows = P(("ca", "cz", "tp"), None)
    return jax.shard_map(
        local,
        mesh=split_mesh,
        in_specs=(rows, rows, rows, P("tp", None)),
        out_specs=rows,
        check_vma=False,
    )
```

time: 812 us -> 310 us (0.38)
  waiting for transfers between devices: 612 us -> 138 us
  local copies, waits for them, and re-layouts: 42.5 us -> 13.2 us
  starting transfers between devices: 0.12 us -> 26.3 us
  blocking collectives: 116 us -> 99.5 us
    all_gather x2 -> x0, waiting for transfers between devices: 557 us -> none  [the longest x1 302 us: local(): lax.all_gather(key_vectors, 'ctx', axis=0, tiled=True)]
    all_gather x1 -> x3, blocking collectives: 22.4 us -> 72.7 us  [the longest x1 26.6 us: local(): query_heads = heads_major(lax.all_gather(block_q, 'ca', axis=0, tiled=True))]
    unnamed x4, waiting for transfers between devices: 1.44 us -> 43.3 us
    pmax x1, blocking collectives: 66 us -> 26.8 us  [local(): top_peak = lax.pmax(row_peak, 'ca')]
    reduce_scatter x1, waiting for transfers between devices: 11.9 us -> 45.8 us  [local(): lax.psum_scatter(numerator, 'ca', scatter_dimension=1, tiled=True)]
    psum x1 -> x0, blocking collectives: 27.3 us -> none  [local(): all_totals = lax.psum(row_total * factor, 'tp')]
    all_to_all x0 -> x3, starting transfers between devices: none -> 26.2 us  [own_group(): return lax.all_to_all(rows, 'tp', 1, 0, tiled=True)]
    dynamic_slice x9 -> x0, local copies, waits for them, and re-layouts: 26.1 us -> none  [the longest x8 26.1 us: attend_piece(): finished, unused = lax.scan(absorb, running, (key_parts, value_parts))]
  transfers between devices with their start and end apart: 4 -> 6, of which waited for: 4 -> 4; matrix products, arithmetic and copies ran while one was open for 1% -> 6% of each run, Pallas kernels for 0% -> 0%
where the time goes in v1:
time: 310 us; the launch traced here: 308 us
  waiting for transfers between devices  138 us (45%)
  blocking collectives  99.5 us (32%)
  starting transfers between devices  26.3 us (8%)
  matrix products  14.4 us (5%)
  local copies, waits for them, and re-layouts  13.2 us (4%)
  between operations  13.2 us (4%)
  other arithmetic  3.11 us (1%)
    reduce_scatter x1, waiting for transfers between devices, local(): lax.psum_scatter(numerator, 'ca', scatter_dimension=1, tiled=True)  45.8 us
    reduce_scatter x1, waiting for transfers between devices, local(): lax.psum_scatter(jnp.dot(attended, out_weight, preferred_element_type=jnp...  44.6 us
    unnamed x4, waiting for transfers between devices  43.3 us
    pmax x1, blocking collectives, local(): top_peak = lax.pmax(row_peak, 'ca')  26.8 us
    all_gather x1, blocking collectives, local(): query_heads = heads_major(lax.all_gather(block_q, 'ca', axis=0, tiled=True))  26.6 us
    all_gather x1, blocking collectives, local(): key_heads = heads_major(lax.all_gather(block_k, 'cz', axis=0, tiled=True))  26.5 us
    all_to_all x3, starting transfers between devices, own_group(): return lax.all_to_all(rows, 'tp', 1, 0, tiled=True)  26.2 us
    all_gather x1, blocking collectives, local(): value_heads = heads_major(lax.all_gather(block_v, 'cz', axis=0, tiled=True))  19.6 us
  transfers between devices with their start and end apart: 6, of which 4 were waited for; matrix products, arithmetic and copies ran while one was open for 6% of the time, Pallas kernels for 0%

profile of v1, /device:TPU:1, one launch (start us, length us, event | category | flops | bytes accessed | tf_op | source)
XLA Modules:
  0.0 308.0 jit_solution(11759176856550018257)
XLA Ops:
  6.5 1.5 copy.47
  8.1 10.1 %all-to-all-start = ((bf16[16,8,384]{2,0,1:T(8,128)(2,1)}), bf16[16,8,384]{2,0,1:T(8,128)(2,1)S(1)}, u32[]{:S(2)}, u32[]{:S(2)}) async-start(bf16[16,8,384]{2,0,1:T(8,128)(2,1)} %bitcast.43), calls=%async_computation | async-start | bytes 196608 | tf_op jit(solution)/shard_map/all_to_all | solution.py:34
  18.2 1.5 copy.46
  19.8 1.6 copy.45
  21.3 4.5 %all-to-all-done = bf16[16,8,384]{2,0,1:T(8,128)(2,1)S(1)} async-done(((bf16[16,8,384]{2,0,1:T(8,128)(2,1)}), bf16[16,8,384]{2,0,1:T(8,128)(2,1)S(1)}, u32[]{:S(2)}, u32[]{:S(2)}) %all-to-all-start) | async-done | bytes 98336 | tf_op jit(solution)/shard_map/all_to_all | solution.py:34
  25.9 4.3 %all-to-all-start.1 = ((bf16[16,8,384]{2,0,1:T(8,128)(2,1)}), bf16[16,8,384]{2,0,1:T(8,128)(2,1)S(1)}, u32[]{:S(2)}, u32[]{:S(2)}) async-start(bf16[16,8,384]{2,0,1:T(8,128)(2,1)} %bitcast.42), calls=%async_computation.1 | async-start | bytes 196608 | tf_op jit(solution)/shard_map/all_to_all | solution.py:34
  30.2 26.6 %all_gather.9 = bf16[1024,384]{1,0:T(8,128)(2,1)S(1)} all-gather(bf16[128,384]{1,0:T(8,128)(2,1)S(1)} %bitcast.50), channel_id=1, replica_groups=mesh['ca'=8,'cz'=8,'tp'=8] {'ca'}, dimensions={0}, use_global_device_ids=true | all-gather | bytes 884736 | tf_op jit(solution)/shard_map/all_gather | solution.py:43
  57.0 0.4 copy.27
  57.4 11.7 %all-to-all-start.2 = ((bf16[16,8,384]{2,0,1:T(8,128)(2,1)}), bf16[16,8,384]{2,0,1:T(8,128)(2,1)S(1)}, u32[]{:S(2)}, u32[]{:S(2)}) async-start(bf16[16,8,384]{2,0,1:T(8,128)(2,1)} %bitcast.41), calls=%async_computation.2 | async-start | bytes 196608 | tf_op jit(solution)/shard_map/all_to_all | solution.py:34
  69.2 26.5 %all_gather.10 = bf16[1024,384]{1,0:T(8,128)(2,1)S(1)} all-gather(bf16[128,384]{1,0:T(8,128)(2,1)S(1)} %bitcast.49), channel_id=1, replica_groups=mesh['ca'=8,'cz'=8,'tp'=8] {'cz'}, dimensions={0}, use_global_device_ids=true | all-gather | bytes 884736 | tf_op jit(solution)/shard_map/all_gather | solution.py:44
  96.4 1.8 multiply_reduce_fusion
  98.2 4.6 %copy-done = f32[3,1024,1024]{1,2,0:T(8,128)} copy-done((f32[3,1024,1024]{1,2,0:T(8,128)}, f32[3,1024,1024]{1,2,0:T(8,128)S(1)}, u32[]{:S(2)}) %copy-start) | copy-done | bytes 12582936
  102.8 2.1 convert_reduce_fusion
  104.8 26.8 %pmax.7 = f32[3,1024]{1,0:T(4,128)S(1)} all-reduce(f32[3,1024]{1,0:T(4,128)S(1)} %get-tuple-element.7), channel_id=1, replica_groups=mesh['ca'=8,'cz'=8,'tp'=8] {'ca'}, use_global_device_ids=true, to_apply=%region_1.0 | all-reduce | flops 3072 | bytes 24576 | tf_op jit(solution)/shard_map/pmax | solution.py:48
  131.7 19.6 %all_gather.11 = bf16[1024,384]{1,0:T(8,128)(2,1)S(1)} all-gather(bf16[128,384]{1,0:T(8,128)(2,1)S(1)} %bitcast.48), channel_id=1, replica_groups=mesh['ca'=8,'cz'=8,'tp'=8] {'cz'}, dimensions={0}, use_global_device_ids=true | all-gather | bytes 884736 | tf_op jit(solution)/shard_map/all_gather | solution.py:45
  151.5 0.4 copy.33
  151.9 1.0 copy.37
  153.1 8.5 %multiply_convert_fusion = bf16[3,1024,128]{2,1,0:T(8,128)(2,1)} fusion(f32[3,1024,1024]{1,2,0:T(8,128)} %copy-done, f32[3,1024]{1,0:T(4,128)S(1)} %get-tuple-element.7, bf16[1024,3,128]{2,0,1:T(8,128)(2,1)S(1)} %copy.33, f32[3,1024]{1,0:T(4,128)S(1)} %get-tuple-element.6), kind=kOutput, calls=%fused_computation.4 | convolution fusion | flops 815529984 | bytes 14180352 | tf_op jit(solution)/shard_map/hij,hjd->hid/dot_general | solution.py:22
  161.7 43.3 %reduce-scatter.10.cloned.1.call-done = f32[128,3]{1,0:T(8,128)} async-done(((f32[1024,3]{1,0:T(8,128)}), f32[128,3]{1,0:T(8,128)}) %reduce-scatter.10.cloned.1.call-update) | async-done | bytes 1552
  204.9 0.9 copy.38
  205.8 45.8 %reduce-scatter.6.cloned.1.call-done = bf16[3,128,128]{2,1,0:T(8,128)(2,1)} async-done(((bf16[3,1024,128]{2,1,0:T(8,128)(2,1)}), bf16[3,128,128]{2,1,0:T(8,128)(2,1)}) %reduce-scatter.6.cloned.1.call-update) | async-done | bytes 98320 | tf_op jit(solution)/shard_map/reduce_scatter | solution.py:52
  251.6 1.0 fusion.4
  252.7 4.1 %convolution_convert_fusion = bf16[128,5120]{1,0:T(8,128)(2,1)} fusion(bf16[128,384]{0,1:T(8,128)(2,1)S(1)} %bitcast.51, bf16[384,5120]{1,0:T(8,128)(2,1)} %param.7), kind=kOutput, calls=%fused_computation.3 | convolution fusion | flops 503971840 | bytes 5341184 | tf_op jit(solution)/shard_map/dot_general | solution.py:56
  256.8 44.6 %reduce-scatter.8.cloned.1.call-done = bf16[16,5120]{1,0:T(8,128)(2,1)} async-done(((bf16[128,5120]{1,0:T(8,128)(2,1)}), bf16[16,5120]{1,0:T(8,128)(2,1)}) %reduce-scatter.8.cloned.1.call-update) | async-done | bytes 163856 | tf_op jit(solution)/shard_map/reduce_scatter | solution.py:55
  (15 shorter events, 1.5 us)
Async XLA Ops:
  8.1 17.8 %all-to-all-start = ((bf16[16,8,384]{2,0,1:T(8,128)(2,1)}), bf16[16,8,384]{2,0,1:T(8,128)(2,1)S(1)}, u32[]{:S(2)}, u32[]{:S(2)}) async-start(bf16[16,8,384]{2,0,1:T(8,128)(2,1)} %bitcast.43), calls=%async_computation | async-start | bytes 196608 | tf_op jit(solution)/shard_map/all_to_all | solution.py:34
  25.9 31.6 %all-to-all-start.1 = ((bf16[16,8,384]{2,0,1:T(8,128)(2,1)}), bf16[16,8,384]{2,0,1:T(8,128)(2,1)S(1)}, u32[]{:S(2)}, u32[]{:S(2)}) async-start(bf16[16,8,384]{2,0,1:T(8,128)(2,1)} %bitcast.42), calls=%async_computation.1 | async-start | bytes 196608 | tf_op jit(solution)/shard_map/all_to_all | solution.py:34
  57.4 74.2 %all-to-all-start.2 = ((bf16[16,8,384]{2,0,1:T(8,128)(2,1)}), bf16[16,8,384]{2,0,1:T(8,128)(2,1)S(1)}, u32[]{:S(2)}, u32[]{:S(2)}) async-start(bf16[16,8,384]{2,0,1:T(8,128)(2,1)} %bitcast.41), calls=%async_computation.2 | async-start | bytes 196608 | tf_op jit(solution)/shard_map/all_to_all | solution.py:34
  69.2 135.7 %reduce-scatter.10.cloned.1.call-start = ((), (), s32[]{:S(2)}) async-start(), calls=%async_computation.8 | async-start | bytes 589824
  98.2 4.6 %copy-start = (f32[3,1024,1024]{1,2,0:T(8,128)}, f32[3,1024,1024]{1,2,0:T(8,128)S(1)}, u32[]{:S(2)}) copy-start(f32[3,1024,1024]{1,2,0:T(8,128)S(1)} %get-tuple-element.8) | copy-start | bytes 37748740
  153.0 98.6 %reduce-scatter.6.cloned.1.call-start = ((), (), s32[]{:S(2)}) async-start(), calls=%async_computation.6 | async-start | bytes 884736 | tf_op jit(solution)/shard_map/reduce_scatter | solution.py:52
  161.6 139.9 %reduce-scatter.8.cloned.1.call-start = ((), (), s32[]{:S(2)}) async-start(), calls=%async_computation.7 | async-start | bytes 1474560 | tf_op jit(solution)/shard_map/reduce_scatter | solution.py:55
Sparse Core Ops, SparseCore 0:
  153.1 51.7 reduce-scatter.9
  208.0 43.5 reduce-scatter.5
  257.0 44.4 reduce-scatter.7

commit v2 on v1

v2 whole, which is shorter than its diff:
```python
import math

import jax
import jax.numpy as jnp
from jax import lax
from jax.sharding import Mesh
from jax.sharding import PartitionSpec as P

HD = 128
KEY_SPLIT = 8


def attend_local(query_heads, key_heads, value_heads, score_scale):
    scores = (
        jnp.einsum("hid,hjd->hij", query_heads, key_heads, preferred_element_type=jnp.float32)
        * score_scale
    )
    row_peak = jnp.max(scores, axis=-1)
    weights_low = jnp.exp(scores - row_peak[..., None]).astype(jnp.bfloat16)
    row_total = jnp.sum(weights_low.astype(jnp.float32), axis=-1)
    weighted = jnp.einsum(
        "hij,hjd->hid", weights_low, value_heads, preferred_element_type=jnp.float32
    )
    return row_peak, row_total, weighted


def gather_by_exchange(block, axis_name):
    count = lax.axis_size(axis_name)
    spread = jnp.broadcast_to(block[None], (count,) + block.shape)
    return lax.all_to_all(spread, axis_name, 0, 0, tiled=True)


def local(query_vectors, key_vectors, value_vectors, out_weight):
    score_scale = 1.0 / math.sqrt(HD)
    tp_count = lax.axis_size("tp")
    ca_count = lax.axis_size("ca")
    token_rows = query_vectors.shape[0]
    own_heads = query_vectors.shape[1] // HD // tp_count
    own_cols = own_heads * HD

    qkv = jnp.stack([query_vectors, key_vectors, value_vectors], axis=1)
    qkv = qkv.reshape(token_rows, 3, tp_count, own_cols)
    block = lax.all_to_all(qkv, "tp", 2, 0, tiled=True)
    block_rows = block.shape[0]
    block = block.reshape(block_rows, 3, own_heads, HD).transpose(1, 2, 0, 3)

    query_heads = gather_by_exchange(block[0], "ca")
    query_heads = query_heads.transpose(1, 0, 2, 3).reshape(own_heads, ca_count * block_rows, HD)
    kv = gather_by_exchange(block[1:], "cz")
    kv = kv.transpose(1, 2, 0, 3, 4).reshape(2, own_heads, -1, HD)

    row_peak, row_total, weighted = attend_local(query_heads, kv[0], kv[1], score_scale)
    stats = jnp.stack([row_peak, row_total], axis=0).reshape(2, own_heads, ca_count, block_rows)
    stats = lax.all_to_all(stats.transpose(2, 0, 1, 3), "ca", 0, 0, tiled=True)
    parts = weighted.astype(jnp.bfloat16).reshape(own_heads, ca_count, block_rows, HD)
    parts = lax.all_to_all(parts.transpose(1, 0, 2, 3), "ca", 0, 0, tiled=True)
    top_peak = jnp.max(stats[:, 0], axis=0)
    factor = jnp.exp(stats[:, 0] - top_peak[None])
    totals = jnp.sum(stats[:, 1] * factor, axis=0)
    numerator = jnp.sum(parts.astype(jnp.float32) * factor[..., None], axis=0)
    attended = (numerator / totals[..., None]).astype(jnp.bfloat16)
    attended = attended.transpose(1, 0, 2).reshape(block_rows, own_cols)

    partial = jnp.dot(attended, out_weight, preferred_element_type=jnp.float32).astype(jnp.bfloat16)
    partial = partial.reshape(tp_count, block_rows // tp_count, -1)
    partial = lax.all_to_all(partial, "tp", 0, 0, tiled=True)
    return jnp.sum(partial.astype(jnp.float32), axis=0).astype(jnp.bfloat16)


def solution(mesh):
    ctx_count, tp_count = mesh.devices.shape
    split_mesh = Mesh(
        mesh.devices.reshape(ctx_count // KEY_SPLIT, KEY_SPLIT, tp_count), ("ca", "cz", "tp")
    )
    rows = P(("ca", "cz", "tp"), None)
    return jax.shard_map(
        local,
        mesh=split_mesh,
        in_specs=(rows, rows, rows, P("tp", None)),
        out_specs=rows,
        check_vma=False,
    )
```

time: 310 us -> 174 us (0.56)
  waiting for transfers between devices: 138 us -> 63.3 us
  blocking collectives: 99.5 us -> 57.6 us
  between operations: 13.2 us -> 0.17 us
    reduce_scatter x2 -> x0, waiting for transfers between devices: 90.4 us -> none  [the longest x1 45.8 us: local(): lax.psum_scatter(numerator, 'ca', scatter_dimension=1, tiled=True)]
    all_gather x3 -> x0, blocking collectives: 72.7 us -> none  [the longest x1 26.6 us: local(): query_heads = heads_major(lax.all_gather(block_q, 'ca', axis=0, tiled=True))]
    all_to_all x3 -> x4, waiting for transfers between devices: 4.55 us -> 63.3 us  [the longest x2 51.8 us: gather_by_exchange(): return lax.all_to_all(spread, axis_name, 0, 0, tiled=True)]
    all_to_all x0 -> x2, blocking collectives: none -> 57.6 us  [the longest x1 36.9 us: local(): partial = lax.all_to_all(partial, 'tp', 0, 0, tiled=True)]
    unnamed x4 -> x0, waiting for transfers between devices: 43.3 us -> none
    pmax x1 -> x0, blocking collectives: 26.8 us -> none  [local(): top_peak = lax.pmax(row_peak, 'ca')]
    all_to_all x3 -> x1, local copies, waits for them, and re-layouts: 4.63 us -> 0.03 us  [local(): block = lax.all_to_all(qkv, 'tp', 2, 0, tiled=True)]
    all_to_all x3 -> x4, starting transfers between devices: 26.2 us -> 23.6 us  [the longest x2 14.6 us: gather_by_exchange(): return lax.all_to_all(spread, axis_name, 0, 0, tiled=True)]
  transfers between devices with their start and end apart: 6 -> 4, of which waited for: 4 -> 3; matrix products, arithmetic and copies ran while one was open for 6% -> 5% of each run, Pallas kernels for 0% -> 0%
where the time goes in v2:
time: 174 us; the launch traced here: 173 us
  waiting for transfers between devices  63.3 us (36%)
  blocking collectives  57.6 us (33%)
  starting transfers between devices  23.6 us (14%)
  matrix products  12.3 us (7%)
  local copies, waits for them, and re-layouts  12.2 us (7%)
  other arithmetic  3.65 us (2%)
    all_to_all x2, waiting for transfers between devices, gather_by_exchange(): return lax.all_to_all(spread, axis_name, 0, 0, tiled=True)  51.8 us
    all_to_all x1, blocking collectives, local(): partial = lax.all_to_all(partial, 'tp', 0, 0, tiled=True)  36.9 us
    all_to_all x1, blocking collectives, local(): block = lax.all_to_all(qkv, 'tp', 2, 0, tiled=True)  20.6 us
    all_to_all x2, starting transfers between devices, gather_by_exchange(): return lax.all_to_all(spread, axis_name, 0, 0, tiled=True)  14.6 us
    all_to_all x1, waiting for transfers between devices, local(): parts = lax.all_to_all(parts.transpose(1, 0, 2, 3), 'ca', 0, 0, tiled=True)  11.5 us
    dot_general x1, matrix products, attend_local(): jnp.einsum('hij,hjd->hid', weights_low, value_heads, preferred_element_ty...  7.51 us
    unnamed x7, local copies, waits for them, and re-layouts  7.3 us
    all_to_all x1, starting transfers between devices, local(): parts = lax.all_to_all(parts.transpose(1, 0, 2, 3), 'ca', 0, 0, tiled=True)  5.14 us
  transfers between devices with their start and end apart: 4, of which 3 were waited for; matrix products, arithmetic and copies ran while one was open for 5% of the time, Pallas kernels for 0%

profile of v2, /device:TPU:1, one launch (start us, length us, event | category | flops | bytes accessed | tf_op | source)
XLA Modules:
  0.0 172.8 jit_solution(16106447294990009302)
XLA Ops:
  0.0 0.9 copy.67
  0.9 0.9 copy.68
  1.8 0.9 copy.69
  2.8 20.6 %all_to_all.40 = bf16[16,3,8,384]{3,0,1,2:T(8,128)(2,1)S(1)} all-to-all(bf16[16,3,8,384]{3,0,1,2:T(8,128)(2,1)S(1)} %copy.47), channel_id=1, replica_groups=mesh['ca'=8,'cz'=8,'tp'=8] {'tp'}, dimensions={2} | all-to-all | bytes 589824 | tf_op jit(solution)/shard_map/all_to_all | solution.py:43
  23.6 1.0 broadcast_in_dim.7
  24.7 4.6 %all-to-all-start.1 = ((bf16[8,3,128,128]{3,2,1,0:T(8,128)(2,1)}), bf16[8,3,128,128]{3,2,1,0:T(8,128)(2,1)S(1)}, u32[]{:S(2)}, u32[]{:S(2)}) async-start(bf16[8,3,128,128]{3,2,1,0:T(8,128)(2,1)} %broadcast_in_dim.7), calls=%async_computation.1 | async-start | bytes 1572864 | tf_op jit(solution)/shard_map/all_to_all | solution.py:30
  29.4 11.5 %all-to-all-done.1 = bf16[8,3,128,128]{3,2,1,0:T(8,128)(2,1)S(1)} async-done(((bf16[8,3,128,128]{3,2,1,0:T(8,128)(2,1)}), bf16[8,3,128,128]{3,2,1,0:T(8,128)(2,1)S(1)}, u32[]{:S(2)}, u32[]{:S(2)}) %all-to-all-start.1) | async-done | bytes 786464 | tf_op jit(solution)/shard_map/all_to_all | solution.py:30
  40.9 1.5 broadcast_in_dim.8
  42.4 10.0 %all-to-all-start.2 = ((bf16[8,2,3,128,128]{4,3,2,1,0:T(8,128)(2,1)}), bf16[8,2,3,128,128]{4,3,2,1,0:T(8,128)(2,1)S(1)}, u32[]{:S(2)}, u32[]{:S(2)}) async-start(bf16[8,2,3,128,128]{4,3,2,1,0:T(8,128)(2,1)} %broadcast_in_dim.8), calls=%async_computation.2 | async-start | bytes 3145728 | tf_op jit(solution)/shard_map/all_to_all | solution.py:30
  52.5 40.4 %all-to-all-done.2 = bf16[8,2,3,128,128]{4,3,2,1,0:T(8,128)(2,1)S(1)} async-done(((bf16[8,2,3,128,128]{4,3,2,1,0:T(8,128)(2,1)}), bf16[8,2,3,128,128]{4,3,2,1,0:T(8,128)(2,1)S(1)}, u32[]{:S(2)}, u32[]{:S(2)}) %all-to-all-start.2) | async-done | bytes 1572896 | tf_op jit(solution)/shard_map/all_to_all | solution.py:30
  93.1 1.8 %multiply_reduce_fusion = (f32[3,1024]{1,0:T(4,128)S(1)}, f32[3,1024,1024]{1,2,0:T(8,128)S(1)}) fusion(bf16[3,1024,128]{2,1,0:T(8,128)(2,1)S(1)} %bitcast.70, bf16[3,1024,128]{2,1,0:T(8,128)(2,1)S(1)} %bitcast.71), kind=kOutput, calls=%fused_computation.2 | convolution fusion | flops 811594752 | bytes 14168064 | tf_op jit(solution)/shard_map/hid,hjd->hij/dot_general | solution.py:15
  94.9 4.6 %copy-done = f32[3,1024,1024]{1,2,0:T(8,128)} copy-done((f32[3,1024,1024]{1,2,0:T(8,128)}, f32[3,1024,1024]{1,2,0:T(8,128)S(1)}, u32[]{:S(2)}) %copy-start) | copy-done | bytes 12582936
  99.5 2.1 %convert_reduce_fusion = f32[3,1024]{1,0:T(4,128)S(1)} fusion(f32[3,1024]{1,0:T(4,128)S(1)} %get-tuple-element.12, f32[3,1024,1024]{1,2,0:T(8,128)S(1)} %get-tuple-element.13), kind=kLoop, calls=%fused_computation | loop fusion | flops 15725568 | bytes 12607488 | tf_op jit(solution)/shard_map/reduce_sum | solution.py:20
  101.6 0.6 copy.56
  102.2 3.8 %all-to-all-start.4 = ((f32[8,2,3,128]{3,1,2,0:T(2,128)}), f32[8,2,3,128]{3,1,2,0:T(2,128)S(1)}, u32[]{:S(2)}, u32[]{:S(2)}) async-start(f32[8,2,3,128]{3,1,2,0:T(2,128)} %copy.56), calls=%async_computation.4 | async-start | bytes 49152 | tf_op jit(solution)/shard_map/all_to_all | solution.py:54
  106.1 7.5 %convolution_convert_fusion.1 = bf16[3,1024,128]{2,1,0:T(8,128)(2,1)S(1)} fusion(bf16[3,1024,128]{2,1,0:T(8,128)(2,1)S(1)} %bitcast.73, f32[3,1024,1024]{1,2,0:T(8,128)} %copy-done, f32[3,1024]{1,0:T(4,128)S(1)} %get-tuple-element.12), kind=kOutput, calls=%fused_computation.5 | convolution fusion | flops 815136768 | bytes 14168064 | tf_op jit(solution)/shard_map/hij,hjd->hid/dot_general | solution.py:21
  113.6 1.0 copy.86
  114.5 5.1 %all-to-all-start.3 = ((bf16[8,3,128,128]{3,2,1,0:T(8,128)(2,1)}), bf16[8,3,128,128]{3,2,1,0:T(8,128)(2,1)S(1)}, u32[]{:S(2)}, u32[]{:S(2)}) async-start(bf16[8,3,128,128]{3,2,1,0:T(8,128)(2,1)} %bitcast.65), calls=%async_computation.3 | async-start | bytes 1572864 | tf_op jit(solution)/shard_map/all_to_all | solution.py:56
  119.8 11.5 %all-to-all-done.3 = bf16[8,3,128,128]{3,2,1,0:T(8,128)(2,1)S(1)} async-done(((bf16[8,3,128,128]{3,2,1,0:T(8,128)(2,1)}), bf16[8,3,128,128]{3,2,1,0:T(8,128)(2,1)S(1)}, u32[]{:S(2)}, u32[]{:S(2)}) %all-to-all-start.3) | async-done | bytes 786464 | tf_op jit(solution)/shard_map/all_to_all | solution.py:56
  131.3 0.5 multiply_reduce_fusion.1
  131.9 0.1 copy.61
  132.0 3.0 %convolution_convert_fusion = bf16[128,5120]{1,0:T(8,128)(2,1)S(1)} fusion(bf16[128,384]{0,1:T(8,128)(2,1)S(1)} %bitcast.81, bf16[384,5120]{1,0:T(8,128)(2,1)} %param.7), kind=kOutput, calls=%fused_computation.3 | convolution fusion | flops 503971840 | bytes 5341184 | tf_op jit(solution)/shard_map/dot_general | solution.py:64
  135.0 36.9 %all_to_all.41 = bf16[8,16,5120]{2,1,0:T(8,128)(2,1)S(1)} all-to-all(bf16[8,16,5120]{2,1,0:T(8,128)(2,1)S(1)} %bitcast.69), channel_id=1, replica_groups=mesh['ca'=8,'cz'=8,'tp'=8] {'tp'}, dimensions={0} | all-to-all | bytes 2621440 | tf_op jit(solution)/shard_map/all_to_all | solution.py:66
  172.0 0.9 reduce_sum.45
  (21 shorter events, 0.9 us)
Async XLA Ops:
  24.7 16.2 %all-to-all-start.1 = ((bf16[8,3,128,128]{3,2,1,0:T(8,128)(2,1)}), bf16[8,3,128,128]{3,2,1,0:T(8,128)(2,1)S(1)}, u32[]{:S(2)}, u32[]{:S(2)}) async-start(bf16[8,3,128,128]{3,2,1,0:T(8,128)(2,1)} %broadcast_in_dim.7), calls=%async_computation.1 | async-start | bytes 1572864 | tf_op jit(solution)/shard_map/all_to_all | solution.py:30
  42.4 50.5 %all-to-all-start.2 = ((bf16[8,2,3,128,128]{4,3,2,1,0:T(8,128)(2,1)}), bf16[8,2,3,128,128]{4,3,2,1,0:T(8,128)(2,1)S(1)}, u32[]{:S(2)}, u32[]{:S(2)}) async-start(bf16[8,2,3,128,128]{4,3,2,1,0:T(8,128)(2,1)} %broadcast_in_dim.8), calls=%async_computation.2 | async-start | bytes 3145728 | tf_op jit(solution)/shard_map/all_to_all | solution.py:30
  94.9 4.6 %copy-start = (f32[3,1024,1024]{1,2,0:T(8,128)}, f32[3,1024,1024]{1,2,0:T(8,128)S(1)}, u32[]{:S(2)}) copy-start(f32[3,1024,1024]{1,2,0:T(8,128)S(1)} %get-tuple-element.13) | copy-start | bytes 37748740
  102.2 12.3 %all-to-all-start.4 = ((f32[8,2,3,128]{3,1,2,0:T(2,128)}), f32[8,2,3,128]{3,1,2,0:T(2,128)S(1)}, u32[]{:S(2)}, u32[]{:S(2)}) async-start(f32[8,2,3,128]{3,1,2,0:T(2,128)} %copy.56), calls=%async_computation.4 | async-start | bytes 49152 | tf_op jit(solution)/shard_map/all_to_all | solution.py:54
  114.5 16.7 %all-to-all-start.3 = ((bf16[8,3,128,128]{3,2,1,0:T(8,128)(2,1)}), bf16[8,3,128,128]{3,2,1,0:T(8,128)(2,1)S(1)}, u32[]{:S(2)}, u32[]{:S(2)}) async-start(bf16[8,3,128,128]{3,2,1,0:T(8,128)(2,1)} %bitcast.65), calls=%async_computation.3 | async-start | bytes 1572864 | tf_op jit(solution)/shard_map/all_to_all | solution.py:56

commit v3 on v2

--- a/solution.py
+++ b/solution.py
@@ -1,3 +1,4 @@
+import functools
 import math
 
 import jax
@@ -5,6 +6,8 @@
 from jax import lax
 from jax.sharding import Mesh
 from jax.sharding import PartitionSpec as P
+from jax.experimental import pallas as pl
+from jax.experimental.pallas import tpu as pltpu
 
 HD = 128
 KEY_SPLIT = 8
@@ -30,6 +33,97 @@
     return lax.all_to_all(spread, axis_name, 0, 0, tiled=True)
 
 
+def exchange_kernel(na, nz, q_ref, kv_ref, q_out, kv_out, q_send, q_recv, r_send, r_recv,
+                    l_send, l_recv, own_sem):
+    mesh_ids = pl.DeviceIdType.MESH
+    a = lax.axis_index("ca")
+    z = lax.axis_index("cz")
+    t = lax.axis_index("tp")
+    right = lax.rem(z + 1, nz)
+    left = lax.rem(z + nz - 1, nz)
+
+    barrier = pltpu.get_barrier_semaphore()
+    for off in range(1, na):
+        pl.semaphore_signal(barrier, inc=1, device_id=(lax.rem(a + off, na), z, t),
+                            device_id_type=mesh_ids)
+    for side in (left, right):
+        pl.semaphore_signal(barrier, inc=1, device_id=(a, side, t), device_id_type=mesh_ids)
+    pl.semaphore_wait(barrier, na - 1 + 2)
+
+    own = [
+        pltpu.make_async_copy(q_ref, q_out.at[a], own_sem.at[0]),
+        pltpu.make_async_copy(kv_ref, kv_out.at[z], own_sem.at[1]),
+    ]
+    for copy in own:
+        copy.start()
+    q_copies = []
+    for off in range(1, na):
+        copy = pltpu.make_async_remote_copy(
+            src_ref=q_ref, dst_ref=q_out.at[a], send_sem=q_send.at[off - 1],
+            recv_sem=q_recv.at[off - 1], device_id=(lax.rem(a + off, na), z, t),
+            device_id_type=mesh_ids)
+        copy.start()
+        q_copies.append(copy)
+
+    n_right = nz // 2
+    n_left = (nz - 1) // 2
+    right_copies = []
+    left_copies = []
+    for step in range(max(n_right, n_left)):
+        if step < n_right:
+            slot = lax.rem(z - step + nz, nz)
+            if step > 0:
+                right_copies[step - 1].wait_recv()
+            copy = pltpu.make_async_remote_copy(
+                src_ref=kv_ref if step == 0 else kv_out.at[slot], dst_ref=kv_out.at[slot],
+                send_sem=r_send.at[step], recv_sem=r_recv.at[step], device_id=(a, right, t),
+                device_id_type=mesh_ids)
+            copy.start()
+            right_copies.append(copy)
+        if step < n_left:
+            slot = lax.rem(z + step, nz)
+            if step > 0:
+                left_copies[step - 1].wait_recv()
+            copy = pltpu.make_async_remote_copy(
+                src_ref=kv_ref if step == 0 else kv_out.at[slot], dst_ref=kv_out.at[slot],
+                send_sem=l_send.at[step], recv_sem=l_recv.at[step], device_id=(a, left, t),
+                device_id_type=mesh_ids)
+            copy.start()
+            left_copies.append(copy)
+    right_copies[-1].wait_recv()
+    left_copies[-1].wait_recv()
+    for copy in right_copies + left_copies:
+        copy.wait_send()
+    for copy in q_copies:
+        copy.wait()
+    for copy in own:
+        copy.wait()
+
+
+def exchange(q_blk, kv_blk, na, nz):
+    n_right = nz // 2
+    n_left = (nz - 1) // 2
+    return pl.pallas_call(
+        functools.partial(exchange_kernel, na, nz),
+        out_shape=(
+            jax.ShapeDtypeStruct((na,) + q_blk.shape, q_blk.dtype),
+            jax.ShapeDtypeStruct((nz,) + kv_blk.shape, kv_blk.dtype),
+        ),
+        in_specs=[pl.BlockSpec(memory_space=pl.ANY)] * 2,
+        out_specs=(pl.BlockSpec(memory_space=pl.ANY), pl.BlockSpec(memory_space=pl.ANY)),
+        scratch_shapes=[
+            pltpu.SemaphoreType.DMA((na - 1,)),
+            pltpu.SemaphoreType.DMA((na - 1,)),
+            pltpu.SemaphoreType.DMA((n_right,)),
+            pltpu.SemaphoreType.DMA((n_right,)),
+            pltpu.SemaphoreType.DMA((n_left,)),
+            pltpu.SemaphoreType.DMA((n_left,)),
+            pltpu.SemaphoreType.DMA((2,)),
+        ],
+        compiler_params=pltpu.CompilerParams(collective_id=0, has_side_effects=True),
+    )(q_blk, kv_blk)
+
+
 def local(query_vectors, key_vectors, value_vectors, out_weight):
     score_scale = 1.0 / math.sqrt(HD)
     tp_count = lax.axis_size("tp")
@@ -44,9 +138,8 @@
     block_rows = block.shape[0]
     block = block.reshape(block_rows, 3, own_heads, HD).transpose(1, 2, 0, 3)
 
-    query_heads = gather_by_exchange(block[0], "ca")
+    query_heads, kv = exchange(block[0], block[1:], ca_count, lax.axis_size("cz"))
     query_heads = query_heads.transpose(1, 0, 2, 3).reshape(own_heads, ca_count * block_rows, HD)
-    kv = gather_by_exchange(block[1:], "cz")
     kv = kv.transpose(1, 2, 0, 3, 4).reshape(2, own_heads, -1, HD)
 
     row_peak, row_total, weighted = attend_local(query_heads, kv[0], kv[1], score_scale)

time: 174 us -> 142 us (0.82)
  waiting for transfers between devices: 63.3 us -> 8.91 us
  Pallas kernels: 0 us -> 30.2 us
  starting transfers between devices: 23.6 us -> 8.41 us
  blocking collectives: 57.6 us -> 64.1 us
    all_to_all x2 -> x0, waiting for transfers between devices: 51.8 us -> none  [gather_by_exchange(): return lax.all_to_all(spread, axis_name, 0, 0, tiled=True)]
    pallas_call x0 -> x1, Pallas kernels: none -> 30.2 us  [exchange(): pl.pallas_call(functools.partial(exchange_kernel, na, nz), out_shape=(jax...]
    all_to_all x2 -> x0, starting transfers between devices: 14.6 us -> none  [gather_by_exchange(): return lax.all_to_all(spread, axis_name, 0, 0, tiled=True)]
    all_to_all x1, blocking collectives: 36.9 us -> 43.5 us  [local(): partial = lax.all_to_all(partial, 'tp', 0, 0, tiled=True)]
    broadcast_in_dim x4 -> x0, local copies, waits for them, and re-layouts: 2.64 us -> none  [gather_by_exchange(): spread = jnp.broadcast_to(block[None], (count,) + block.shape)]
    all_to_all x1, waiting for transfers between devices: 11.5 us -> 8.91 us  [local(): parts = lax.all_to_all(parts.transpose(1, 0, 2, 3), 'ca', 0, 0, tiled=True)]
  transfers between devices with their start and end apart: 4 -> 2, of which waited for: 3 -> 1; matrix products, arithmetic and copies ran while one was open for 5% -> 6% of each run, Pallas kernels for 0% -> 0%
where the time goes in v3:
time: 142 us; the launch traced here: 141 us
  blocking collectives  64.1 us (45%)
  Pallas kernels  30.2 us (21%)
  local copies, waits for them, and re-layouts  13.4 us (9%)
  matrix products  12.3 us (9%)
  waiting for transfers between devices  8.91 us (6%)
  starting transfers between devices  8.41 us (6%)
  other arithmetic  3.65 us (3%)
    all_to_all x1, blocking collectives, local(): partial = lax.all_to_all(partial, 'tp', 0, 0, tiled=True)  43.5 us
    pallas_call x1, Pallas kernels, exchange(): pl.pallas_call(functools.partial(exchange_kernel, na, nz), out_shape=(jax...  30.2 us
    all_to_all x1, blocking collectives, local(): block = lax.all_to_all(qkv, 'tp', 2, 0, tiled=True)  20.6 us
    all_to_all x1, waiting for transfers between devices, local(): parts = lax.all_to_all(parts.transpose(1, 0, 2, 3), 'ca', 0, 0, tiled=True)  8.91 us
    dot_general x1, matrix products, attend_local(): jnp.einsum('hij,hjd->hid', weights_low, value_heads, preferred_element_ty...  7.51 us
    unnamed x7, local copies, waits for them, and re-layouts  7.3 us
    all_to_all x1, starting transfers between devices, local(): parts = lax.all_to_all(parts.transpose(1, 0, 2, 3), 'ca', 0, 0, tiled=True)  5.07 us
    all_to_all x1, starting transfers between devices, local(): stats = lax.all_to_all(stats.transpose(2, 0, 1, 3), 'ca', 0, 0, tiled=True)  3.34 us
  transfers between devices with their start and end apart: 2, of which 1 were waited for; matrix products, arithmetic and copies ran while one was open for 6% of the time, Pallas kernels for 0%

profile of v3, /device:TPU:1, one launch (start us, length us, event | category | flops | bytes accessed | tf_op | source)
XLA Modules:
  0.0 141.1 jit_solution(7993742141629300400)
XLA Ops:
  0.0 0.9 copy.65
  0.9 0.9 copy.66
  1.8 0.9 copy.67
  2.8 20.6 %all_to_all.30 = bf16[16,3,8,384]{3,0,1,2:T(8,128)(2,1)S(1)} all-to-all(bf16[16,3,8,384]{3,0,1,2:T(8,128)(2,1)S(1)} %copy.46), channel_id=1, replica_groups=mesh['ca'=8,'cz'=8,'tp'=8] {'tp'}, dimensions={2} | all-to-all | bytes 589824 | tf_op jit(solution)/shard_map/all_to_all | solution.py:137
  23.6 0.6 slice_bitcast_fusion.q_ref
  24.3 0.7 slice.28.kv_ref
  24.9 30.2 %shard_map.46 = (bf16[8,3,128,128]{3,2,1,0:T(8,128)(2,1)}, bf16[8,2,3,128,128]{4,3,2,1,0:T(8,128)(2,1)}) custom-call(bf16[3,128,128]{2,1,0:T(8,128)(2,1)} %slice_bitcast_fusion.q_ref, bf16[2,3,128,128]{3,2,1,0:T(8,128)(2,1)} %slice.28.kv_ref), custom_call_target="tpu_custom_call" | custom-call | tf_op jit(solution)/shard_map/pallas_call | solution.py:106
  55.2 1.2 copy.49
  56.4 1.5 %fusion.7 = (bf16[1,3,8,128,128]{4,3,1,0,2:T(8,128)(2,1)S(1)}, bf16[1,3,8,128,128]{4,3,1,0,2:T(8,128)(2,1)S(1)}) fusion(bf16[2,3,8,128,128]{4,3,1,0,2:T(8,128)(2,1)} %bitcast.75), kind=kLoop, calls=%fused_computation.23 | loop fusion | bytes 3145728 | tf_op jit(solution)/shard_map/slice | solution.py:145
  58.0 1.8 %multiply_reduce_fusion = (f32[3,1024]{1,0:T(4,128)S(1)}, f32[3,1024,1024]{1,2,0:T(8,128)S(1)}) fusion(bf16[3,1024,128]{2,1,0:T(8,128)(2,1)S(1)} %bitcast.71, bf16[3,1024,128]{2,1,0:T(8,128)(2,1)S(1)} %bitcast.72), kind=kOutput, calls=%fused_computation.2 | convolution fusion | flops 811594752 | bytes 14168064 | tf_op jit(solution)/shard_map/hid,hjd->hij/dot_general | solution.py:18
  59.9 4.6 %copy-done = f32[3,1024,1024]{1,2,0:T(8,128)} copy-done((f32[3,1024,1024]{1,2,0:T(8,128)}, f32[3,1024,1024]{1,2,0:T(8,128)S(1)}, u32[]{:S(2)}) %copy-start) | copy-done | bytes 12582936
  64.4 2.1 %convert_reduce_fusion = f32[3,1024]{1,0:T(4,128)S(1)} fusion(f32[3,1024]{1,0:T(4,128)S(1)} %get-tuple-element.16, f32[3,1024,1024]{1,2,0:T(8,128)S(1)} %get-tuple-element.17), kind=kLoop, calls=%fused_computation | loop fusion | flops 15725568 | bytes 12607488 | tf_op jit(solution)/shard_map/reduce_sum | solution.py:23
  66.5 0.6 copy.54
  67.2 3.3 %all-to-all-start.2 = ((f32[8,2,3,128]{3,1,2,0:T(2,128)}), f32[8,2,3,128]{3,1,2,0:T(2,128)S(1)}, u32[]{:S(2)}, u32[]{:S(2)}) async-start(f32[8,2,3,128]{3,1,2,0:T(2,128)} %copy.54), calls=%async_computation.2 | async-start | bytes 49152 | tf_op jit(solution)/shard_map/all_to_all | solution.py:147
  70.5 7.5 %convolution_convert_fusion.1 = bf16[3,1024,128]{2,1,0:T(8,128)(2,1)S(1)} fusion(bf16[3,1024,128]{2,1,0:T(8,128)(2,1)S(1)} %bitcast.73, f32[3,1024,1024]{1,2,0:T(8,128)} %copy-done, f32[3,1024]{1,0:T(4,128)S(1)} %get-tuple-element.16), kind=kOutput, calls=%fused_computation.5 | convolution fusion | flops 815136768 | bytes 14168064 | tf_op jit(solution)/shard_map/hij,hjd->hid/dot_general | solution.py:24
  78.0 1.0 copy.85
  79.0 5.1 %all-to-all-start.1 = ((bf16[8,3,128,128]{3,2,1,0:T(8,128)(2,1)}), bf16[8,3,128,128]{3,2,1,0:T(8,128)(2,1)S(1)}, u32[]{:S(2)}, u32[]{:S(2)}) async-start(bf16[8,3,128,128]{3,2,1,0:T(8,128)(2,1)} %bitcast.66), calls=%async_computation.1 | async-start | bytes 1572864 | tf_op jit(solution)/shard_map/all_to_all | solution.py:149
  84.1 8.9 %all-to-all-done.1 = bf16[8,3,128,128]{3,2,1,0:T(8,128)(2,1)S(1)} async-done(((bf16[8,3,128,128]{3,2,1,0:T(8,128)(2,1)}), bf16[8,3,128,128]{3,2,1,0:T(8,128)(2,1)S(1)}, u32[]{:S(2)}, u32[]{:S(2)}) %all-to-all-start.1) | async-done | bytes 786464 | tf_op jit(solution)/shard_map/all_to_all | solution.py:149
  93.0 0.5 multiply_reduce_fusion.1
  93.5 0.1 fusion
  93.6 0.1 copy.59
  93.8 3.0 %convolution_convert_fusion = bf16[128,5120]{1,0:T(8,128)(2,1)S(1)} fusion(bf16[128,384]{0,1:T(8,128)(2,1)S(1)} %bitcast.83, bf16[384,5120]{1,0:T(8,128)(2,1)} %param.7), kind=kOutput, calls=%fused_computation.3 | convolution fusion | flops 503971840 | bytes 5341184 | tf_op jit(solution)/shard_map/dot_general | solution.py:157
  96.8 43.5 %all_to_all.31 = bf16[8,16,5120]{2,1,0:T(8,128)(2,1)S(1)} all-to-all(bf16[8,16,5120]{2,1,0:T(8,128)(2,1)S(1)} %bitcast.70), channel_id=1, replica_groups=mesh['ca'=8,'cz'=8,'tp'=8] {'tp'}, dimensions={0} | all-to-all | bytes 2621440 | tf_op jit(solution)/shard_map/all_to_all | solution.py:159
  140.3 0.9 reduce_sum.45
  (15 shorter events, 0.4 us)
Async XLA Ops:
  59.9 4.6 %copy-start = (f32[3,1024,1024]{1,2,0:T(8,128)}, f32[3,1024,1024]{1,2,0:T(8,128)S(1)}, u32[]{:S(2)}) copy-start(f32[3,1024,1024]{1,2,0:T(8,128)S(1)} %get-tuple-element.17) | copy-start | bytes 37748740
  67.2 11.8 %all-to-all-start.2 = ((f32[8,2,3,128]{3,1,2,0:T(2,128)}), f32[8,2,3,128]{3,1,2,0:T(2,128)S(1)}, u32[]{:S(2)}, u32[]{:S(2)}) async-start(f32[8,2,3,128]{3,1,2,0:T(2,128)} %copy.54), calls=%async_computation.2 | async-start | bytes 49152 | tf_op jit(solution)/shard_map/all_to_all | solution.py:147
  79.0 14.1 %all-to-all-start.1 = ((bf16[8,3,128,128]{3,2,1,0:T(8,128)(2,1)}), bf16[8,3,128,128]{3,2,1,0:T(8,128)(2,1)S(1)}, u32[]{:S(2)}, u32[]{:S(2)}) async-start(bf16[8,3,128,128]{3,2,1,0:T(8,128)(2,1)} %bitcast.66), calls=%async_computation.1 | async-start | bytes 1572864 | tf_op jit(solution)/shard_map/all_to_all | solution.py:149

commit v4 on v3

--- a/solution.py
+++ b/solution.py
@@ -124,6 +124,82 @@
     )(q_blk, kv_blk)
 
 
+def project_kernel(n_hi, att_ref, w_ref, out_ref, send1, recv1, total, send2, recv2, sems1,
+                   send_sems2, recv_sems2):
+    mesh_ids = pl.DeviceIdType.MESH
+    a = lax.axis_index("ca")
+    z = lax.axis_index("cz")
+    t = lax.axis_index("tp")
+    core = lax.rem(t, 2)
+    hi = t // 2
+    partner = (a, z, hi * 2 + 1 - core)
+    rows = send2.shape[1]
+
+    barrier = pltpu.get_barrier_semaphore()
+    pl.semaphore_signal(barrier, inc=1, device_id=partner, device_id_type=mesh_ids)
+    for off in range(1, n_hi):
+        pl.semaphore_signal(barrier, inc=1, device_id=(a, z, lax.rem(hi + off, n_hi) * 2 + core),
+                            device_id_type=mesh_ids)
+    pl.semaphore_wait(barrier, n_hi)
+
+    send1[...] = jnp.dot(
+        att_ref[1 - core], w_ref[...], preferred_element_type=jnp.float32
+    ).astype(jnp.bfloat16)
+    first = pltpu.make_async_remote_copy(
+        src_ref=send1, dst_ref=recv1, send_sem=sems1.at[0], recv_sem=sems1.at[1],
+        device_id=partner, device_id_type=mesh_ids)
+    first.start()
+    total[...] = jnp.dot(
+        att_ref[core], w_ref[...], preferred_element_type=jnp.float32
+    ).astype(jnp.bfloat16).astype(jnp.float32)
+    first.wait()
+    total[...] = total[...] + recv1[...].astype(jnp.float32)
+    for j in range(n_hi):
+        send2[j] = total[pl.ds(j * rows, rows), :].astype(jnp.bfloat16)
+    second = []
+    for off in range(1, n_hi):
+        dest = lax.rem(hi + off, n_hi)
+        copy = pltpu.make_async_remote_copy(
+            src_ref=send2.at[dest], dst_ref=recv2.at[off - 1], send_sem=send_sems2.at[off - 1],
+            recv_sem=recv_sems2.at[off - 1], device_id=(a, z, dest * 2 + core),
+            device_id_type=mesh_ids)
+        copy.start()
+        second.append(copy)
+    own = total[pl.ds(pl.multiple_of(hi * rows, rows), rows), :]
+    for copy in second:
+        copy.wait()
+    for off in range(1, n_hi):
+        own = own + recv2[off - 1].astype(jnp.float32)
+    out_ref[...] = own.astype(out_ref.dtype)
+
+
+def project(attended, out_weight, tp_count):
+    n_hi = tp_count // 2
+    block_rows, width = attended.shape
+    rows = block_rows // tp_count
+    by_core = attended.reshape(n_hi, 2, rows, width).transpose(1, 0, 2, 3)
+    by_core = by_core.reshape(2, n_hi * rows, width)
+    cols = out_weight.shape[1]
+    vmem = pl.BlockSpec(memory_space=pltpu.VMEM)
+    return pl.pallas_call(
+        functools.partial(project_kernel, n_hi),
+        out_shape=jax.ShapeDtypeStruct((rows, cols), jnp.bfloat16),
+        in_specs=[vmem, vmem],
+        out_specs=vmem,
+        scratch_shapes=[
+            pltpu.VMEM((n_hi * rows, cols), jnp.bfloat16),
+            pltpu.VMEM((n_hi * rows, cols), jnp.bfloat16),
+            pltpu.VMEM((n_hi * rows, cols), jnp.float32),
+            pltpu.VMEM((n_hi, rows, cols), jnp.bfloat16),
+            pltpu.VMEM((n_hi - 1, rows, cols), jnp.bfloat16),
+            pltpu.SemaphoreType.DMA((2,)),
+            pltpu.SemaphoreType.DMA((n_hi - 1,)),
+            pltpu.SemaphoreType.DMA((n_hi - 1,)),
+        ],
+        compiler_params=pltpu.CompilerParams(collective_id=1, has_side_effects=True),
+    )(by_core, out_weight)
+
+
 def local(query_vectors, key_vectors, value_vectors, out_weight):
     score_scale = 1.0 / math.sqrt(HD)
     tp_count = lax.axis_size("tp")
@@ -154,10 +230,7 @@
     attended = (numerator / totals[..., None]).astype(jnp.bfloat16)
     attended = attended.transpose(1, 0, 2).reshape(block_rows, own_cols)
 
-    partial = jnp.dot(attended, out_weight, preferred_element_type=jnp.float32).astype(jnp.bfloat16)
-    partial = partial.reshape(tp_count, block_rows // tp_count, -1)
-    partial = lax.all_to_all(partial, "tp", 0, 0, tiled=True)
-    return jnp.sum(partial.astype(jnp.float32), axis=0).astype(jnp.bfloat16)
+    return project(attended, out_weight, tp_count)
 
 
 def solution(mesh):

time: 142 us -> 129 us (0.908)
  blocking collectives: 64.1 us -> 20.6 us
  Pallas kernels: 30.2 us -> 62.6 us
  matrix products: 12.3 us -> 9.32 us
  local copies, waits for them, and re-layouts: 13.4 us -> 15.7 us
    all_to_all x1 -> x0, blocking collectives: 43.5 us -> none  [local(): partial = lax.all_to_all(partial, 'tp', 0, 0, tiled=True)]
    pallas_call x0 -> x1, Pallas kernels: none -> 32.4 us  [project(): pl.pallas_call(functools.partial(project_kernel, n_hi), out_shape=jax.Sha...]
    dot_general x1 -> x0, matrix products: 3 us -> none  [local(): jnp.dot(attended, out_weight, preferred_element_type=jnp.float32)]
    unnamed x7 -> x8, local copies, waits for them, and re-layouts: 7.3 us -> 8.89 us
  transfers between devices with their start and end apart: 2 -> 2, of which waited for: 1 -> 1; matrix products, arithmetic and copies ran while one was open for 6% -> 7% of each run, Pallas kernels for 0% -> 0%
where the time goes in v4:
time: 129 us; the launch traced here: 128 us
  Pallas kernels  62.6 us (49%)
  blocking collectives  20.6 us (16%)
  local copies, waits for them, and re-layouts  15.7 us (12%)
  matrix products  9.32 us (7%)
  waiting for transfers between devices  8.91 us (7%)
  starting transfers between devices  8.41 us (7%)
  other arithmetic  2.78 us (2%)
    pallas_call x1, Pallas kernels, project(): pl.pallas_call(functools.partial(project_kernel, n_hi), out_shape=jax.Sha...  32.4 us
    pallas_call x1, Pallas kernels, exchange(): pl.pallas_call(functools.partial(exchange_kernel, na, nz), out_shape=(jax...  30.2 us
    all_to_all x1, blocking collectives, local(): block = lax.all_to_all(qkv, 'tp', 2, 0, tiled=True)  20.6 us
    all_to_all x1, waiting for transfers between devices, local(): parts = lax.all_to_all(parts.transpose(1, 0, 2, 3), 'ca', 0, 0, tiled=True)  8.91 us
    unnamed x8, local copies, waits for them, and re-layouts  8.89 us
    dot_general x1, matrix products, attend_local(): jnp.einsum('hij,hjd->hid', weights_low, value_heads, preferred_element_ty...  7.51 us
    all_to_all x1, starting transfers between devices, local(): parts = lax.all_to_all(parts.transpose(1, 0, 2, 3), 'ca', 0, 0, tiled=True)  5.07 us
    all_to_all x1, starting transfers between devices, local(): stats = lax.all_to_all(stats.transpose(2, 0, 1, 3), 'ca', 0, 0, tiled=True)  3.34 us
  transfers between devices with their start and end apart: 2, of which 1 were waited for; matrix products, arithmetic and copies ran while one was open for 7% of the time, Pallas kernels for 0%

profile of v4, /device:TPU:1, one launch (start us, length us, event | category | flops | bytes accessed | tf_op | source)
XLA Modules:
  0.0 128.4 jit_solution(17897735122493456043)
XLA Ops:
  0.0 0.9 copy.73
  0.9 0.9 copy.74
  1.8 0.9 copy.75
  2.8 20.6 %all_to_all.25 = bf16[16,3,8,384]{3,0,1,2:T(8,128)(2,1)S(1)} all-to-all(bf16[16,3,8,384]{3,0,1,2:T(8,128)(2,1)S(1)} %copy.53), channel_id=1, replica_groups=mesh['ca'=8,'cz'=8,'tp'=8] {'tp'}, dimensions={2} | all-to-all | bytes 589824 | tf_op jit(solution)/shard_map/all_to_all | solution.py:213
  23.6 0.6 slice_bitcast_fusion.q_ref
  24.3 0.7 slice.28.kv_ref
  24.9 30.2 %shard_map.46 = (bf16[8,3,128,128]{3,2,1,0:T(8,128)(2,1)}, bf16[8,2,3,128,128]{4,3,2,1,0:T(8,128)(2,1)}) custom-call(bf16[3,128,128]{2,1,0:T(8,128)(2,1)} %slice_bitcast_fusion.q_ref, bf16[2,3,128,128]{3,2,1,0:T(8,128)(2,1)} %slice.28.kv_ref), custom_call_target="tpu_custom_call" | custom-call | tf_op jit(solution)/shard_map/pallas_call | solution.py:106
  55.2 1.2 copy.56
  56.4 1.5 %fusion.7 = (bf16[1,3,8,128,128]{4,3,1,0,2:T(8,128)(2,1)S(1)}, bf16[1,3,8,128,128]{4,3,1,0,2:T(8,128)(2,1)S(1)}) fusion(bf16[2,3,8,128,128]{4,3,1,0,2:T(8,128)(2,1)} %bitcast.72), kind=kLoop, calls=%fused_computation.22 | loop fusion | bytes 3145728 | tf_op jit(solution)/shard_map/slice | solution.py:221
  58.0 1.8 %multiply_reduce_fusion = (f32[3,1024]{1,0:T(4,128)S(1)}, f32[3,1024,1024]{1,2,0:T(8,128)S(1)}) fusion(bf16[3,1024,128]{2,1,0:T(8,128)(2,1)S(1)} %bitcast.68, bf16[3,1024,128]{2,1,0:T(8,128)(2,1)S(1)} %bitcast.69), kind=kOutput, calls=%fused_computation.2 | convolution fusion | flops 811594752 | bytes 14168064 | tf_op jit(solution)/shard_map/hid,hjd->hij/dot_general | solution.py:18
  59.9 4.6 %copy-done = f32[3,1024,1024]{1,2,0:T(8,128)} copy-done((f32[3,1024,1024]{1,2,0:T(8,128)}, f32[3,1024,1024]{1,2,0:T(8,128)S(1)}, u32[]{:S(2)}) %copy-start) | copy-done | bytes 12582936
  64.4 2.1 %convert_reduce_fusion = f32[3,1024]{1,0:T(4,128)S(1)} fusion(f32[3,1024]{1,0:T(4,128)S(1)} %get-tuple-element.16, f32[3,1024,1024]{1,2,0:T(8,128)S(1)} %get-tuple-element.17), kind=kLoop, calls=%fused_computation | loop fusion | flops 15725568 | bytes 12607488 | tf_op jit(solution)/shard_map/reduce_sum | solution.py:23
  66.5 0.6 copy.61
  67.2 3.3 %all-to-all-start.2 = ((f32[8,2,3,128]{3,1,2,0:T(2,128)}), f32[8,2,3,128]{3,1,2,0:T(2,128)S(1)}, u32[]{:S(2)}, u32[]{:S(2)}) async-start(f32[8,2,3,128]{3,1,2,0:T(2,128)} %copy.61), calls=%async_computation.2 | async-start | bytes 49152 | tf_op jit(solution)/shard_map/all_to_all | solution.py:223
  70.5 7.5 %convolution_convert_fusion = bf16[3,1024,128]{2,1,0:T(8,128)(2,1)S(1)} fusion(bf16[3,1024,128]{2,1,0:T(8,128)(2,1)S(1)} %bitcast.70, f32[3,1024,1024]{1,2,0:T(8,128)} %copy-done, f32[3,1024]{1,0:T(4,128)S(1)} %get-tuple-element.16), kind=kOutput, calls=%fused_computation.4 | convolution fusion | flops 815136768 | bytes 14168064 | tf_op jit(solution)/shard_map/hij,hjd->hid/dot_general | solution.py:24
  78.0 1.0 copy.93
  79.0 5.1 %all-to-all-start.1 = ((bf16[8,3,128,128]{3,2,1,0:T(8,128)(2,1)}), bf16[8,3,128,128]{3,2,1,0:T(8,128)(2,1)S(1)}, u32[]{:S(2)}, u32[]{:S(2)}) async-start(bf16[8,3,128,128]{3,2,1,0:T(8,128)(2,1)} %bitcast.64), calls=%async_computation.1 | async-start | bytes 1572864 | tf_op jit(solution)/shard_map/all_to_all | solution.py:225
  84.1 8.9 %all-to-all-done.1 = bf16[8,3,128,128]{3,2,1,0:T(8,128)(2,1)S(1)} async-done(((bf16[8,3,128,128]{3,2,1,0:T(8,128)(2,1)}), bf16[8,3,128,128]{3,2,1,0:T(8,128)(2,1)S(1)}, u32[]{:S(2)}, u32[]{:S(2)}) %all-to-all-start.1) | async-done | bytes 786464 | tf_op jit(solution)/shard_map/all_to_all | solution.py:225
  93.0 0.5 multiply_reduce_fusion.1
  93.5 0.1 fusion
  93.6 0.1 copy.66
  93.8 0.7 copy.67
  94.5 32.4 %shard_map.47 = bf16[16,5120]{1,0:T(8,128)(2,1)} custom-call(bf16[2,64,384]{2,1,0:T(8,128)(2,1)} %bitcast.81, bf16[384,5120]{1,0:T(8,128)(2,1)} %w_ref.1), custom_call_target="tpu_custom_call" | custom-call | tf_op jit(solution)/shard_map/pallas_call | solution.py:184
  126.8 1.6 %copy.98 = bf16[16,5120]{1,0:T(8,128)(2,1)} copy(bf16[16,5120]{1,0:T(8,128)(2,1)} %shard_map.47) | data formatting | bytes 327680
  (16 shorter events, 0.5 us)
Async XLA Ops:
  59.9 4.6 %copy-start = (f32[3,1024,1024]{1,2,0:T(8,128)}, f32[3,1024,1024]{1,2,0:T(8,128)S(1)}, u32[]{:S(2)}) copy-start(f32[3,1024,1024]{1,2,0:T(8,128)S(1)} %get-tuple-element.17) | copy-start | bytes 37748740
  67.2 11.8 %all-to-all-start.2 = ((f32[8,2,3,128]{3,1,2,0:T(2,128)}), f32[8,2,3,128]{3,1,2,0:T(2,128)S(1)}, u32[]{:S(2)}, u32[]{:S(2)}) async-start(f32[8,2,3,128]{3,1,2,0:T(2,128)} %copy.61), calls=%async_computation.2 | async-start | bytes 49152 | tf_op jit(solution)/shard_map/all_to_all | solution.py:223
  79.0 14.1 %all-to-all-start.1 = ((bf16[8,3,128,128]{3,2,1,0:T(8,128)(2,1)}), bf16[8,3,128,128]{3,2,1,0:T(8,128)(2,1)S(1)}, u32[]{:S(2)}, u32[]{:S(2)}) async-start(bf16[8,3,128,128]{3,2,1,0:T(8,128)(2,1)} %bitcast.64), calls=%async_computation.1 | async-start | bytes 1572864 | tf_op jit(solution)/shard_map/all_to_all | solution.py:225

commit v5 on v4

--- a/solution.py
+++ b/solution.py
@@ -124,8 +124,9 @@
     )(q_blk, kv_blk)
 
 
-def project_kernel(n_hi, att_ref, w_ref, out_ref, send1, recv1, total, send2, recv2, sems1,
-                   send_sems2, recv_sems2):
+def project_kernel(na, n_hi, parts_ref, stats_ref, w_ref, out_ref, got_parts, got_stats, full,
+                   send1, recv1, total, send2, recv2, part_sems, stat_sems, sems1, send_sems2,
+                   recv_sems2):
     mesh_ids = pl.DeviceIdType.MESH
     a = lax.axis_index("ca")
     z = lax.axis_index("cz")
@@ -134,28 +135,64 @@
     hi = t // 2
     partner = (a, z, hi * 2 + 1 - core)
     rows = send2.shape[1]
+    heads = parts_ref.shape[1]
 
     barrier = pltpu.get_barrier_semaphore()
+    for off in range(1, na):
+        pl.semaphore_signal(barrier, inc=1, device_id=(lax.rem(a + off, na), z, t),
+                            device_id_type=mesh_ids)
     pl.semaphore_signal(barrier, inc=1, device_id=partner, device_id_type=mesh_ids)
     for off in range(1, n_hi):
         pl.semaphore_signal(barrier, inc=1, device_id=(a, z, lax.rem(hi + off, n_hi) * 2 + core),
                             device_id_type=mesh_ids)
-    pl.semaphore_wait(barrier, n_hi)
-
-    send1[...] = jnp.dot(
-        att_ref[1 - core], w_ref[...], preferred_element_type=jnp.float32
-    ).astype(jnp.bfloat16)
+    pl.semaphore_wait(barrier, na - 1 + n_hi)
+
+    gathered = []
+    for off in range(1, na):
+        dest = lax.rem(a + off, na)
+        for src, dst, sems in ((parts_ref, got_parts, part_sems), (stats_ref, got_stats, stat_sems)):
+            copy = pltpu.make_async_remote_copy(
+                src_ref=src.at[dest], dst_ref=dst.at[off - 1], send_sem=sems.at[0, off - 1],
+                recv_sem=sems.at[1, off - 1], device_id=(dest, z, t), device_id_type=mesh_ids)
+            copy.start()
+            gathered.append(copy)
+    for copy in gathered:
+        copy.wait()
+
+    peaks = [stats_ref[a, 0]] + [got_stats[off - 1, 0] for off in range(1, na)]
+    sums = [stats_ref[a, 1]] + [got_stats[off - 1, 1] for off in range(1, na)]
+    top = peaks[0]
+    for peak in peaks[1:]:
+        top = jnp.maximum(top, peak)
+    factors = [jnp.exp(peak - top) for peak in peaks]
+    totals = factors[0] * sums[0]
+    for factor, part_sum in zip(factors[1:], sums[1:]):
+        totals = totals + factor * part_sum
+    for h in range(heads):
+        numerator = parts_ref[a, h].astype(jnp.float32) * factors[0][h][:, None]
+        for off in range(1, na):
+            numerator = numerator + (
+                got_parts[off - 1, h].astype(jnp.float32) * factors[off][h][:, None]
+            )
+        attended = (numerator / totals[h][:, None]).astype(jnp.bfloat16)
+        product = jnp.dot(attended, w_ref[pl.ds(h * HD, HD), :], preferred_element_type=jnp.float32)
+        if h == 0:
+            full[...] = product
+        else:
+            full[...] = full[...] + product
+
+    for j in range(n_hi):
+        their = pl.multiple_of((j * 2 + 1 - core) * rows, rows)
+        mine = pl.multiple_of((j * 2 + core) * rows, rows)
+        send1[j] = full[pl.ds(their, rows), :].astype(jnp.bfloat16)
+        total[j] = full[pl.ds(mine, rows), :].astype(jnp.bfloat16).astype(jnp.float32)
     first = pltpu.make_async_remote_copy(
         src_ref=send1, dst_ref=recv1, send_sem=sems1.at[0], recv_sem=sems1.at[1],
         device_id=partner, device_id_type=mesh_ids)
     first.start()
-    total[...] = jnp.dot(
-        att_ref[core], w_ref[...], preferred_element_type=jnp.float32
-    ).astype(jnp.bfloat16).astype(jnp.float32)
     first.wait()
-    total[...] = total[...] + recv1[...].astype(jnp.float32)
     for j in range(n_hi):
-        send2[j] = total[pl.ds(j * rows, rows), :].astype(jnp.bfloat16)
+        send2[j] = (total[j] + recv1[j].astype(jnp.float32)).astype(jnp.bfloat16)
     second = []
     for off in range(1, n_hi):
         dest = lax.rem(hi + off, n_hi)
@@ -165,7 +202,7 @@
             device_id_type=mesh_ids)
         copy.start()
         second.append(copy)
-    own = total[pl.ds(pl.multiple_of(hi * rows, rows), rows), :]
+    own = total[hi] + recv1[hi].astype(jnp.float32)
     for copy in second:
         copy.wait()
     for off in range(1, n_hi):
@@ -173,31 +210,34 @@
     out_ref[...] = own.astype(out_ref.dtype)
 
 
-def project(attended, out_weight, tp_count):
+def project(parts, stats, out_weight, tp_count):
+    na, heads, block_rows, _ = parts.shape
     n_hi = tp_count // 2
-    block_rows, width = attended.shape
     rows = block_rows // tp_count
-    by_core = attended.reshape(n_hi, 2, rows, width).transpose(1, 0, 2, 3)
-    by_core = by_core.reshape(2, n_hi * rows, width)
     cols = out_weight.shape[1]
     vmem = pl.BlockSpec(memory_space=pltpu.VMEM)
     return pl.pallas_call(
-        functools.partial(project_kernel, n_hi),
+        functools.partial(project_kernel, na, n_hi),
         out_shape=jax.ShapeDtypeStruct((rows, cols), jnp.bfloat16),
-        in_specs=[vmem, vmem],
+        in_specs=[vmem, vmem, vmem],
         out_specs=vmem,
         scratch_shapes=[
-            pltpu.VMEM((n_hi * rows, cols), jnp.bfloat16),
-            pltpu.VMEM((n_hi * rows, cols), jnp.bfloat16),
-            pltpu.VMEM((n_hi * rows, cols), jnp.float32),
+            pltpu.VMEM((na - 1,) + parts.shape[1:], parts.dtype),
+            pltpu.VMEM((na - 1,) + stats.shape[1:], stats.dtype),
+            pltpu.VMEM((block_rows, cols), jnp.float32),
+            pltpu.VMEM((n_hi, rows, cols), jnp.bfloat16),
+            pltpu.VMEM((n_hi, rows, cols), jnp.bfloat16),
+            pltpu.VMEM((n_hi, rows, cols), jnp.float32),
             pltpu.VMEM((n_hi, rows, cols), jnp.bfloat16),
             pltpu.VMEM((n_hi - 1, rows, cols), jnp.bfloat16),
+            pltpu.SemaphoreType.DMA((2, na - 1)),
+            pltpu.SemaphoreType.DMA((2, na - 1)),
             pltpu.SemaphoreType.DMA((2,)),
             pltpu.SemaphoreType.DMA((n_hi - 1,)),
             pltpu.SemaphoreType.DMA((n_hi - 1,)),
         ],
         compiler_params=pltpu.CompilerParams(collective_id=1, has_side_effects=True),
-    )(by_core, out_weight)
+    )(parts, stats, out_weight)
 
 
 def local(query_vectors, key_vectors, value_vectors, out_weight):
@@ -220,17 +260,8 @@
 
     row_peak, row_total, weighted = attend_local(query_heads, kv[0], kv[1], score_scale)
     stats = jnp.stack([row_peak, row_total], axis=0).reshape(2, own_heads, ca_count, block_rows)
-    stats = lax.all_to_all(stats.transpose(2, 0, 1, 3), "ca", 0, 0, tiled=True)
     parts = weighted.astype(jnp.bfloat16).reshape(own_heads, ca_count, block_rows, HD)
-    parts = lax.all_to_all(parts.transpose(1, 0, 2, 3), "ca", 0, 0, tiled=True)
-    top_peak = jnp.max(stats[:, 0], axis=0)
-    factor = jnp.exp(stats[:, 0] - top_peak[None])
-    totals = jnp.sum(stats[:, 1] * factor, axis=0)
-    numerator = jnp.sum(parts.astype(jnp.float32) * factor[..., None], axis=0)
-    attended = (numerator / totals[..., None]).astype(jnp.bfloat16)
-    attended = attended.transpose(1, 0, 2).reshape(block_rows, own_cols)
-
-    return project(attended, out_weight, tp_count)
+    return project(parts.transpose(1, 0, 2, 3), stats.transpose(2, 0, 1, 3), out_weight, tp_count)
 
 
 def solution(mesh):

time: 129 us -> 107 us (0.83)
  waiting for transfers between devices: 8.91 us -> 0 us
  starting transfers between devices: 8.41 us -> 0 us
  local copies, waits for them, and re-layouts: 15.7 us -> 9.63 us
  Pallas kernels: 62.6 us -> 68.3 us
  matrix products: 9.32 us -> 4.9 us
    all_to_all x2 -> x0, waiting for transfers between devices: 8.91 us -> none  [the longest x1 8.91 us: local(): parts = lax.all_to_all(parts.transpose(1, 0, 2, 3), 'ca', 0, 0, tiled=True)]
    all_to_all x2 -> x0, starting transfers between devices: 8.41 us -> none  [the longest x1 5.07 us: local(): parts = lax.all_to_all(parts.transpose(1, 0, 2, 3), 'ca', 0, 0, tiled=True)]
    pallas_call x1, Pallas kernels: 32.4 us -> 38.1 us  [project(): pl.pallas_call(functools.partial(project_kernel, na, n_hi), out_shape=jax...]
    unnamed x8 -> x4, local copies, waits for them, and re-layouts: 8.89 us -> 4.32 us
    dot_general x1, matrix products: 7.51 us -> 3.09 us  [attend_local(): jnp.einsum('hij,hjd->hid', weights_low, value_heads, preferred_element_ty...]
  transfers between devices with their start and end apart: 2 -> 0, of which waited for: 1 -> 0; matrix products, arithmetic and copies ran while one was open for 7% -> 0% of each run, Pallas kernels for 0% -> 0%
where the time goes in v5:
time: 107 us; the launch traced here: 106 us
  Pallas kernels  68.3 us (64%)
  blocking collectives  20.6 us (19%)
  local copies, waits for them, and re-layouts  9.63 us (9%)
  matrix products  4.9 us (5%)
  other arithmetic  2.73 us (3%)
    pallas_call x1, Pallas kernels, project(): pl.pallas_call(functools.partial(project_kernel, na, n_hi), out_shape=jax...  38.1 us
    pallas_call x1, Pallas kernels, exchange(): pl.pallas_call(functools.partial(exchange_kernel, na, nz), out_shape=(jax...  30.2 us
    all_to_all x1, blocking collectives, local(): block = lax.all_to_all(qkv, 'tp', 2, 0, tiled=True)  20.6 us
    unnamed x4, local copies, waits for them, and re-layouts  4.32 us
    dot_general x1, matrix products, attend_local(): jnp.einsum('hij,hjd->hid', weights_low, value_heads, preferred_element_ty...  3.09 us

profile of v5, /device:TPU:1, one launch (start us, length us, event | category | flops | bytes accessed | tf_op | source)
XLA Modules:
  0.0 106.3 jit_solution(5873134909288944048)
XLA Ops:
  0.0 0.9 copy.31
  0.9 0.9 copy.32
  1.8 0.9 copy.33
  2.8 20.6 %all_to_all.15 = bf16[16,3,8,384]{3,0,1,2:T(8,128)(2,1)S(1)} all-to-all(bf16[16,3,8,384]{3,0,1,2:T(8,128)(2,1)S(1)} %copy.22), channel_id=1, replica_groups=mesh['ca'=8,'cz'=8,'tp'=8] {'tp'}, dimensions={2} | all-to-all | bytes 589824 | tf_op jit(solution)/shard_map/all_to_all | solution.py:253
  23.5 0.1 reshape.28
  23.6 0.6 slice_bitcast_fusion.q_ref
  24.3 0.7 slice.19.kv_ref
  24.9 30.2 %shard_map.46 = (bf16[8,3,128,128]{3,2,1,0:T(8,128)(2,1)}, bf16[8,2,3,128,128]{4,3,2,1,0:T(8,128)(2,1)}) custom-call(bf16[3,128,128]{2,1,0:T(8,128)(2,1)} %slice_bitcast_fusion.q_ref, bf16[2,3,128,128]{3,2,1,0:T(8,128)(2,1)} %slice.19.kv_ref), custom_call_target="tpu_custom_call" | custom-call | tf_op jit(solution)/shard_map/pallas_call | solution.py:106
  55.2 1.2 %copy.25 = bf16[3,8,128,128]{3,2,1,0:T(8,128)(2,1)S(1)} copy(bf16[3,8,128,128]{3,2,0,1:T(8,128)(2,1)} %bitcast.49) | data formatting | bytes 1572864 | tf_op jit(solution)/shard_map/transpose | solution.py:258
  56.4 1.5 %fusion.1 = (bf16[1,3,8,128,128]{4,3,1,0,2:T(8,128)(2,1)S(1)}, bf16[1,3,8,128,128]{4,3,1,0,2:T(8,128)(2,1)S(1)}) fusion(bf16[2,3,8,128,128]{4,3,1,0,2:T(8,128)(2,1)} %bitcast.45), kind=kLoop, calls=%fused_computation.10 | loop fusion | bytes 3145728 | tf_op jit(solution)/shard_map/slice | solution.py:261
  57.9 0.1 copy.26
  58.0 0.1 copy.27
  58.0 1.8 %multiply_reduce_fusion = (f32[3,1024]{1,0:T(4,128)S(1)}, f32[3,1024,1024]{1,2,0:T(8,128)S(1)}) fusion(bf16[3,1024,128]{2,1,0:T(8,128)(2,1)S(1)} %bitcast.40, bf16[3,1024,128]{2,1,0:T(8,128)(2,1)S(1)} %bitcast.41), kind=kOutput, calls=%fused_computation.2 | convolution fusion | flops 811594752 | bytes 14168064 | tf_op jit(solution)/shard_map/hid,hjd->hij/dot_general | solution.py:18
  59.9 2.1 %convert_reduce_fusion = f32[3,1024]{1,0:T(4,128)S(1)} fusion(f32[3,1024]{1,0:T(4,128)S(1)} %get-tuple-element.11, f32[3,1024,1024]{1,2,0:T(8,128)S(1)} %get-tuple-element.12), kind=kLoop, calls=%fused_computation | loop fusion | flops 15725568 | bytes 12607488 | tf_op jit(solution)/shard_map/reduce_sum | solution.py:23
  61.9 3.1 %convolution_convert_fusion = bf16[3,1024,128]{2,1,0:T(8,128)(2,1)S(1)} fusion(bf16[3,1024,128]{2,1,0:T(8,128)(2,1)S(1)} %bitcast.43, f32[3,1024,1024]{1,2,0:T(8,128)S(1)} %get-tuple-element.12, f32[3,1024]{1,0:T(4,128)S(1)} %get-tuple-element.11), kind=kOutput, calls=%fused_computation.3 | convolution fusion | flops 815136768 | bytes 14168064 | tf_op jit(solution)/shard_map/hij,hjd->hid/dot_general | solution.py:24
  65.0 1.0 copy.36
  66.0 0.6 maximum_bitcast_fusion.stats_ref
  66.6 38.1 %shard_map.47 = bf16[16,5120]{1,0:T(8,128)(2,1)} custom-call(bf16[8,3,128,128]{3,2,1,0:T(8,128)(2,1)} %bitcast.42, f32[8,2,3,128]{3,2,1,0:T(4,128)} %maximum_bitcast_fusion.stats_ref, bf16[384,5120]{1,0:T(8,128)(2,1)} %w_ref.1), custom_call_target="tpu_custom_call" | custom-call | tf_op jit(solution)/shard_map/pallas_call | solution.py:219
  104.7 1.6 %copy.39 = bf16[16,5120]{1,0:T(8,128)(2,1)} copy(bf16[16,5120]{1,0:T(8,128)(2,1)} %shard_map.47) | data formatting | bytes 327680
  (4 shorter events, 0.2 us)

commit v6 on v5

--- a/solution.py
+++ b/solution.py
@@ -33,95 +33,109 @@
     return lax.all_to_all(spread, axis_name, 0, 0, tiled=True)
 
 
-def exchange_kernel(na, nz, q_ref, kv_ref, q_out, kv_out, q_send, q_recv, r_send, r_recv,
-                    l_send, l_recv, own_sem):
+def exchange_kernel(na, nz, nt, staged, q_out, kv_out, tq_sems, tkv_sems, own_sems, q_sems,
+                    r_sems, l_sems):
     mesh_ids = pl.DeviceIdType.MESH
     a = lax.axis_index("ca")
     z = lax.axis_index("cz")
     t = lax.axis_index("tp")
     right = lax.rem(z + 1, nz)
     left = lax.rem(z + nz - 1, nz)
+    rows = staged.shape[3]
 
     barrier = pltpu.get_barrier_semaphore()
+    for off in range(1, nt):
+        pl.semaphore_signal(barrier, inc=1, device_id=(a, z, lax.rem(t + off, nt)),
+                            device_id_type=mesh_ids)
     for off in range(1, na):
         pl.semaphore_signal(barrier, inc=1, device_id=(lax.rem(a + off, na), z, t),
                             device_id_type=mesh_ids)
     for side in (left, right):
         pl.semaphore_signal(barrier, inc=1, device_id=(a, side, t), device_id_type=mesh_ids)
-    pl.semaphore_wait(barrier, na - 1 + 2)
-
+    pl.semaphore_wait(barrier, nt - 1 + na - 1 + 2)
+
+    mine = pl.ds(pl.multiple_of(t * rows, rows), rows)
     own = [
-        pltpu.make_async_copy(q_ref, q_out.at[a], own_sem.at[0]),
-        pltpu.make_async_copy(kv_ref, kv_out.at[z], own_sem.at[1]),
+        pltpu.make_async_copy(staged.at[t, 0], q_out.at[a, :, mine], own_sems.at[0]),
+        pltpu.make_async_copy(staged.at[t, pl.ds(1, 2)], kv_out.at[z, :, :, mine], own_sems.at[1]),
     ]
     for copy in own:
         copy.start()
+    spread = []
+    for off in range(1, nt):
+        dest = lax.rem(t + off, nt)
+        spread.append(pltpu.make_async_remote_copy(
+            src_ref=staged.at[dest, 0], dst_ref=q_out.at[a, :, mine],
+            send_sem=tq_sems.at[0, off - 1], recv_sem=tq_sems.at[1, off - 1],
+            device_id=(a, z, dest), device_id_type=mesh_ids))
+        spread.append(pltpu.make_async_remote_copy(
+            src_ref=staged.at[dest, pl.ds(1, 2)], dst_ref=kv_out.at[z, :, :, mine],
+            send_sem=tkv_sems.at[0, off - 1], recv_sem=tkv_sems.at[1, off - 1],
+            device_id=(a, z, dest), device_id_type=mesh_ids))
+    for copy in spread:
+        copy.start()
+    for copy in spread:
+        copy.wait()
+    for copy in own:
+        copy.wait()
+
     q_copies = []
     for off in range(1, na):
         copy = pltpu.make_async_remote_copy(
-            src_ref=q_ref, dst_ref=q_out.at[a], send_sem=q_send.at[off - 1],
-            recv_sem=q_recv.at[off - 1], device_id=(lax.rem(a + off, na), z, t),
+            src_ref=q_out.at[a], dst_ref=q_out.at[a], send_sem=q_sems.at[0, off - 1],
+            recv_sem=q_sems.at[1, off - 1], device_id=(lax.rem(a + off, na), z, t),
             device_id_type=mesh_ids)
         copy.start()
         q_copies.append(copy)
 
     n_right = nz // 2
     n_left = (nz - 1) // 2
-    right_copies = []
-    left_copies = []
-    for step in range(max(n_right, n_left)):
-        if step < n_right:
-            slot = lax.rem(z - step + nz, nz)
-            if step > 0:
-                right_copies[step - 1].wait_recv()
-            copy = pltpu.make_async_remote_copy(
-                src_ref=kv_ref if step == 0 else kv_out.at[slot], dst_ref=kv_out.at[slot],
-                send_sem=r_send.at[step], recv_sem=r_recv.at[step], device_id=(a, right, t),
-                device_id_type=mesh_ids)
-            copy.start()
-            right_copies.append(copy)
-        if step < n_left:
-            slot = lax.rem(z + step, nz)
-            if step > 0:
-                left_copies[step - 1].wait_recv()
-            copy = pltpu.make_async_remote_copy(
-                src_ref=kv_ref if step == 0 else kv_out.at[slot], dst_ref=kv_out.at[slot],
-                send_sem=l_send.at[step], recv_sem=l_recv.at[step], device_id=(a, left, t),
-                device_id_type=mesh_ids)
-            copy.start()
-            left_copies.append(copy)
-    right_copies[-1].wait_recv()
-    left_copies[-1].wait_recv()
-    for copy in right_copies + left_copies:
-        copy.wait_send()
+    chains = ((right, n_right, r_sems, -1, []), (left, n_left, l_sems, 1, []))
+    for step in range(n_right):
+        for part in range(2):
+            for side, count, sems, sign, copies in chains:
+                if step >= count:
+                    continue
+                slot = lax.rem(z + sign * step + nz, nz)
+                if step > 0:
+                    copies[(step - 1) * 2 + part].wait_recv()
+                copy = pltpu.make_async_remote_copy(
+                    src_ref=kv_out.at[slot, part], dst_ref=kv_out.at[slot, part],
+                    send_sem=sems.at[0, step * 2 + part], recv_sem=sems.at[1, step * 2 + part],
+                    device_id=(a, side, t), device_id_type=mesh_ids)
+                copy.start()
+                copies.append(copy)
+    for side, count, sems, sign, copies in chains:
+        copies[-2].wait_recv()
+        copies[-1].wait_recv()
+        for copy in copies:
+            copy.wait_send()
     for copy in q_copies:
         copy.wait()
-    for copy in own:
-        copy.wait()
-
-
-def exchange(q_blk, kv_blk, na, nz):
+
+
+def exchange(staged, na, nz):
+    nt, _, heads, rows, width = staged.shape
     n_right = nz // 2
     n_left = (nz - 1) // 2
     return pl.pallas_call(
-        functools.partial(exchange_kernel, na, nz),
+        functools.partial(exchange_kernel, na, nz, nt),
         out_shape=(
-            jax.ShapeDtypeStruct((na,) + q_blk.shape, q_blk.dtype),
-            jax.ShapeDtypeStruct((nz,) + kv_blk.shape, kv_blk.dtype),
+            jax.ShapeDtypeStruct((na, heads, nt * rows, width), staged.dtype),
+            jax.ShapeDtypeStruct((nz, 2, heads, nt * rows, width), staged.dtype),
         ),
-        in_specs=[pl.BlockSpec(memory_space=pl.ANY)] * 2,
+        in_specs=[pl.BlockSpec(memory_space=pl.ANY)],
         out_specs=(pl.BlockSpec(memory_space=pl.ANY), pl.BlockSpec(memory_space=pl.ANY)),
         scratch_shapes=[
-            pltpu.SemaphoreType.DMA((na - 1,)),
-            pltpu.SemaphoreType.DMA((na - 1,)),
-            pltpu.SemaphoreType.DMA((n_right,)),
-            pltpu.SemaphoreType.DMA((n_right,)),
-            pltpu.SemaphoreType.DMA((n_left,)),
-            pltpu.SemaphoreType.DMA((n_left,)),
+            pltpu.SemaphoreType.DMA((2, nt - 1)),
+            pltpu.SemaphoreType.DMA((2, nt - 1)),
             pltpu.SemaphoreType.DMA((2,)),
+            pltpu.SemaphoreType.DMA((2, na - 1)),
+            pltpu.SemaphoreType.DMA((2, 2 * n_right)),
+            pltpu.SemaphoreType.DMA((2, 2 * n_left)),
         ],
         compiler_params=pltpu.CompilerParams(collective_id=0, has_side_effects=True),
-    )(q_blk, kv_blk)
+    )(staged)
 
 
 def project_kernel(na, n_hi, parts_ref, stats_ref, w_ref, out_ref, got_parts, got_stats, full,
@@ -248,13 +262,10 @@
     own_heads = query_vectors.shape[1] // HD // tp_count
     own_cols = own_heads * HD
 
-    qkv = jnp.stack([query_vectors, key_vectors, value_vectors], axis=1)
-    qkv = qkv.reshape(token_rows, 3, tp_count, own_cols)
-    block = lax.all_to_all(qkv, "tp", 2, 0, tiled=True)
-    block_rows = block.shape[0]
-    block = block.reshape(block_rows, 3, own_heads, HD).transpose(1, 2, 0, 3)
-
-    query_heads, kv = exchange(block[0], block[1:], ca_count, lax.axis_size("cz"))
+    qkv = jnp.stack([query_vectors, key_vectors, value_vectors], axis=0)
+    staged = qkv.reshape(3, token_rows, tp_count, own_heads, HD).transpose(2, 0, 3, 1, 4)
+    block_rows = token_rows * tp_count
+    query_heads, kv = exchange(staged, ca_count, lax.axis_size("cz"))
     query_heads = query_heads.transpose(1, 0, 2, 3).reshape(own_heads, ca_count * block_rows, HD)
     kv = kv.transpose(1, 2, 0, 3, 4).reshape(2, own_heads, -1, HD)
 

time: 107 us -> 99.8 us (0.933)
  blocking collectives: 20.6 us -> 0 us
  Pallas kernels: 68.3 us -> 81.8 us
    all_to_all x1 -> x0, blocking collectives: 20.6 us -> none  [local(): block = lax.all_to_all(qkv, 'tp', 2, 0, tiled=True)]
    pallas_call x1, Pallas kernels: 30.2 us -> 44.4 us  [exchange(): pl.pallas_call(functools.partial(exchange_kernel, na, nz, nt), out_shape=...]
    another operation x1 -> x6, local copies, waits for them, and re-layouts: 0.04 us -> 3.25 us  [local(): qkv = jnp.stack([query_vectors, key_vectors, value_vectors], axis=0)]
    unnamed x4 -> x1, local copies, waits for them, and re-layouts: 4.32 us -> 1.59 us
where the time goes in v6:
time: 99.8 us; the launch traced here: 98.9 us
  Pallas kernels  81.8 us (82%)
  local copies, waits for them, and re-layouts  8.61 us (9%)
  matrix products  4.9 us (5%)
  other arithmetic  3.44 us (3%)
    pallas_call x1, Pallas kernels, exchange(): pl.pallas_call(functools.partial(exchange_kernel, na, nz, nt), out_shape=...  44.4 us
    pallas_call x1, Pallas kernels, project(): pl.pallas_call(functools.partial(project_kernel, na, n_hi), out_shape=jax...  37.4 us
    another operation x6, local copies, waits for them, and re-layouts, local(): qkv = jnp.stack([query_vectors, key_vectors, value_vectors], axis=0)  3.25 us
    dot_general x1, matrix products, attend_local(): jnp.einsum('hij,hjd->hid', weights_low, value_heads, preferred_element_ty...  3.09 us
    reduce_sum x1, other arithmetic, attend_local(): row_total = jnp.sum(weights_low.astype(jnp.float32), axis=-1)  2.06 us

profile of v6, /device:TPU:1, one launch (start us, length us, event | category | flops | bytes accessed | tf_op | source)
XLA Modules:
  0.0 98.9 jit_solution(4072948460712960606)
XLA Ops:
  0.0 1.0 %stack.21 = bf16[1,16,8,3,128]{4,3,2,1,0:T(4,128)(2,1)S(1)} reshape(bf16[16,3072]{1,0:T(8,128)(2,1)} %param.4) | data formatting | bytes 196608 | tf_op jit(solution)/shard_map/stack | solution.py:265
  1.0 0.1 copy.6
  1.1 1.0 %stack.22 = bf16[1,16,8,3,128]{4,3,2,1,0:T(4,128)(2,1)S(1)} reshape(bf16[16,3072]{1,0:T(8,128)(2,1)} %param.5) | data formatting | bytes 196608 | tf_op jit(solution)/shard_map/stack | solution.py:265
  2.1 0.1 copy.7
  2.2 1.0 %stack.23 = bf16[1,16,8,3,128]{4,3,2,1,0:T(4,128)(2,1)S(1)} reshape(bf16[16,3072]{1,0:T(8,128)(2,1)} %param.6) | data formatting | bytes 196608 | tf_op jit(solution)/shard_map/stack | solution.py:265
  3.2 0.1 copy.8
  3.3 0.8 maximum_bitcast_fusion.staged
  4.1 44.4 %shard_map.46 = (bf16[8,3,128,128]{3,2,1,0:T(8,128)(2,1)}, bf16[8,2,3,128,128]{4,3,2,1,0:T(8,128)(2,1)}) custom-call(bf16[8,3,3,16,128]{4,3,2,1,0:T(8,128)(2,1)} %maximum_bitcast_fusion.staged), custom_call_target="tpu_custom_call" | custom-call | tf_op jit(solution)/shard_map/pallas_call | solution.py:121
  48.5 1.2 %copy.9 = bf16[3,8,128,128]{3,2,1,0:T(8,128)(2,1)S(1)} copy(bf16[3,8,128,128]{3,2,0,1:T(8,128)(2,1)} %bitcast.24) | data formatting | bytes 1572864 | tf_op jit(solution)/shard_map/transpose | solution.py:269
  49.7 1.5 %fusion.1 = (bf16[1,3,8,128,128]{4,3,1,0,2:T(8,128)(2,1)S(1)}, bf16[1,3,8,128,128]{4,3,1,0,2:T(8,128)(2,1)S(1)}) fusion(bf16[2,3,8,128,128]{4,3,1,0,2:T(8,128)(2,1)} %bitcast.23), kind=kLoop, calls=%fused_computation.8 | loop fusion | bytes 3145728 | tf_op jit(solution)/shard_map/slice | solution.py:272
  51.2 0.1 copy.10
  51.3 0.1 copy.11
  51.3 1.8 %multiply_reduce_fusion = (f32[3,1024]{1,0:T(4,128)S(1)}, f32[3,1024,1024]{1,2,0:T(8,128)S(1)}) fusion(bf16[3,1024,128]{2,1,0:T(8,128)(2,1)S(1)} %bitcast.18, bf16[3,1024,128]{2,1,0:T(8,128)(2,1)S(1)} %bitcast.19), kind=kOutput, calls=%fused_computation.2 | convolution fusion | flops 811594752 | bytes 14168064 | tf_op jit(solution)/shard_map/hid,hjd->hij/dot_general | solution.py:18
  53.1 3.1 %convolution_convert_fusion = bf16[3,1024,128]{2,1,0:T(8,128)(2,1)S(1)} fusion(bf16[3,1024,128]{2,1,0:T(8,128)(2,1)S(1)} %bitcast.21, f32[3,1024,1024]{1,2,0:T(8,128)S(1)} %get-tuple-element.12, f32[3,1024]{1,0:T(4,128)S(1)} %get-tuple-element.11), kind=kOutput, calls=%fused_computation.3 | convolution fusion | flops 815136768 | bytes 14168064 | tf_op jit(solution)/shard_map/hij,hjd->hid/dot_general | solution.py:24
  56.2 2.1 %convert_reduce_fusion = f32[3,1024]{1,0:T(4,128)S(1)} fusion(f32[3,1024]{1,0:T(4,128)S(1)} %get-tuple-element.11, f32[3,1024,1024]{1,2,0:T(8,128)S(1)} %get-tuple-element.12), kind=kLoop, calls=%fused_computation | loop fusion | flops 15725568 | bytes 12607488 | tf_op jit(solution)/shard_map/reduce_sum | solution.py:23
  58.3 0.9 copy.16
  59.2 0.6 maximum_bitcast_fusion.1.stats_ref
  59.8 37.4 %shard_map.47 = bf16[16,5120]{1,0:T(8,128)(2,1)} custom-call(bf16[8,3,128,128]{3,2,1,0:T(8,128)(2,1)} %bitcast.20, f32[8,2,3,128]{3,2,1,0:T(4,128)} %maximum_bitcast_fusion.1.stats_ref, bf16[384,5120]{1,0:T(8,128)(2,1)} %w_ref.1), custom_call_target="tpu_custom_call" | custom-call | tf_op jit(solution)/shard_map/pallas_call | solution.py:233
  97.3 1.6 %copy.18 = bf16[16,5120]{1,0:T(8,128)(2,1)} copy(bf16[16,5120]{1,0:T(8,128)(2,1)} %shard_map.47) | data formatting | bytes 327680

commit v7 on v6

--- a/solution.py
+++ b/solution.py
@@ -33,14 +33,15 @@
     return lax.all_to_all(spread, axis_name, 0, 0, tiled=True)
 
 
-def exchange_kernel(na, nz, nt, staged, q_out, kv_out, tq_sems, tkv_sems, own_sems, q_sems,
-                    r_sems, l_sems):
+def attend_kernel(na, nz, nt, score_scale, staged, parts_out, peak_out, total_out, q_buf,
+                  kv_buf, acc, tq_sems, tkv_sems, own_sems, q_sems, r_sems, l_sems):
     mesh_ids = pl.DeviceIdType.MESH
     a = lax.axis_index("ca")
     z = lax.axis_index("cz")
     t = lax.axis_index("tp")
     right = lax.rem(z + 1, nz)
     left = lax.rem(z + nz - 1, nz)
+    heads = staged.shape[2]
     rows = staged.shape[3]
 
     barrier = pltpu.get_barrier_semaphore()
@@ -56,8 +57,8 @@
 
     mine = pl.ds(pl.multiple_of(t * rows, rows), rows)
     own = [
-        pltpu.make_async_copy(staged.at[t, 0], q_out.at[a, :, mine], own_sems.at[0]),
-        pltpu.make_async_copy(staged.at[t, pl.ds(1, 2)], kv_out.at[z, :, :, mine], own_sems.at[1]),
+        pltpu.make_async_copy(staged.at[t, 0], q_buf.at[a, :, mine], own_sems.at[0]),
+        pltpu.make_async_copy(staged.at[t, pl.ds(1, 2)], kv_buf.at[z, :, :, mine], own_sems.at[1]),
     ]
     for copy in own:
         copy.start()
@@ -65,15 +66,18 @@
     for off in range(1, nt):
         dest = lax.rem(t + off, nt)
         spread.append(pltpu.make_async_remote_copy(
-            src_ref=staged.at[dest, 0], dst_ref=q_out.at[a, :, mine],
+            src_ref=staged.at[dest, 0], dst_ref=q_buf.at[a, :, mine],
             send_sem=tq_sems.at[0, off - 1], recv_sem=tq_sems.at[1, off - 1],
             device_id=(a, z, dest), device_id_type=mesh_ids))
         spread.append(pltpu.make_async_remote_copy(
-            src_ref=staged.at[dest, pl.ds(1, 2)], dst_ref=kv_out.at[z, :, :, mine],
+            src_ref=staged.at[dest, pl.ds(1, 2)], dst_ref=kv_buf.at[z, :, :, mine],
             send_sem=tkv_sems.at[0, off - 1], recv_sem=tkv_sems.at[1, off - 1],
             device_id=(a, z, dest), device_id_type=mesh_ids))
     for copy in spread:
         copy.start()
+    peak_out[...] = jnp.full(peak_out.shape, -1e30, jnp.float32)
+    total_out[...] = jnp.zeros(total_out.shape, jnp.float32)
+    acc[...] = jnp.zeros(acc.shape, jnp.float32)
     for copy in spread:
         copy.wait()
     for copy in own:
@@ -82,16 +86,36 @@
     q_copies = []
     for off in range(1, na):
         copy = pltpu.make_async_remote_copy(
-            src_ref=q_out.at[a], dst_ref=q_out.at[a], send_sem=q_sems.at[0, off - 1],
+            src_ref=q_buf.at[a], dst_ref=q_buf.at[a], send_sem=q_sems.at[0, off - 1],
             recv_sem=q_sems.at[1, off - 1], device_id=(lax.rem(a + off, na), z, t),
             device_id_type=mesh_ids)
         copy.start()
         q_copies.append(copy)
 
+    def absorb(slot):
+        def body(c, carry):
+            for h in range(heads):
+                query = q_buf[c, h]
+                scores = lax.dot_general(
+                    query, kv_buf[slot, 0, h], (((1,), (1,)), ((), ())),
+                    preferred_element_type=jnp.float32) * score_scale
+                old_peak = peak_out[c, h]
+                new_peak = jnp.maximum(old_peak, jnp.max(scores, axis=-1, keepdims=True))
+                weights_low = jnp.exp(scores - new_peak).astype(jnp.bfloat16)
+                shrink = jnp.exp(old_peak - new_peak)
+                total_out[c, h] = total_out[c, h] * shrink + jnp.sum(
+                    weights_low.astype(jnp.float32), axis=-1, keepdims=True)
+                acc[c, h] = acc[c, h] * shrink + jnp.dot(
+                    weights_low, kv_buf[slot, 1, h], preferred_element_type=jnp.float32)
+                peak_out[c, h] = new_peak
+            return carry
+        lax.fori_loop(0, na, body, 0)
+
     n_right = nz // 2
     n_left = (nz - 1) // 2
     chains = ((right, n_right, r_sems, -1, []), (left, n_left, l_sems, 1, []))
-    for step in range(n_right):
+
+    def ring_step(step):
         for part in range(2):
             for side, count, sems, sign, copies in chains:
                 if step >= count:
@@ -100,33 +124,51 @@
                 if step > 0:
                     copies[(step - 1) * 2 + part].wait_recv()
                 copy = pltpu.make_async_remote_copy(
-                    src_ref=kv_out.at[slot, part], dst_ref=kv_out.at[slot, part],
+                    src_ref=kv_buf.at[slot, part], dst_ref=kv_buf.at[slot, part],
                     send_sem=sems.at[0, step * 2 + part], recv_sem=sems.at[1, step * 2 + part],
                     device_id=(a, side, t), device_id_type=mesh_ids)
                 copy.start()
                 copies.append(copy)
+
+    ring_step(0)
+    for copy in q_copies:
+        copy.wait()
+    absorb(z)
+    for step in range(1, n_right + 1):
+        if step < n_right:
+            ring_step(step)
+        for side, count, sems, sign, copies in chains:
+            if step == count:
+                copies[-2].wait_recv()
+                copies[-1].wait_recv()
+        absorb(lax.rem(z - step + nz, nz))
+        if step <= n_left:
+            absorb(lax.rem(z + step, nz))
     for side, count, sems, sign, copies in chains:
-        copies[-2].wait_recv()
-        copies[-1].wait_recv()
         for copy in copies:
             copy.wait_send()
-    for copy in q_copies:
-        copy.wait()
-
-
-def exchange(staged, na, nz):
+    parts_out[...] = acc[...].astype(parts_out.dtype)
+
+
+def attend(staged, na, nz, score_scale):
     nt, _, heads, rows, width = staged.shape
     n_right = nz // 2
     n_left = (nz - 1) // 2
+    block = nt * rows
+    vmem = pl.BlockSpec(memory_space=pltpu.VMEM)
     return pl.pallas_call(
-        functools.partial(exchange_kernel, na, nz, nt),
+        functools.partial(attend_kernel, na, nz, nt, score_scale),
         out_shape=(
-            jax.ShapeDtypeStruct((na, heads, nt * rows, width), staged.dtype),
-            jax.ShapeDtypeStruct((nz, 2, heads, nt * rows, width), staged.dtype),
+            jax.ShapeDtypeStruct((na, heads, block, width), staged.dtype),
+            jax.ShapeDtypeStruct((na, heads, block, 1), jnp.float32),
+            jax.ShapeDtypeStruct((na, heads, block, 1), jnp.float32),
         ),
         in_specs=[pl.BlockSpec(memory_space=pl.ANY)],
-        out_specs=(pl.BlockSpec(memory_space=pl.ANY), pl.BlockSpec(memory_space=pl.ANY)),
+        out_specs=(vmem, vmem, vmem),
         scratch_shapes=[
+            pltpu.VMEM((na, heads, block, width), staged.dtype),
+            pltpu.VMEM((nz, 2, heads, block, width), staged.dtype),
+            pltpu.VMEM((na, heads, block, width), jnp.float32),
             pltpu.SemaphoreType.DMA((2, nt - 1)),
             pltpu.SemaphoreType.DMA((2, nt - 1)),
             pltpu.SemaphoreType.DMA((2,)),
@@ -265,14 +307,9 @@
     qkv = jnp.stack([query_vectors, key_vectors, value_vectors], axis=0)
     staged = qkv.reshape(3, token_rows, tp_count, own_heads, HD).transpose(2, 0, 3, 1, 4)
     block_rows = token_rows * tp_count
-    query_heads, kv = exchange(staged, ca_count, lax.axis_size("cz"))
-    query_heads = query_heads.transpose(1, 0, 2, 3).reshape(own_heads, ca_count * block_rows, HD)
-    kv = kv.transpose(1, 2, 0, 3, 4).reshape(2, own_heads, -1, HD)
-
-    row_peak, row_total, weighted = attend_local(query_heads, kv[0], kv[1], score_scale)
-    stats = jnp.stack([row_peak, row_total], axis=0).reshape(2, own_heads, ca_count, block_rows)
-    parts = weighted.astype(jnp.bfloat16).reshape(own_heads, ca_count, block_rows, HD)
-    return project(parts.transpose(1, 0, 2, 3), stats.transpose(2, 0, 1, 3), out_weight, tp_count)
+    parts, peak, total = attend(staged, ca_count, lax.axis_size("cz"), score_scale)
+    stats = jnp.stack([peak[..., 0], total[..., 0]], axis=1)
+    return project(parts, stats, out_weight, tp_count)
 
 
 def solution(mesh):

time: 99.8 us -> 151 us (1.51)
  Pallas kernels: 81.8 us -> 141 us
  matrix products: 4.9 us -> 0 us
  other arithmetic: 3.44 us -> 1.39 us
    pallas_call x1, Pallas kernels: 44.4 us -> 104 us  [attend(): pl.pallas_call(functools.partial(attend_kernel, na, nz, nt, score_scale),...]
    dot_general x2 -> x0, matrix products: 4.9 us -> none  [the longest x1 3.09 us: attend_local(): jnp.einsum('hij,hjd->hid', weights_low, value_heads, preferred_element_ty...]
    pallas_call x0 -> x2, local copies, waits for them, and re-layouts: none -> 2.46 us  [attend(): pl.pallas_call(functools.partial(attend_kernel, na, nz, nt, score_scale),...]
    reduce_sum x1 -> x0, other arithmetic: 2.06 us -> none  [attend_local(): row_total = jnp.sum(weights_low.astype(jnp.float32), axis=-1)]
    slice x3 -> x0, local copies, waits for them, and re-layouts: 1.65 us -> none  [the longest x2 1.6 us: local(): kv[0]]
where the time goes in v7:
time: 151 us; the launch traced here: 150 us
  Pallas kernels  141 us (93%)
  local copies, waits for them, and re-layouts  7.33 us (5%)
    pallas_call x1, Pallas kernels, attend(): pl.pallas_call(functools.partial(attend_kernel, na, nz, nt, score_scale),...  104 us
    pallas_call x1, Pallas kernels, project(): pl.pallas_call(functools.partial(project_kernel, na, n_hi), out_shape=jax...  37.5 us
    another operation x6, local copies, waits for them, and re-layouts, local(): qkv = jnp.stack([query_vectors, key_vectors, value_vectors], axis=0)  3.25 us

profile of v7, /device:TPU:1, one launch (start us, length us, event | category | flops | bytes accessed | tf_op | source)
XLA Modules:
  0.0 150.2 jit_solution(12513058045570696763)
XLA Ops:
  0.0 1.0 stack.15
  1.0 0.1 copy.5
  1.1 1.0 stack.16
  2.1 0.1 copy.6
  2.2 1.0 stack.17
  3.2 0.1 copy.7
  3.3 0.7 maximum_bitcast_fusion.staged
  4.0 104.0 %shard_map.46 = (bf16[8,3,128,128]{3,2,1,0:T(8,128)(2,1)}, f32[8,3,128,1]{3,2,1,0:T(8,128)}, f32[8,3,128,1]{3,2,1,0:T(8,128)}) custom-call(bf16[8,3,3,16,128]{4,3,2,1,0:T(8,128)(2,1)} %maximum_bitcast_fusion.staged), custom_call_target="tpu_custom_call" | custom-call | tf_op jit(solution)/shard_map/pallas_call | solution.py:159
  108.0 0.0 copy-start
  108.1 2.0 %copy.8 = f32[8,3,128,1]{2,0,3,1:T(8,128)S(1)} copy(f32[8,3,128,1]{3,2,1,0:T(8,128)} %get-tuple-element.9) | data formatting | bytes 24576 | tf_op jit(solution)/shard_map/pallas_call | solution.py:159
  110.1 0.0 copy-done
  110.1 0.5 copy.9
  110.5 0.6 pad_maximum_fusion.stats_ref
  111.2 37.5 %shard_map.47 = bf16[16,5120]{1,0:T(8,128)(2,1)} custom-call(bf16[8,3,128,128]{3,2,1,0:T(8,128)(2,1)} %get-tuple-element.8.parts_ref, f32[8,2,3,128]{3,2,1,0:T(4,128)} %pad_maximum_fusion.stats_ref, bf16[384,5120]{1,0:T(8,128)(2,1)} %w_ref.1), custom_call_target="tpu_custom_call" | custom-call | tf_op jit(solution)/shard_map/pallas_call | solution.py:275
  148.7 1.6 %copy.13 = bf16[16,5120]{1,0:T(8,128)(2,1)} copy(bf16[16,5120]{1,0:T(8,128)(2,1)} %shard_map.47) | data formatting | bytes 327680
  (2 shorter events, 0.0 us)
Async XLA Ops:
  108.0 2.0 %copy-start = (f32[8,3,128,1]{3,2,1,0:T(8,128)S(1)}, f32[8,3,128,1]{3,2,1,0:T(8,128)}, u32[]{:S(2)}) copy-start(f32[8,3,128,1]{3,2,1,0:T(8,128)} %get-tuple-element.10) | copy-start | bytes 36868

commit v8 on v6

--- a/solution.py
+++ b/solution.py
@@ -33,15 +33,16 @@
     return lax.all_to_all(spread, axis_name, 0, 0, tiled=True)
 
 
-def exchange_kernel(na, nz, nt, staged, q_out, kv_out, tq_sems, tkv_sems, own_sems, q_sems,
-                    r_sems, l_sems):
+def exchange_kernel(na, nz, nt, q_ref, k_ref, v_ref, q_out, kv_out, spread_sems, own_sems,
+                    q_sems, r_sems, l_sems):
     mesh_ids = pl.DeviceIdType.MESH
     a = lax.axis_index("ca")
     z = lax.axis_index("cz")
     t = lax.axis_index("tp")
     right = lax.rem(z + 1, nz)
     left = lax.rem(z + nz - 1, nz)
-    rows = staged.shape[3]
+    rows = q_ref.shape[0]
+    cols = q_out.shape[2]
 
     barrier = pltpu.get_barrier_semaphore()
     for off in range(1, nt):
@@ -55,23 +56,25 @@
     pl.semaphore_wait(barrier, nt - 1 + na - 1 + 2)
 
     mine = pl.ds(pl.multiple_of(t * rows, rows), rows)
-    own = [
-        pltpu.make_async_copy(staged.at[t, 0], q_out.at[a, :, mine], own_sems.at[0]),
-        pltpu.make_async_copy(staged.at[t, pl.ds(1, 2)], kv_out.at[z, :, :, mine], own_sems.at[1]),
-    ]
-    for copy in own:
-        copy.start()
+    targets = (q_out.at[a, mine], kv_out.at[z, 0, mine], kv_out.at[z, 1, mine])
+    sources = (q_ref, k_ref, v_ref)
+
+    def columns(dest):
+        return pl.ds(pl.multiple_of(dest * cols, cols), cols)
+
+    own = []
+    for i in range(3):
+        copy = pltpu.make_async_copy(sources[i].at[:, columns(t)], targets[i], own_sems.at[i])
+        copy.start()
+        own.append(copy)
     spread = []
     for off in range(1, nt):
         dest = lax.rem(t + off, nt)
-        spread.append(pltpu.make_async_remote_copy(
-            src_ref=staged.at[dest, 0], dst_ref=q_out.at[a, :, mine],
-            send_sem=tq_sems.at[0, off - 1], recv_sem=tq_sems.at[1, off - 1],
-            device_id=(a, z, dest), device_id_type=mesh_ids))
-        spread.append(pltpu.make_async_remote_copy(
-            src_ref=staged.at[dest, pl.ds(1, 2)], dst_ref=kv_out.at[z, :, :, mine],
-            send_sem=tkv_sems.at[0, off - 1], recv_sem=tkv_sems.at[1, off - 1],
-            device_id=(a, z, dest), device_id_type=mesh_ids))
+        for i in range(3):
+            spread.append(pltpu.make_async_remote_copy(
+                src_ref=sources[i].at[:, columns(dest)], dst_ref=targets[i],
+                send_sem=spread_sems.at[0, i, off - 1], recv_sem=spread_sems.at[1, i, off - 1],
+                device_id=(a, z, dest), device_id_type=mesh_ids))
     for copy in spread:
         copy.start()
     for copy in spread:
@@ -114,28 +117,29 @@
         copy.wait()
 
 
-def exchange(staged, na, nz):
-    nt, _, heads, rows, width = staged.shape
+def exchange(query_vectors, key_vectors, value_vectors, na, nz, nt):
+    rows, width = query_vectors.shape
+    cols = width // nt
     n_right = nz // 2
     n_left = (nz - 1) // 2
+    dtype = query_vectors.dtype
     return pl.pallas_call(
         functools.partial(exchange_kernel, na, nz, nt),
         out_shape=(
-            jax.ShapeDtypeStruct((na, heads, nt * rows, width), staged.dtype),
-            jax.ShapeDtypeStruct((nz, 2, heads, nt * rows, width), staged.dtype),
+            jax.ShapeDtypeStruct((na, nt * rows, cols), dtype),
+            jax.ShapeDtypeStruct((nz, 2, nt * rows, cols), dtype),
         ),
-        in_specs=[pl.BlockSpec(memory_space=pl.ANY)],
+        in_specs=[pl.BlockSpec(memory_space=pl.ANY)] * 3,
         out_specs=(pl.BlockSpec(memory_space=pl.ANY), pl.BlockSpec(memory_space=pl.ANY)),
         scratch_shapes=[
-            pltpu.SemaphoreType.DMA((2, nt - 1)),
-            pltpu.SemaphoreType.DMA((2, nt - 1)),
-            pltpu.SemaphoreType.DMA((2,)),
+            pltpu.SemaphoreType.DMA((2, 3, nt - 1)),
+            pltpu.SemaphoreType.DMA((3,)),
             pltpu.SemaphoreType.DMA((2, na - 1)),
             pltpu.SemaphoreType.DMA((2, 2 * n_right)),
             pltpu.SemaphoreType.DMA((2, 2 * n_left)),
         ],
         compiler_params=pltpu.CompilerParams(collective_id=0, has_side_effects=True),
-    )(staged)
+    )(query_vectors, key_vectors, value_vectors)
 
 
 def project_kernel(na, n_hi, parts_ref, stats_ref, w_ref, out_ref, got_parts, got_stats, full,
@@ -262,12 +266,11 @@
     own_heads = query_vectors.shape[1] // HD // tp_count
     own_cols = own_heads * HD
 
-    qkv = jnp.stack([query_vectors, key_vectors, value_vectors], axis=0)
-    staged = qkv.reshape(3, token_rows, tp_count, own_heads, HD).transpose(2, 0, 3, 1, 4)
     block_rows = token_rows * tp_count
-    query_heads, kv = exchange(staged, ca_count, lax.axis_size("cz"))
-    query_heads = query_heads.transpose(1, 0, 2, 3).reshape(own_heads, ca_count * block_rows, HD)
-    kv = kv.transpose(1, 2, 0, 3, 4).reshape(2, own_heads, -1, HD)
+    query_rows, kv = exchange(
+        query_vectors, key_vectors, value_vectors, ca_count, lax.axis_size("cz"), tp_count)
+    query_heads = query_rows.reshape(-1, own_heads, HD).transpose(1, 0, 2)
+    kv = kv.transpose(1, 0, 2, 3).reshape(2, -1, own_heads, HD).transpose(0, 2, 1, 3)
 
     row_peak, row_total, weighted = attend_local(query_heads, kv[0], kv[1], score_scale)
     stats = jnp.stack([row_peak, row_total], axis=0).reshape(2, own_heads, ca_count, block_rows)

time: 99.8 us -> 102 us (1.022)
  matrix products: 4.9 us -> 7.11 us
  local copies, waits for them, and re-layouts: 8.61 us -> 9.85 us
    reshape x0 -> x3, local copies, waits for them, and re-layouts: none -> 3.54 us  [the longest x2 2.32 us: local(): kv.transpose(1, 0, 2, 3).reshape(2, -1, own_heads, HD).transpose(0, 2, 1, 3)]
    another operation x6 -> x0, local copies, waits for them, and re-layouts: 3.25 us -> none  [local(): qkv = jnp.stack([query_vectors, key_vectors, value_vectors], axis=0)]
    slice x3 -> x0, local copies, waits for them, and re-layouts: 1.65 us -> none  [the longest x2 1.6 us: local(): kv[0]]
    pallas_call x0 -> x1, local copies, waits for them, and re-layouts: none -> 1.62 us  [exchange(): pl.pallas_call(functools.partial(exchange_kernel, na, nz, nt), out_shape=...]
    dot_general x1, matrix products: 1.81 us -> 3.28 us  [attend_local(): jnp.einsum('hid,hjd->hij', query_heads, key_heads, preferred_element_type...]
where the time goes in v8:
time: 102 us
  Pallas kernels  82.1 us (80%)
  local copies, waits for them, and re-layouts  9.85 us (10%)
  matrix products  7.11 us (7%)
  other arithmetic  2.68 us (3%)
    pallas_call x1, Pallas kernels, exchange(): pl.pallas_call(functools.partial(exchange_kernel, na, nz, nt), out_shape=...  44.6 us
    pallas_call x1, Pallas kernels, project(): pl.pallas_call(functools.partial(project_kernel, na, n_hi), out_shape=jax...  37.5 us
    dot_general x1, matrix products, attend_local(): jnp.einsum('hij,hjd->hid', weights_low, value_heads, preferred_element_ty...  3.83 us
    dot_general x1, matrix products, attend_local(): jnp.einsum('hid,hjd->hij', query_heads, key_heads, preferred_element_type...  3.28 us
    reshape x2, local copies, waits for them, and re-layouts, local(): kv.transpose(1, 0, 2, 3).reshape(2, -1, own_heads, HD).transpose(0, 2, 1, 3)  2.32 us
    transpose x1, local copies, waits for them, and re-layouts, local(): kv.transpose(1, 0, 2, 3).reshape(2, -1, own_heads, HD).transpose(0, 2, 1, 3)  2.15 us
    reduce_sum x1, other arithmetic, attend_local(): row_total = jnp.sum(weights_low.astype(jnp.float32), axis=-1)  2.06 us

profile of v8, /device:TPU:1, one launch (start us, length us, event | category | flops | bytes accessed | tf_op | source)
XLA Modules:
  0.0 101.8 jit_solution(6101988631158565140)
XLA Ops:
  0.0 44.6 %shard_map.46 = (bf16[8,128,384]{2,1,0:T(8,128)(2,1)}, bf16[8,2,128,384]{3,2,1,0:T(8,128)(2,1)}) custom-call(bf16[16,3072]{1,0:T(8,128)(2,1)} %q_ref.1, bf16[16,3072]{1,0:T(8,128)(2,1)} %k_ref.1, bf16[16,3072]{1,0:T(8,128)(2,1)} %v_ref.1), custom_call_target="tpu_custom_call" | custom-call | tf_op jit(solution)/shard_map/pallas_call | solution.py:126
  44.6 1.6 %copy.7 = bf16[8,128,384]{1,0,2:T(8,128)(2,1)S(1)} copy(bf16[8,128,384]{2,1,0:T(8,128)(2,1)} %get-tuple-element.7) | data formatting | bytes 1572864 | tf_op jit(solution)/shard_map/pallas_call | solution.py:126
  46.2 1.2 %reshape.15 = bf16[1024,3,128]{0,2,1:T(8,128)(2,1)} reshape(bf16[8,128,384]{1,0,2:T(8,128)(2,1)S(1)} %copy.7) | data formatting | bytes 1572864 | tf_op jit(solution)/shard_map/reshape | solution.py:272
  47.4 2.2 %copy.8 = bf16[2,8,128,384]{2,1,3,0:T(8,128)(2,1)S(1)} copy(bf16[2,8,128,384]{3,2,0,1:T(8,128)(2,1)} %bitcast.32) | data formatting | bytes 3145728 | tf_op jit(solution)/shard_map/transpose | solution.py:273
  49.6 0.7 reshape.16
  50.3 1.6 %copy.9 = bf16[2,1024,3,128]{3,1,2,0:T(8,128)(2,1)} copy(bf16[2,1024,3,128]{1,3,2,0:T(8,128)(2,1)S(1)} %reshape.16) | data formatting | bytes 3145728 | tf_op jit(solution)/shard_map/reshape | solution.py:273
  51.9 0.0 copy-start
  51.9 3.3 %multiply_reduce_fusion = (f32[3,1024]{1,0:T(4,128)S(1)}, f32[3,1024,1024]{1,2,0:T(8,128)S(1)}) fusion(bf16[1024,3,128]{0,2,1:T(8,128)(2,1)} %reshape.15, bf16[2,3,1024,128]{3,2,1,0:T(8,128)(2,1)} %bitcast.29), kind=kOutput, calls=%fused_computation.2 | convolution fusion | flops 811594752 | bytes 14168064 | tf_op jit(solution)/shard_map/hid,hjd->hij/dot_general | solution.py:18
  55.2 0.0 copy-done
  55.2 3.8 %convolution_convert_fusion = bf16[3,1024,128]{2,1,0:T(8,128)(2,1)} fusion(f32[3,1024,1024]{1,2,0:T(8,128)S(1)} %get-tuple-element.10, f32[3,1024]{1,0:T(4,128)S(1)} %get-tuple-element.9, bf16[2,3,1024,128]{3,2,1,0:T(8,128)(2,1)S(1)} %bitcast.30), kind=kOutput, calls=%fused_computation.3 | convolution fusion | flops 815136768 | bytes 14172160 | tf_op jit(solution)/shard_map/hij,hjd->hid/dot_general | solution.py:24
  59.1 0.0 copy-start.1
  59.1 2.1 %convert_reduce_fusion = f32[3,1024]{1,0:T(4,128)S(1)} fusion(f32[3,1024]{1,0:T(4,128)S(1)} %get-tuple-element.9, f32[3,1024,1024]{1,2,0:T(8,128)S(1)} %get-tuple-element.10), kind=kLoop, calls=%fused_computation | loop fusion | flops 15725568 | bytes 12607488 | tf_op jit(solution)/shard_map/reduce_sum | solution.py:23
  61.1 0.0 copy-done.1
  61.1 0.9 copy.16
  62.1 0.6 maximum_bitcast_fusion.stats_ref
  62.7 37.5 %shard_map.47 = bf16[16,5120]{1,0:T(8,128)(2,1)} custom-call(bf16[8,3,128,128]{3,2,1,0:T(8,128)(2,1)} %bitcast.31, f32[8,2,3,128]{3,2,1,0:T(4,128)} %maximum_bitcast_fusion.stats_ref, bf16[384,5120]{1,0:T(8,128)(2,1)} %w_ref.1), custom_call_target="tpu_custom_call" | custom-call | tf_op jit(solution)/shard_map/pallas_call | solution.py:237
  100.2 1.6 %copy.18 = bf16[16,5120]{1,0:T(8,128)(2,1)} copy(bf16[16,5120]{1,0:T(8,128)(2,1)} %shard_map.47) | data formatting | bytes 327680
Async XLA Ops:
  51.9 3.3 %copy-start = (bf16[2,1024,3,128]{3,1,2,0:T(8,128)(2,1)S(1)}, bf16[2,1024,3,128]{3,1,2,0:T(8,128)(2,1)}, u32[]{:S(2)}) copy-start(bf16[2,1024,3,128]{3,1,2,0:T(8,128)(2,1)} %copy.9) | copy-start | bytes 4718596
  59.1 2.1 %copy-start.1 = (bf16[3,1024,128]{2,1,0:T(8,128)(2,1)S(1)}, bf16[3,1024,128]{2,1,0:T(8,128)(2,1)}, u32[]{:S(2)}) copy-start(bf16[3,1024,128]{2,1,0:T(8,128)(2,1)} %convolution_convert_fusion) | copy-start | bytes 2359300

commit v9 on v8

--- a/solution.py
+++ b/solution.py
@@ -42,7 +42,7 @@
     right = lax.rem(z + 1, nz)
     left = lax.rem(z + nz - 1, nz)
     rows = q_ref.shape[0]
-    cols = q_out.shape[2]
+    heads = q_out.shape[0]
 
     barrier = pltpu.get_barrier_semaphore()
     for off in range(1, nt):
@@ -56,25 +56,33 @@
     pl.semaphore_wait(barrier, nt - 1 + na - 1 + 2)
 
     mine = pl.ds(pl.multiple_of(t * rows, rows), rows)
-    targets = (q_out.at[a, mine], kv_out.at[z, 0, mine], kv_out.at[z, 1, mine])
     sources = (q_ref, k_ref, v_ref)
 
-    def columns(dest):
-        return pl.ds(pl.multiple_of(dest * cols, cols), cols)
+    def target(i, h):
+        if i == 0:
+            return q_out.at[h, a, mine]
+        return kv_out.at[i - 1, h, z, mine]
+
+    def columns(dest, h):
+        return pl.ds(pl.multiple_of((dest * heads + h) * HD, HD), HD)
 
     own = []
     for i in range(3):
-        copy = pltpu.make_async_copy(sources[i].at[:, columns(t)], targets[i], own_sems.at[i])
-        copy.start()
-        own.append(copy)
+        for h in range(heads):
+            copy = pltpu.make_async_copy(
+                sources[i].at[:, columns(t, h)], target(i, h), own_sems.at[i, h])
+            copy.start()
+            own.append(copy)
     spread = []
     for off in range(1, nt):
         dest = lax.rem(t + off, nt)
         for i in range(3):
-            spread.append(pltpu.make_async_remote_copy(
-                src_ref=sources[i].at[:, columns(dest)], dst_ref=targets[i],
-                send_sem=spread_sems.at[0, i, off - 1], recv_sem=spread_sems.at[1, i, off - 1],
-                device_id=(a, z, dest), device_id_type=mesh_ids))
+            for h in range(heads):
+                spread.append(pltpu.make_async_remote_copy(
+                    src_ref=sources[i].at[:, columns(dest, h)], dst_ref=target(i, h),
+                    send_sem=spread_sems.at[0, i, h, off - 1],
+                    recv_sem=spread_sems.at[1, i, h, off - 1],
+                    device_id=(a, z, dest), device_id_type=mesh_ids))
     for copy in spread:
         copy.start()
     for copy in spread:
@@ -85,7 +93,7 @@
     q_copies = []
     for off in range(1, na):
         copy = pltpu.make_async_remote_copy(
-            src_ref=q_out.at[a], dst_ref=q_out.at[a], send_sem=q_sems.at[0, off - 1],
+            src_ref=q_out.at[:, a], dst_ref=q_out.at[:, a], send_sem=q_sems.at[0, off - 1],
             recv_sem=q_sems.at[1, off - 1], device_id=(lax.rem(a + off, na), z, t),
             device_id_type=mesh_ids)
         copy.start()
@@ -103,7 +111,7 @@
                 if step > 0:
                     copies[(step - 1) * 2 + part].wait_recv()
                 copy = pltpu.make_async_remote_copy(
-                    src_ref=kv_out.at[slot, part], dst_ref=kv_out.at[slot, part],
+                    src_ref=kv_out.at[part, :, slot], dst_ref=kv_out.at[part, :, slot],
                     send_sem=sems.at[0, step * 2 + part], recv_sem=sems.at[1, step * 2 + part],
                     device_id=(a, side, t), device_id_type=mesh_ids)
                 copy.start()
@@ -119,21 +127,21 @@
 
 def exchange(query_vectors, key_vectors, value_vectors, na, nz, nt):
     rows, width = query_vectors.shape
-    cols = width // nt
+    heads = width // nt // HD
     n_right = nz // 2
     n_left = (nz - 1) // 2
     dtype = query_vectors.dtype
     return pl.pallas_call(
         functools.partial(exchange_kernel, na, nz, nt),
         out_shape=(
-            jax.ShapeDtypeStruct((na, nt * rows, cols), dtype),
-            jax.ShapeDtypeStruct((nz, 2, nt * rows, cols), dtype),
+            jax.ShapeDtypeStruct((heads, na, nt * rows, HD), dtype),
+            jax.ShapeDtypeStruct((2, heads, nz, nt * rows, HD), dtype),
         ),
         in_specs=[pl.BlockSpec(memory_space=pl.ANY)] * 3,
         out_specs=(pl.BlockSpec(memory_space=pl.ANY), pl.BlockSpec(memory_space=pl.ANY)),
         scratch_shapes=[
-            pltpu.SemaphoreType.DMA((2, 3, nt - 1)),
-            pltpu.SemaphoreType.DMA((3,)),
+            pltpu.SemaphoreType.DMA((2, 3, heads, nt - 1)),
+            pltpu.SemaphoreType.DMA((3, heads)),
             pltpu.SemaphoreType.DMA((2, na - 1)),
             pltpu.SemaphoreType.DMA((2, 2 * n_right)),
             pltpu.SemaphoreType.DMA((2, 2 * n_left)),
@@ -144,7 +152,7 @@
 
 def project_kernel(na, n_hi, parts_ref, stats_ref, w_ref, out_ref, got_parts, got_stats, full,
                    send1, recv1, total, send2, recv2, part_sems, stat_sems, sems1, send_sems2,
-                   recv_sems2):
+                   recv_sems2, own_stat_sem):
     mesh_ids = pl.DeviceIdType.MESH
     a = lax.axis_index("ca")
     z = lax.axis_index("cz")
@@ -153,7 +161,7 @@
     hi = t // 2
     partner = (a, z, hi * 2 + 1 - core)
     rows = send2.shape[1]
-    heads = parts_ref.shape[1]
+    heads = parts_ref.shape[0]
 
     barrier = pltpu.get_barrier_semaphore()
     for off in range(1, na):
@@ -165,20 +173,24 @@
                             device_id_type=mesh_ids)
     pl.semaphore_wait(barrier, na - 1 + n_hi)
 
+    own_stats = pltpu.make_async_copy(stats_ref.at[:, :, a], got_stats.at[na - 1], own_stat_sem)
+    own_stats.start()
     gathered = []
     for off in range(1, na):
         dest = lax.rem(a + off, na)
-        for src, dst, sems in ((parts_ref, got_parts, part_sems), (stats_ref, got_stats, stat_sems)):
+        for src, dst, sems in ((parts_ref.at[:, dest], got_parts, part_sems),
+                               (stats_ref.at[:, :, dest], got_stats, stat_sems)):
             copy = pltpu.make_async_remote_copy(
-                src_ref=src.at[dest], dst_ref=dst.at[off - 1], send_sem=sems.at[0, off - 1],
+                src_ref=src, dst_ref=dst.at[off - 1], send_sem=sems.at[0, off - 1],
                 recv_sem=sems.at[1, off - 1], device_id=(dest, z, t), device_id_type=mesh_ids)
             copy.start()
             gathered.append(copy)
     for copy in gathered:
         copy.wait()
-
-    peaks = [stats_ref[a, 0]] + [got_stats[off - 1, 0] for off in range(1, na)]
-    sums = [stats_ref[a, 1]] + [got_stats[off - 1, 1] for off in range(1, na)]
+    own_stats.wait()
+
+    peaks = [got_stats[na - 1, 0]] + [got_stats[off - 1, 0] for off in range(1, na)]
+    sums = [got_stats[na - 1, 1]] + [got_stats[off - 1, 1] for off in range(1, na)]
     top = peaks[0]
     for peak in peaks[1:]:
         top = jnp.maximum(top, peak)
@@ -187,7 +199,7 @@
     for factor, part_sum in zip(factors[1:], sums[1:]):
         totals = totals + factor * part_sum
     for h in range(heads):
-        numerator = parts_ref[a, h].astype(jnp.float32) * factors[0][h][:, None]
+        numerator = parts_ref[h, a].astype(jnp.float32) * factors[0][h][:, None]
         for off in range(1, na):
             numerator = numerator + (
                 got_parts[off - 1, h].astype(jnp.float32) * factors[off][h][:, None]
@@ -229,7 +241,7 @@
 
 
 def project(parts, stats, out_weight, tp_count):
-    na, heads, block_rows, _ = parts.shape
+    heads, na, block_rows, _ = parts.shape
     n_hi = tp_count // 2
     rows = block_rows // tp_count
     cols = out_weight.shape[1]
@@ -240,8 +252,8 @@
         in_specs=[vmem, vmem, vmem],
         out_specs=vmem,
         scratch_shapes=[
-            pltpu.VMEM((na - 1,) + parts.shape[1:], parts.dtype),
-            pltpu.VMEM((na - 1,) + stats.shape[1:], stats.dtype),
+            pltpu.VMEM((na - 1, heads, block_rows, HD), parts.dtype),
+            pltpu.VMEM((na, 2, heads, block_rows), stats.dtype),
             pltpu.VMEM((block_rows, cols), jnp.float32),
             pltpu.VMEM((n_hi, rows, cols), jnp.bfloat16),
             pltpu.VMEM((n_hi, rows, cols), jnp.bfloat16),
@@ -253,6 +265,7 @@
             pltpu.SemaphoreType.DMA((2,)),
             pltpu.SemaphoreType.DMA((n_hi - 1,)),
             pltpu.SemaphoreType.DMA((n_hi - 1,)),
+            pltpu.SemaphoreType.DMA(()),
         ],
         compiler_params=pltpu.CompilerParams(collective_id=1, has_side_effects=True),
     )(parts, stats, out_weight)
@@ -267,15 +280,15 @@
     own_cols = own_heads * HD
 
     block_rows = token_rows * tp_count
-    query_rows, kv = exchange(
+    query_heads, kv = exchange(
         query_vectors, key_vectors, value_vectors, ca_count, lax.axis_size("cz"), tp_count)
-    query_heads = query_rows.reshape(-1, own_heads, HD).transpose(1, 0, 2)
-    kv = kv.transpose(1, 0, 2, 3).reshape(2, -1, own_heads, HD).transpose(0, 2, 1, 3)
+    query_heads = query_heads.reshape(own_heads, -1, HD)
+    kv = kv.reshape(2, own_heads, -1, HD)
 
     row_peak, row_total, weighted = attend_local(query_heads, kv[0], kv[1], score_scale)
     stats = jnp.stack([row_peak, row_total], axis=0).reshape(2, own_heads, ca_count, block_rows)
     parts = weighted.astype(jnp.bfloat16).reshape(own_heads, ca_count, block_rows, HD)
-    return project(parts.transpose(1, 0, 2, 3), stats.transpose(2, 0, 1, 3), out_weight, tp_count)
+    return project(parts, stats, out_weight, tp_count)
 
 
 def solution(mesh):

time: 102 us -> 96.4 us (0.945)
  local copies, waits for them, and re-layouts: 9.85 us -> 3.1 us
    reshape x4 -> x0, local copies, waits for them, and re-layouts: 4.47 us -> none  [the longest x2 2.32 us: local(): kv.transpose(1, 0, 2, 3).reshape(2, -1, own_heads, HD).transpose(0, 2, 1, 3)]
    transpose x1 -> x0, local copies, waits for them, and re-layouts: 2.15 us -> none  [local(): kv.transpose(1, 0, 2, 3).reshape(2, -1, own_heads, HD).transpose(0, 2, 1, 3)]
    pallas_call x1 -> x0, local copies, waits for them, and re-layouts: 1.62 us -> none  [exchange(): pl.pallas_call(functools.partial(exchange_kernel, na, nz, nt), out_shape=...]
    slice x0 -> x1, local copies, waits for them, and re-layouts: none -> 1.5 us  [local(): kv[0]]
where the time goes in v9:
time: 96.4 us; the launch traced here: 95.8 us
  Pallas kernels  83.1 us (86%)
  matrix products  6.92 us (7%)
  local copies, waits for them, and re-layouts  3.1 us (3%)
  other arithmetic  2.67 us (3%)
    pallas_call x1, Pallas kernels, exchange(): pl.pallas_call(functools.partial(exchange_kernel, na, nz, nt), out_shape=...  45.5 us
    pallas_call x1, Pallas kernels, project(): pl.pallas_call(functools.partial(project_kernel, na, n_hi), out_shape=jax...  37.6 us
    dot_general x1, matrix products, attend_local(): jnp.einsum('hij,hjd->hid', weights_low, value_heads, preferred_element_ty...  3.98 us
    dot_general x1, matrix products, attend_local(): jnp.einsum('hid,hjd->hij', query_heads, key_heads, preferred_element_type...  2.94 us
    reduce_sum x1, other arithmetic, attend_local(): row_total = jnp.sum(weights_low.astype(jnp.float32), axis=-1)  2.06 us

profile of v9, /device:TPU:1, one launch (start us, length us, event | category | flops | bytes accessed | tf_op | source)
XLA Modules:
  0.0 95.8 jit_solution(556756648538787382)
XLA Ops:
  0.0 45.5 %shard_map.46 = (bf16[3,8,128,128]{3,2,1,0:T(8,128)(2,1)}, bf16[2,3,8,128,128]{4,3,2,1,0:T(8,128)(2,1)}) custom-call(bf16[16,3072]{1,0:T(8,128)(2,1)} %q_ref.1, bf16[16,3072]{1,0:T(8,128)(2,1)} %k_ref.1, bf16[16,3072]{1,0:T(8,128)(2,1)} %v_ref.1), custom_call_target="tpu_custom_call" | custom-call | tf_op jit(solution)/shard_map/pallas_call | solution.py:134
  45.5 1.5 %fusion.1 = (bf16[1,3,8,128,128]{4,3,2,1,0:T(8,128)(2,1)S(1)}, bf16[1,3,8,128,128]{4,3,2,1,0:T(8,128)(2,1)S(1)}) fusion(bf16[2,3,8,128,128]{4,3,2,1,0:T(8,128)(2,1)} %get-tuple-element.8), kind=kLoop, calls=%fused_computation.8 | loop fusion | bytes 3145728 | tf_op jit(solution)/shard_map/slice | solution.py:288
  47.0 2.9 %multiply_reduce_fusion = (f32[3,1024]{1,0:T(4,128)S(1)}, f32[3,1024,1024]{1,2,0:T(8,128)S(1)}) fusion(bf16[3,1024,128]{2,1,0:T(8,128)(2,1)} %bitcast.18, bf16[3,1024,128]{2,1,0:T(8,128)(2,1)S(1)} %bitcast.15), kind=kOutput, calls=%fused_computation.2 | convolution fusion | flops 811594752 | bytes 14168064 | tf_op jit(solution)/shard_map/hid,hjd->hij/dot_general | solution.py:18
  49.9 4.0 %convolution_convert_fusion = bf16[3,1024,128]{2,1,0:T(8,128)(2,1)} fusion(bf16[3,1024,128]{2,1,0:T(8,128)(2,1)S(1)} %bitcast.17, f32[3,1024,1024]{1,2,0:T(8,128)S(1)} %get-tuple-element.12, f32[3,1024]{1,0:T(4,128)S(1)} %get-tuple-element.11), kind=kOutput, calls=%fused_computation.3 | convolution fusion | flops 815136768 | bytes 14168064 | tf_op jit(solution)/shard_map/hij,hjd->hid/dot_general | solution.py:24
  53.9 2.1 %convert_reduce_fusion = f32[3,1024]{1,0:T(4,128)S(1)} fusion(f32[3,1024]{1,0:T(4,128)S(1)} %get-tuple-element.11, f32[3,1024,1024]{1,2,0:T(8,128)S(1)} %get-tuple-element.12), kind=kLoop, calls=%fused_computation | loop fusion | flops 15725568 | bytes 12607488 | tf_op jit(solution)/shard_map/reduce_sum | solution.py:23
  56.0 0.6 pad_maximum_fusion.stats_ref
  56.6 37.6 %shard_map.47 = bf16[16,5120]{1,0:T(8,128)(2,1)} custom-call(bf16[3,8,128,128]{3,2,1,0:T(8,128)(2,1)} %bitcast.16, f32[2,3,8,128]{3,2,1,0:T(8,128)} %pad_maximum_fusion.stats_ref, bf16[384,5120]{1,0:T(8,128)(2,1)} %w_ref.1), custom_call_target="tpu_custom_call" | custom-call | tf_op jit(solution)/shard_map/pallas_call | solution.py:249
  94.2 1.6 %copy.12 = bf16[16,5120]{1,0:T(8,128)(2,1)} copy(bf16[16,5120]{1,0:T(8,128)(2,1)} %shard_map.47) | data formatting | bytes 327680
  (1 shorter events, 0.0 us)

commit v10 on v9

--- a/solution.py
+++ b/solution.py
@@ -150,8 +150,8 @@
     )(query_vectors, key_vectors, value_vectors)
 
 
-def project_kernel(na, n_hi, parts_ref, stats_ref, w_ref, out_ref, got_parts, got_stats, full,
-                   send1, recv1, total, send2, recv2, part_sems, stat_sems, sems1, send_sems2,
+def project_kernel(na, n_hi, parts_ref, stats_ref, w_ref, out_ref, got_parts, got_stats, att_buf,
+                   pick, send1, recv1, total, send2, recv2, part_sems, stat_sems, sems1, send_sems2,
                    recv_sems2, own_stat_sem):
     mesh_ids = pl.DeviceIdType.MESH
     a = lax.axis_index("ca")
@@ -204,25 +204,25 @@
             numerator = numerator + (
                 got_parts[off - 1, h].astype(jnp.float32) * factors[off][h][:, None]
             )
-        attended = (numerator / totals[h][:, None]).astype(jnp.bfloat16)
-        product = jnp.dot(attended, w_ref[pl.ds(h * HD, HD), :], preferred_element_type=jnp.float32)
-        if h == 0:
-            full[...] = product
-        else:
-            full[...] = full[...] + product
+        att_buf[:, pl.ds(h * HD, HD)] = (numerator / totals[h][:, None]).astype(jnp.bfloat16)
 
     for j in range(n_hi):
         their = pl.multiple_of((j * 2 + 1 - core) * rows, rows)
         mine = pl.multiple_of((j * 2 + core) * rows, rows)
-        send1[j] = full[pl.ds(their, rows), :].astype(jnp.bfloat16)
-        total[j] = full[pl.ds(mine, rows), :].astype(jnp.bfloat16).astype(jnp.float32)
+        pick[0, pl.ds(j * rows, rows), :] = att_buf[pl.ds(their, rows), :]
+        pick[1, pl.ds(j * rows, rows), :] = att_buf[pl.ds(mine, rows), :]
+    send1[...] = jnp.dot(pick[0], w_ref[...], preferred_element_type=jnp.float32).astype(
+        jnp.bfloat16)
     first = pltpu.make_async_remote_copy(
         src_ref=send1, dst_ref=recv1, send_sem=sems1.at[0], recv_sem=sems1.at[1],
         device_id=partner, device_id_type=mesh_ids)
     first.start()
+    total[...] = jnp.dot(pick[1], w_ref[...], preferred_element_type=jnp.float32).astype(
+        jnp.bfloat16).astype(jnp.float32)
     first.wait()
     for j in range(n_hi):
-        send2[j] = (total[j] + recv1[j].astype(jnp.float32)).astype(jnp.bfloat16)
+        block = pl.ds(j * rows, rows)
+        send2[j] = (total[block, :] + recv1[block, :].astype(jnp.float32)).astype(jnp.bfloat16)
     second = []
     for off in range(1, n_hi):
         dest = lax.rem(hi + off, n_hi)
@@ -232,7 +232,8 @@
             device_id_type=mesh_ids)
         copy.start()
         second.append(copy)
-    own = total[hi] + recv1[hi].astype(jnp.float32)
+    own_rows = pl.ds(pl.multiple_of(hi * rows, rows), rows)
+    own = total[own_rows, :] + recv1[own_rows, :].astype(jnp.float32)
     for copy in second:
         copy.wait()
     for off in range(1, n_hi):
@@ -254,10 +255,11 @@
         scratch_shapes=[
             pltpu.VMEM((na - 1, heads, block_rows, HD), parts.dtype),
             pltpu.VMEM((na, 2, heads, block_rows), stats.dtype),
-            pltpu.VMEM((block_rows, cols), jnp.float32),
-            pltpu.VMEM((n_hi, rows, cols), jnp.bfloat16),
-            pltpu.VMEM((n_hi, rows, cols), jnp.bfloat16),
-            pltpu.VMEM((n_hi, rows, cols), jnp.float32),
+            pltpu.VMEM((block_rows, heads * HD), jnp.bfloat16),
+            pltpu.VMEM((2, n_hi * rows, heads * HD), jnp.bfloat16),
+            pltpu.VMEM((n_hi * rows, cols), jnp.bfloat16),
+            pltpu.VMEM((n_hi * rows, cols), jnp.bfloat16),
+            pltpu.VMEM((n_hi * rows, cols), jnp.float32),
             pltpu.VMEM((n_hi, rows, cols), jnp.bfloat16),
             pltpu.VMEM((n_hi - 1, rows, cols), jnp.bfloat16),
             pltpu.SemaphoreType.DMA((2, na - 1)),

time: 96.4 us -> 95.9 us (level)
  no operation moved by 1% of the time
where the time goes in v10:
time: 95.9 us; the launch traced here: 95.1 us
  Pallas kernels  82.4 us (86%)
  matrix products  6.92 us (7%)
  local copies, waits for them, and re-layouts  3.1 us (3%)
  other arithmetic  2.67 us (3%)
    pallas_call x1, Pallas kernels, exchange(): pl.pallas_call(functools.partial(exchange_kernel, na, nz, nt), out_shape=...  45.5 us
    pallas_call x1, Pallas kernels, project(): pl.pallas_call(functools.partial(project_kernel, na, n_hi), out_shape=jax...  36.9 us
    dot_general x1, matrix products, attend_local(): jnp.einsum('hij,hjd->hid', weights_low, value_heads, preferred_element_ty...  3.98 us
    dot_general x1, matrix products, attend_local(): jnp.einsum('hid,hjd->hij', query_heads, key_heads, preferred_element_type...  2.94 us
    reduce_sum x1, other arithmetic, attend_local(): row_total = jnp.sum(weights_low.astype(jnp.float32), axis=-1)  2.06 us

profile of v10, /device:TPU:1, one launch (start us, length us, event | category | flops | bytes accessed | tf_op | source)
XLA Modules:
  0.0 95.1 jit_solution(13967267962381613403)
XLA Ops:
  0.0 45.5 %shard_map.46 = (bf16[3,8,128,128]{3,2,1,0:T(8,128)(2,1)}, bf16[2,3,8,128,128]{4,3,2,1,0:T(8,128)(2,1)}) custom-call(bf16[16,3072]{1,0:T(8,128)(2,1)} %q_ref.1, bf16[16,3072]{1,0:T(8,128)(2,1)} %k_ref.1, bf16[16,3072]{1,0:T(8,128)(2,1)} %v_ref.1), custom_call_target="tpu_custom_call" | custom-call | tf_op jit(solution)/shard_map/pallas_call | solution.py:134
  45.5 1.5 %fusion.1 = (bf16[1,3,8,128,128]{4,3,2,1,0:T(8,128)(2,1)S(1)}, bf16[1,3,8,128,128]{4,3,2,1,0:T(8,128)(2,1)S(1)}) fusion(bf16[2,3,8,128,128]{4,3,2,1,0:T(8,128)(2,1)} %get-tuple-element.8), kind=kLoop, calls=%fused_computation.8 | loop fusion | bytes 3145728 | tf_op jit(solution)/shard_map/slice | solution.py:290
  47.0 2.9 %multiply_reduce_fusion = (f32[3,1024]{1,0:T(4,128)S(1)}, f32[3,1024,1024]{1,2,0:T(8,128)S(1)}) fusion(bf16[3,1024,128]{2,1,0:T(8,128)(2,1)} %bitcast.18, bf16[3,1024,128]{2,1,0:T(8,128)(2,1)S(1)} %bitcast.15), kind=kOutput, calls=%fused_computation.2 | convolution fusion | flops 811594752 | bytes 14168064 | tf_op jit(solution)/shard_map/hid,hjd->hij/dot_general | solution.py:18
  49.9 4.0 %convolution_convert_fusion = bf16[3,1024,128]{2,1,0:T(8,128)(2,1)} fusion(bf16[3,1024,128]{2,1,0:T(8,128)(2,1)S(1)} %bitcast.17, f32[3,1024,1024]{1,2,0:T(8,128)S(1)} %get-tuple-element.12, f32[3,1024]{1,0:T(4,128)S(1)} %get-tuple-element.11), kind=kOutput, calls=%fused_computation.3 | convolution fusion | flops 815136768 | bytes 14168064 | tf_op jit(solution)/shard_map/hij,hjd->hid/dot_general | solution.py:24
  53.9 2.1 %convert_reduce_fusion = f32[3,1024]{1,0:T(4,128)S(1)} fusion(f32[3,1024]{1,0:T(4,128)S(1)} %get-tuple-element.11, f32[3,1024,1024]{1,2,0:T(8,128)S(1)} %get-tuple-element.12), kind=kLoop, calls=%fused_computation | loop fusion | flops 15725568 | bytes 12607488 | tf_op jit(solution)/shard_map/reduce_sum | solution.py:23
  56.0 0.6 pad_maximum_fusion.stats_ref
  56.6 36.9 %shard_map.47 = bf16[16,5120]{1,0:T(8,128)(2,1)} custom-call(bf16[3,8,128,128]{3,2,1,0:T(8,128)(2,1)} %bitcast.16, f32[2,3,8,128]{3,2,1,0:T(8,128)} %pad_maximum_fusion.stats_ref, bf16[384,5120]{1,0:T(8,128)(2,1)} %w_ref.1), custom_call_target="tpu_custom_call" | custom-call | tf_op jit(solution)/shard_map/pallas_call | solution.py:250
  93.5 1.6 %copy.12 = bf16[16,5120]{1,0:T(8,128)(2,1)} copy(bf16[16,5120]{1,0:T(8,128)(2,1)} %shard_map.47) | data formatting | bytes 327680
  (1 shorter events, 0.0 us)

commit v11 on v10

--- a/solution.py
+++ b/solution.py
@@ -151,8 +151,8 @@
 
 
 def project_kernel(na, n_hi, parts_ref, stats_ref, w_ref, out_ref, got_parts, got_stats, att_buf,
-                   pick, send1, recv1, total, send2, recv2, part_sems, stat_sems, sems1, send_sems2,
-                   recv_sems2, own_stat_sem):
+                   pick, send1, recv1, total, send2, recv2, relay_in, far_in, part_sems, stat_sems,
+                   sems1, direct_sems, relay_sems, onward_sems, own_stat_sem):
     mesh_ids = pl.DeviceIdType.MESH
     a = lax.axis_index("ca")
     z = lax.axis_index("cz")
@@ -223,21 +223,41 @@
     for j in range(n_hi):
         block = pl.ds(j * rows, rows)
         send2[j] = (total[block, :] + recv1[block, :].astype(jnp.float32)).astype(jnp.bfloat16)
-    second = []
-    for off in range(1, n_hi):
-        dest = lax.rem(hi + off, n_hi)
+    half = send2.shape[2] // 2
+    up = lax.rem(hi + 1, n_hi)
+    down = lax.rem(hi + n_hi - 1, n_hi)
+    far = lax.rem(hi + 2, n_hi)
+
+    def to(dest):
+        return (a, z, dest * 2 + core)
+
+    def remote(src_ref, dst_ref, sems, slot, dest):
         copy = pltpu.make_async_remote_copy(
-            src_ref=send2.at[dest], dst_ref=recv2.at[off - 1], send_sem=send_sems2.at[off - 1],
-            recv_sem=recv_sems2.at[off - 1], device_id=(a, z, dest * 2 + core),
-            device_id_type=mesh_ids)
+            src_ref=src_ref, dst_ref=dst_ref, send_sem=sems.at[0, slot],
+            recv_sem=sems.at[1, slot], device_id=to(dest), device_id_type=mesh_ids)
         copy.start()
-        second.append(copy)
+        return copy
+
+    direct = [
+        remote(send2.at[up], recv2.at[0], direct_sems, 0, up),
+        remote(send2.at[down], recv2.at[1], direct_sems, 1, down),
+    ]
+    relay = [
+        remote(send2.at[far, :, pl.ds(0, half)], relay_in.at[0], relay_sems, 0, up),
+        remote(send2.at[far, :, pl.ds(half, half)], relay_in.at[1], relay_sems, 1, down),
+    ]
+    relay[0].wait_recv()
+    onward = [remote(relay_in.at[0], far_in.at[0], onward_sems, 0, up)]
+    relay[1].wait_recv()
+    onward.append(remote(relay_in.at[1], far_in.at[1], onward_sems, 1, down))
     own_rows = pl.ds(pl.multiple_of(hi * rows, rows), rows)
     own = total[own_rows, :] + recv1[own_rows, :].astype(jnp.float32)
-    for copy in second:
-        copy.wait()
-    for off in range(1, n_hi):
-        own = own + recv2[off - 1].astype(jnp.float32)
+    for copy in direct + onward:
+        copy.wait()
+    for copy in relay:
+        copy.wait_send()
+    own = own + recv2[0].astype(jnp.float32) + recv2[1].astype(jnp.float32)
+    own = own + jnp.concatenate([far_in[0], far_in[1]], axis=1).astype(jnp.float32)
     out_ref[...] = own.astype(out_ref.dtype)
 
 
@@ -261,12 +281,15 @@
             pltpu.VMEM((n_hi * rows, cols), jnp.bfloat16),
             pltpu.VMEM((n_hi * rows, cols), jnp.float32),
             pltpu.VMEM((n_hi, rows, cols), jnp.bfloat16),
-            pltpu.VMEM((n_hi - 1, rows, cols), jnp.bfloat16),
+            pltpu.VMEM((2, rows, cols), jnp.bfloat16),
+            pltpu.VMEM((2, rows, cols // 2), jnp.bfloat16),
+            pltpu.VMEM((2, rows, cols // 2), jnp.bfloat16),
             pltpu.SemaphoreType.DMA((2, na - 1)),
             pltpu.SemaphoreType.DMA((2, na - 1)),
             pltpu.SemaphoreType.DMA((2,)),
-            pltpu.SemaphoreType.DMA((n_hi - 1,)),
-            pltpu.SemaphoreType.DMA((n_hi - 1,)),
+            pltpu.SemaphoreType.DMA((2, 2)),
+            pltpu.SemaphoreType.DMA((2, 2)),
+            pltpu.SemaphoreType.DMA((2, 2)),
             pltpu.SemaphoreType.DMA(()),
         ],
         compiler_params=pltpu.CompilerParams(collective_id=1, has_side_effects=True),

time: 95.9 us -> 98.1 us (1.023)
  the two profiles are of different devices: /device:TPU:1 before, /device:TPU:9 now
where the time goes in v11:
time: 98.1 us; the launch traced here: 97.9 us
  Pallas kernels  85.2 us (87%)
  matrix products  6.93 us (7%)
  local copies, waits for them, and re-layouts  3.1 us (3%)
  other arithmetic  2.67 us (3%)
    pallas_call x1, Pallas kernels, project(): pl.pallas_call(functools.partial(project_kernel, na, n_hi), out_shape=jax...  43.1 us
    pallas_call x1, Pallas kernels, exchange(): pl.pallas_call(functools.partial(exchange_kernel, na, nz, nt), out_shape=...  42.1 us
    dot_general x1, matrix products, attend_local(): jnp.einsum('hij,hjd->hid', weights_low, value_heads, preferred_element_ty...  3.98 us
    dot_general x1, matrix products, attend_local(): jnp.einsum('hid,hjd->hij', query_heads, key_heads, preferred_element_type...  2.94 us
    reduce_sum x1, other arithmetic, attend_local(): row_total = jnp.sum(weights_low.astype(jnp.float32), axis=-1)  2.06 us

profile of v11, /device:TPU:9, one launch (start us, length us, event | category | flops | bytes accessed | tf_op | source)
XLA Modules:
  0.0 97.9 jit_solution(1479386538245146864)
XLA Ops:
  0.0 42.1 %shard_map.46 = (bf16[3,8,128,128]{3,2,1,0:T(8,128)(2,1)}, bf16[2,3,8,128,128]{4,3,2,1,0:T(8,128)(2,1)}) custom-call(bf16[16,3072]{1,0:T(8,128)(2,1)} %q_ref.1, bf16[16,3072]{1,0:T(8,128)(2,1)} %k_ref.1, bf16[16,3072]{1,0:T(8,128)(2,1)} %v_ref.1), custom_call_target="tpu_custom_call" | custom-call | tf_op jit(solution)/shard_map/pallas_call | solution.py:134
  42.1 1.5 %fusion.1 = (bf16[1,3,8,128,128]{4,3,2,1,0:T(8,128)(2,1)S(1)}, bf16[1,3,8,128,128]{4,3,2,1,0:T(8,128)(2,1)S(1)}) fusion(bf16[2,3,8,128,128]{4,3,2,1,0:T(8,128)(2,1)} %get-tuple-element.8), kind=kLoop, calls=%fused_computation.8 | loop fusion | bytes 3145728 | tf_op jit(solution)/shard_map/slice | solution.py:313
  43.6 2.9 %multiply_reduce_fusion = (f32[3,1024]{1,0:T(4,128)S(1)}, f32[3,1024,1024]{1,2,0:T(8,128)S(1)}) fusion(bf16[3,1024,128]{2,1,0:T(8,128)(2,1)} %bitcast.18, bf16[3,1024,128]{2,1,0:T(8,128)(2,1)S(1)} %bitcast.15), kind=kOutput, calls=%fused_computation.2 | convolution fusion | flops 811594752 | bytes 14168064 | tf_op jit(solution)/shard_map/hid,hjd->hij/dot_general | solution.py:18
  46.6 4.0 %convolution_convert_fusion = bf16[3,1024,128]{2,1,0:T(8,128)(2,1)} fusion(bf16[3,1024,128]{2,1,0:T(8,128)(2,1)S(1)} %bitcast.17, f32[3,1024,1024]{1,2,0:T(8,128)S(1)} %get-tuple-element.12, f32[3,1024]{1,0:T(4,128)S(1)} %get-tuple-element.11), kind=kOutput, calls=%fused_computation.3 | convolution fusion | flops 815136768 | bytes 14168064 | tf_op jit(solution)/shard_map/hij,hjd->hid/dot_general | solution.py:24
  50.6 2.1 %convert_reduce_fusion = f32[3,1024]{1,0:T(4,128)S(1)} fusion(f32[3,1024]{1,0:T(4,128)S(1)} %get-tuple-element.11, f32[3,1024,1024]{1,2,0:T(8,128)S(1)} %get-tuple-element.12), kind=kLoop, calls=%fused_computation | loop fusion | flops 15725568 | bytes 12607488 | tf_op jit(solution)/shard_map/reduce_sum | solution.py:23
  52.6 0.6 pad_maximum_fusion.stats_ref
  53.2 43.1 %shard_map.47 = bf16[16,5120]{1,0:T(8,128)(2,1)} custom-call(bf16[3,8,128,128]{3,2,1,0:T(8,128)(2,1)} %bitcast.16, f32[2,3,8,128]{3,2,1,0:T(8,128)} %pad_maximum_fusion.stats_ref, bf16[384,5120]{1,0:T(8,128)(2,1)} %w_ref.1), custom_call_target="tpu_custom_call" | custom-call | tf_op jit(solution)/shard_map/pallas_call | solution.py:270
  96.3 1.6 %copy.12 = bf16[16,5120]{1,0:T(8,128)(2,1)} copy(bf16[16,5120]{1,0:T(8,128)(2,1)} %shard_map.47) | data formatting | bytes 327680
  (1 shorter events, 0.0 us)

commit v12 on v10

--- a/solution.py
+++ b/solution.py
@@ -102,23 +102,27 @@
     n_right = nz // 2
     n_left = (nz - 1) // 2
     chains = ((right, n_right, r_sems, -1, []), (left, n_left, l_sems, 1, []))
+    pieces = 2 * heads
     for step in range(n_right):
         for part in range(2):
-            for side, count, sems, sign, copies in chains:
-                if step >= count:
-                    continue
-                slot = lax.rem(z + sign * step + nz, nz)
-                if step > 0:
-                    copies[(step - 1) * 2 + part].wait_recv()
-                copy = pltpu.make_async_remote_copy(
-                    src_ref=kv_out.at[part, :, slot], dst_ref=kv_out.at[part, :, slot],
-                    send_sem=sems.at[0, step * 2 + part], recv_sem=sems.at[1, step * 2 + part],
-                    device_id=(a, side, t), device_id_type=mesh_ids)
-                copy.start()
-                copies.append(copy)
+            for h in range(heads):
+                piece = part * heads + h
+                for side, count, sems, sign, copies in chains:
+                    if step >= count:
+                        continue
+                    slot = lax.rem(z + sign * step + nz, nz)
+                    if step > 0:
+                        copies[(step - 1) * pieces + piece].wait_recv()
+                    copy = pltpu.make_async_remote_copy(
+                        src_ref=kv_out.at[part, h, slot], dst_ref=kv_out.at[part, h, slot],
+                        send_sem=sems.at[0, step * pieces + piece],
+                        recv_sem=sems.at[1, step * pieces + piece],
+                        device_id=(a, side, t), device_id_type=mesh_ids)
+                    copy.start()
+                    copies.append(copy)
     for side, count, sems, sign, copies in chains:
-        copies[-2].wait_recv()
-        copies[-1].wait_recv()
+        for copy in copies[-pieces:]:
+            copy.wait_recv()
         for copy in copies:
             copy.wait_send()
     for copy in q_copies:
@@ -143,8 +147,8 @@
             pltpu.SemaphoreType.DMA((2, 3, heads, nt - 1)),
             pltpu.SemaphoreType.DMA((3, heads)),
             pltpu.SemaphoreType.DMA((2, na - 1)),
-            pltpu.SemaphoreType.DMA((2, 2 * n_right)),
-            pltpu.SemaphoreType.DMA((2, 2 * n_left)),
+            pltpu.SemaphoreType.DMA((2, 2 * heads * n_right)),
+            pltpu.SemaphoreType.DMA((2, 2 * heads * n_left)),
         ],
         compiler_params=pltpu.CompilerParams(collective_id=0, has_side_effects=True),
     )(query_vectors, key_vectors, value_vectors)

time: 95.9 us -> 97.3 us (1.015)
  Pallas kernels: 82.4 us -> 84.4 us
    pallas_call x1, Pallas kernels: 45.5 us -> 46.9 us  [exchange(): pl.pallas_call(functools.partial(exchange_kernel, na, nz, nt), out_shape=...]
where the time goes in v12:
time: 97.3 us; the launch traced here: 97.1 us
  Pallas kernels  84.4 us (87%)
  matrix products  6.93 us (7%)
  local copies, waits for them, and re-layouts  3.1 us (3%)
  other arithmetic  2.67 us (3%)
    pallas_call x1, Pallas kernels, exchange(): pl.pallas_call(functools.partial(exchange_kernel, na, nz, nt), out_shape=...  46.9 us
    pallas_call x1, Pallas kernels, project(): pl.pallas_call(functools.partial(project_kernel, na, n_hi), out_shape=jax...  37.4 us
    dot_general x1, matrix products, attend_local(): jnp.einsum('hij,hjd->hid', weights_low, value_heads, preferred_element_ty...  3.98 us
    dot_general x1, matrix products, attend_local(): jnp.einsum('hid,hjd->hij', query_heads, key_heads, preferred_element_type...  2.94 us
    reduce_sum x1, other arithmetic, attend_local(): row_total = jnp.sum(weights_low.astype(jnp.float32), axis=-1)  2.06 us

profile of v12, /device:TPU:1, one launch (start us, length us, event | category | flops | bytes accessed | tf_op | source)
XLA Modules:
  0.0 97.1 jit_solution(2869486391709696206)
XLA Ops:
  0.0 46.9 %shard_map.46 = (bf16[3,8,128,128]{3,2,1,0:T(8,128)(2,1)}, bf16[2,3,8,128,128]{4,3,2,1,0:T(8,128)(2,1)}) custom-call(bf16[16,3072]{1,0:T(8,128)(2,1)} %q_ref.1, bf16[16,3072]{1,0:T(8,128)(2,1)} %k_ref.1, bf16[16,3072]{1,0:T(8,128)(2,1)} %v_ref.1), custom_call_target="tpu_custom_call" | custom-call | tf_op jit(solution)/shard_map/pallas_call | solution.py:138
  47.0 1.5 %fusion.1 = (bf16[1,3,8,128,128]{4,3,2,1,0:T(8,128)(2,1)S(1)}, bf16[1,3,8,128,128]{4,3,2,1,0:T(8,128)(2,1)S(1)}) fusion(bf16[2,3,8,128,128]{4,3,2,1,0:T(8,128)(2,1)} %get-tuple-element.8), kind=kLoop, calls=%fused_computation.8 | loop fusion | bytes 3145728 | tf_op jit(solution)/shard_map/slice | solution.py:294
  48.5 2.9 %multiply_reduce_fusion = (f32[3,1024]{1,0:T(4,128)S(1)}, f32[3,1024,1024]{1,2,0:T(8,128)S(1)}) fusion(bf16[3,1024,128]{2,1,0:T(8,128)(2,1)} %bitcast.18, bf16[3,1024,128]{2,1,0:T(8,128)(2,1)S(1)} %bitcast.15), kind=kOutput, calls=%fused_computation.2 | convolution fusion | flops 811594752 | bytes 14168064 | tf_op jit(solution)/shard_map/hid,hjd->hij/dot_general | solution.py:18
  51.4 4.0 %convolution_convert_fusion = bf16[3,1024,128]{2,1,0:T(8,128)(2,1)} fusion(bf16[3,1024,128]{2,1,0:T(8,128)(2,1)S(1)} %bitcast.17, f32[3,1024,1024]{1,2,0:T(8,128)S(1)} %get-tuple-element.12, f32[3,1024]{1,0:T(4,128)S(1)} %get-tuple-element.11), kind=kOutput, calls=%fused_computation.3 | convolution fusion | flops 815136768 | bytes 14168064 | tf_op jit(solution)/shard_map/hij,hjd->hid/dot_general | solution.py:24
  55.4 2.1 %convert_reduce_fusion = f32[3,1024]{1,0:T(4,128)S(1)} fusion(f32[3,1024]{1,0:T(4,128)S(1)} %get-tuple-element.11, f32[3,1024,1024]{1,2,0:T(8,128)S(1)} %get-tuple-element.12), kind=kLoop, calls=%fused_computation | loop fusion | flops 15725568 | bytes 12607488 | tf_op jit(solution)/shard_map/reduce_sum | solution.py:23
  57.5 0.6 pad_maximum_fusion.stats_ref
  58.1 37.4 %shard_map.47 = bf16[16,5120]{1,0:T(8,128)(2,1)} custom-call(bf16[3,8,128,128]{3,2,1,0:T(8,128)(2,1)} %bitcast.16, f32[2,3,8,128]{3,2,1,0:T(8,128)} %pad_maximum_fusion.stats_ref, bf16[384,5120]{1,0:T(8,128)(2,1)} %w_ref.1), custom_call_target="tpu_custom_call" | custom-call | tf_op jit(solution)/shard_map/pallas_call | solution.py:254
  95.5 1.6 %copy.12 = bf16[16,5120]{1,0:T(8,128)(2,1)} copy(bf16[16,5120]{1,0:T(8,128)(2,1)} %shard_map.47) | data formatting | bytes 327680
  (1 shorter events, 0.0 us)

commit v13 on v10

--- a/solution.py
+++ b/solution.py
@@ -33,8 +33,8 @@
     return lax.all_to_all(spread, axis_name, 0, 0, tiled=True)
 
 
-def exchange_kernel(na, nz, nt, q_ref, k_ref, v_ref, q_out, kv_out, spread_sems, own_sems,
-                    q_sems, r_sems, l_sems):
+def exchange_kernel(na, nz, nt, q_ref, k_ref, v_ref, q_out, k_out, v_out, spread_sems,
+                    own_sems, q_sems, r_sems, l_sems):
     mesh_ids = pl.DeviceIdType.MESH
     a = lax.axis_index("ca")
     z = lax.axis_index("cz")
@@ -61,7 +61,7 @@
     def target(i, h):
         if i == 0:
             return q_out.at[h, a, mine]
-        return kv_out.at[i - 1, h, z, mine]
+        return (k_out, v_out)[i - 1].at[h, z, mine]
 
     def columns(dest, h):
         return pl.ds(pl.multiple_of((dest * heads + h) * HD, HD), HD)
@@ -111,7 +111,7 @@
                 if step > 0:
                     copies[(step - 1) * 2 + part].wait_recv()
                 copy = pltpu.make_async_remote_copy(
-                    src_ref=kv_out.at[part, :, slot], dst_ref=kv_out.at[part, :, slot],
+                    src_ref=(k_out, v_out)[part].at[:, slot], dst_ref=(k_out, v_out)[part].at[:, slot],
                     send_sem=sems.at[0, step * 2 + part], recv_sem=sems.at[1, step * 2 + part],
                     device_id=(a, side, t), device_id_type=mesh_ids)
                 copy.start()
@@ -135,10 +135,11 @@
         functools.partial(exchange_kernel, na, nz, nt),
         out_shape=(
             jax.ShapeDtypeStruct((heads, na, nt * rows, HD), dtype),
-            jax.ShapeDtypeStruct((2, heads, nz, nt * rows, HD), dtype),
+            jax.ShapeDtypeStruct((heads, nz, nt * rows, HD), dtype),
+            jax.ShapeDtypeStruct((heads, nz, nt * rows, HD), dtype),
         ),
         in_specs=[pl.BlockSpec(memory_space=pl.ANY)] * 3,
-        out_specs=(pl.BlockSpec(memory_space=pl.ANY), pl.BlockSpec(memory_space=pl.ANY)),
+        out_specs=tuple(pl.BlockSpec(memory_space=pl.ANY) for _ in range(3)),
         scratch_shapes=[
             pltpu.SemaphoreType.DMA((2, 3, heads, nt - 1)),
             pltpu.SemaphoreType.DMA((3, heads)),
@@ -282,12 +283,11 @@
     own_cols = own_heads * HD
 
     block_rows = token_rows * tp_count
-    query_heads, kv = exchange(
+    query_heads, key_heads, value_heads = exchange(
         query_vectors, key_vectors, value_vectors, ca_count, lax.axis_size("cz"), tp_count)
-    query_heads = query_heads.reshape(own_heads, -1, HD)
-    kv = kv.reshape(2, own_heads, -1, HD)
-
-    row_peak, row_total, weighted = attend_local(query_heads, kv[0], kv[1], score_scale)
+    row_peak, row_total, weighted = attend_local(
+        query_heads.reshape(own_heads, -1, HD), key_heads.reshape(own_heads, -1, HD),
+        value_heads.reshape(own_heads, -1, HD), score_scale)
     stats = jnp.stack([row_peak, row_total], axis=0).reshape(2, own_heads, ca_count, block_rows)
     parts = weighted.astype(jnp.bfloat16).reshape(own_heads, ca_count, block_rows, HD)
     return project(parts, stats, out_weight, tp_count)

time: 95.9 us -> 94.6 us (0.986)
  local copies, waits for them, and re-layouts: 3.1 us -> 1.6 us
    slice x1 -> x0, local copies, waits for them, and re-layouts: 1.5 us -> none  [local(): kv[0]]
where the time goes in v13:
time: 94.6 us; the launch traced here: 94 us
  Pallas kernels  82.5 us (87%)
  matrix products  7.24 us (8%)
  other arithmetic  2.67 us (3%)
  local copies, waits for them, and re-layouts  1.6 us (2%)
    pallas_call x1, Pallas kernels, exchange(): pl.pallas_call(functools.partial(exchange_kernel, na, nz, nt), out_shape=...  45.5 us
    pallas_call x1, Pallas kernels, project(): pl.pallas_call(functools.partial(project_kernel, na, n_hi), out_shape=jax...  37 us
    dot_general x1, matrix products, attend_local(): jnp.einsum('hij,hjd->hid', weights_low, value_heads, preferred_element_ty...  3.99 us
    dot_general x1, matrix products, attend_local(): jnp.einsum('hid,hjd->hij', query_heads, key_heads, preferred_element_type...  3.25 us
    reduce_sum x1, other arithmetic, attend_local(): row_total = jnp.sum(weights_low.astype(jnp.float32), axis=-1)  2.06 us

profile of v13, /device:TPU:1, one launch (start us, length us, event | category | flops | bytes accessed | tf_op | source)
XLA Modules:
  0.0 94.0 jit_solution(17603525044905914170)
XLA Ops:
  0.0 45.5 %shard_map.46 = (bf16[3,8,128,128]{3,2,1,0:T(8,128)(2,1)}, bf16[3,8,128,128]{3,2,1,0:T(8,128)(2,1)}, bf16[3,8,128,128]{3,2,1,0:T(8,128)(2,1)}) custom-call(bf16[16,3072]{1,0:T(8,128)(2,1)} %q_ref.1, bf16[16,3072]{1,0:T(8,128)(2,1)} %k_ref.1, bf16[16,3072]{1,0:T(8,128)(2,1)} %v_ref.1), custom_call_target="tpu_custom_call" | custom-call | tf_op jit(solution)/shard_map/pallas_call | solution.py:134
  45.5 0.0 copy-start
  45.5 3.3 %multiply_reduce_fusion = (f32[3,1024]{1,0:T(4,128)S(1)}, f32[3,1024,1024]{1,2,0:T(8,128)S(1)}) fusion(bf16[3,1024,128]{2,1,0:T(8,128)(2,1)} %bitcast.16, bf16[3,1024,128]{2,1,0:T(8,128)(2,1)} %bitcast.17), kind=kOutput, calls=%fused_computation.2 | convolution fusion | flops 811594752 | bytes 14168064 | tf_op jit(solution)/shard_map/hid,hjd->hij/dot_general | solution.py:18
  48.7 0.0 copy-done
  48.7 4.0 %convolution_convert_fusion = bf16[3,1024,128]{2,1,0:T(8,128)(2,1)} fusion(bf16[3,1024,128]{2,1,0:T(8,128)(2,1)S(1)} %bitcast.18, f32[3,1024,1024]{1,2,0:T(8,128)S(1)} %get-tuple-element.12, f32[3,1024]{1,0:T(4,128)S(1)} %get-tuple-element.11), kind=kOutput, calls=%fused_computation.3 | convolution fusion | flops 815136768 | bytes 14168064 | tf_op jit(solution)/shard_map/hij,hjd->hid/dot_general | solution.py:24
  52.7 2.1 %convert_reduce_fusion = f32[3,1024]{1,0:T(4,128)S(1)} fusion(f32[3,1024]{1,0:T(4,128)S(1)} %get-tuple-element.11, f32[3,1024,1024]{1,2,0:T(8,128)S(1)} %get-tuple-element.12), kind=kLoop, calls=%fused_computation | loop fusion | flops 15725568 | bytes 12607488 | tf_op jit(solution)/shard_map/reduce_sum | solution.py:23
  54.8 0.6 pad_maximum_fusion.stats_ref
  55.4 37.0 %shard_map.47 = bf16[16,5120]{1,0:T(8,128)(2,1)} custom-call(bf16[3,8,128,128]{3,2,1,0:T(8,128)(2,1)} %bitcast.15, f32[2,3,8,128]{3,2,1,0:T(8,128)} %pad_maximum_fusion.stats_ref, bf16[384,5120]{1,0:T(8,128)(2,1)} %w_ref.1), custom_call_target="tpu_custom_call" | custom-call | tf_op jit(solution)/shard_map/pallas_call | solution.py:251
  92.4 1.6 %copy.12 = bf16[16,5120]{1,0:T(8,128)(2,1)} copy(bf16[16,5120]{1,0:T(8,128)(2,1)} %shard_map.47) | data formatting | bytes 327680
  (1 shorter events, 0.0 us)
Async XLA Ops:
  45.5 3.3 %copy-start = (bf16[3,8,128,128]{3,2,1,0:T(8,128)(2,1)S(1)}, bf16[3,8,128,128]{3,2,1,0:T(8,128)(2,1)}, u32[]{:S(2)}) copy-start(bf16[3,8,128,128]{3,2,1,0:T(8,128)(2,1)} %get-tuple-element.10) | copy-start | bytes 2359300

commit v14 on v13

--- a/solution.py
+++ b/solution.py
@@ -99,28 +99,36 @@
         copy.start()
         q_copies.append(copy)
 
-    n_right = nz // 2
-    n_left = (nz - 1) // 2
-    chains = ((right, n_right, r_sems, -1, []), (left, n_left, l_sems, 1, []))
-    for step in range(n_right):
+    n_steps = nz // 2
+    chains = ((right, r_sems, -1, {}), (left, l_sems, 1, {}))
+
+    def parts_of(chain, step):
+        if nz % 2 == 0 and step == n_steps - 1:
+            return (chain,)
+        return (0, 1)
+
+    sent = []
+    for step in range(n_steps):
         for part in range(2):
-            for side, count, sems, sign, copies in chains:
-                if step >= count:
+            for chain, (side, sems, sign, copies) in enumerate(chains):
+                if part not in parts_of(chain, step):
                     continue
                 slot = lax.rem(z + sign * step + nz, nz)
                 if step > 0:
-                    copies[(step - 1) * 2 + part].wait_recv()
+                    copies.pop((step - 1, part)).wait_recv()
+                buf = (k_out, v_out)[part]
                 copy = pltpu.make_async_remote_copy(
-                    src_ref=(k_out, v_out)[part].at[:, slot], dst_ref=(k_out, v_out)[part].at[:, slot],
+                    src_ref=buf.at[:, slot], dst_ref=buf.at[:, slot],
                     send_sem=sems.at[0, step * 2 + part], recv_sem=sems.at[1, step * 2 + part],
                     device_id=(a, side, t), device_id_type=mesh_ids)
                 copy.start()
-                copies.append(copy)
-    for side, count, sems, sign, copies in chains:
-        copies[-2].wait_recv()
-        copies[-1].wait_recv()
-        for copy in copies:
-            copy.wait_send()
+                copies[(step, part)] = copy
+                sent.append(copy)
+    for side, sems, sign, copies in chains:
+        for copy in copies.values():
+            copy.wait_recv()
+    for copy in sent:
+        copy.wait_send()
     for copy in q_copies:
         copy.wait()
 
@@ -144,8 +152,8 @@
             pltpu.SemaphoreType.DMA((2, 3, heads, nt - 1)),
             pltpu.SemaphoreType.DMA((3, heads)),
             pltpu.SemaphoreType.DMA((2, na - 1)),
-            pltpu.SemaphoreType.DMA((2, 2 * n_right)),
-            pltpu.SemaphoreType.DMA((2, 2 * n_left)),
+            pltpu.SemaphoreType.DMA((2, 2 * (nz // 2))),
+            pltpu.SemaphoreType.DMA((2, 2 * (nz // 2))),
         ],
         compiler_params=pltpu.CompilerParams(collective_id=0, has_side_effects=True),
     )(query_vectors, key_vectors, value_vectors)

time: 94.6 us -> 93.8 us (level)
    pallas_call x1, Pallas kernels: 45.5 us -> 43.4 us  [exchange(): pl.pallas_call(functools.partial(exchange_kernel, na, nz, nt), out_shape=...]
    pallas_call x1, Pallas kernels: 37 us -> 38.7 us  [project(): pl.pallas_call(functools.partial(project_kernel, na, n_hi), out_shape=jax...]
where the time goes in v14:
time: 93.8 us; the launch traced here: 93.6 us
  Pallas kernels  82 us (87%)
  matrix products  7.24 us (8%)
  other arithmetic  2.67 us (3%)
  local copies, waits for them, and re-layouts  1.6 us (2%)
    pallas_call x1, Pallas kernels, exchange(): pl.pallas_call(functools.partial(exchange_kernel, na, nz, nt), out_shape=...  43.4 us
    pallas_call x1, Pallas kernels, project(): pl.pallas_call(functools.partial(project_kernel, na, n_hi), out_shape=jax...  38.7 us
    dot_general x1, matrix products, attend_local(): jnp.einsum('hij,hjd->hid', weights_low, value_heads, preferred_element_ty...  3.99 us
    dot_general x1, matrix products, attend_local(): jnp.einsum('hid,hjd->hij', query_heads, key_heads, preferred_element_type...  3.25 us
    reduce_sum x1, other arithmetic, attend_local(): row_total = jnp.sum(weights_low.astype(jnp.float32), axis=-1)  2.06 us

profile of v14, /device:TPU:1, one launch (start us, length us, event | category | flops | bytes accessed | tf_op | source)
XLA Modules:
  0.0 93.6 jit_solution(17034643230079403468)
XLA Ops:
  0.0 43.4 %shard_map.46 = (bf16[3,8,128,128]{3,2,1,0:T(8,128)(2,1)}, bf16[3,8,128,128]{3,2,1,0:T(8,128)(2,1)}, bf16[3,8,128,128]{3,2,1,0:T(8,128)(2,1)}) custom-call(bf16[16,3072]{1,0:T(8,128)(2,1)} %q_ref.1, bf16[16,3072]{1,0:T(8,128)(2,1)} %k_ref.1, bf16[16,3072]{1,0:T(8,128)(2,1)} %v_ref.1), custom_call_target="tpu_custom_call" | custom-call | tf_op jit(solution)/shard_map/pallas_call | solution.py:142
  43.4 0.0 copy-start
  43.4 3.3 %multiply_reduce_fusion = (f32[3,1024]{1,0:T(4,128)S(1)}, f32[3,1024,1024]{1,2,0:T(8,128)S(1)}) fusion(bf16[3,1024,128]{2,1,0:T(8,128)(2,1)} %bitcast.16, bf16[3,1024,128]{2,1,0:T(8,128)(2,1)} %bitcast.17), kind=kOutput, calls=%fused_computation.2 | convolution fusion | flops 811594752 | bytes 14168064 | tf_op jit(solution)/shard_map/hid,hjd->hij/dot_general | solution.py:18
  46.6 0.0 copy-done
  46.6 4.0 %convolution_convert_fusion = bf16[3,1024,128]{2,1,0:T(8,128)(2,1)} fusion(bf16[3,1024,128]{2,1,0:T(8,128)(2,1)S(1)} %bitcast.18, f32[3,1024,1024]{1,2,0:T(8,128)S(1)} %get-tuple-element.12, f32[3,1024]{1,0:T(4,128)S(1)} %get-tuple-element.11), kind=kOutput, calls=%fused_computation.3 | convolution fusion | flops 815136768 | bytes 14168064 | tf_op jit(solution)/shard_map/hij,hjd->hid/dot_general | solution.py:24
  50.6 2.1 %convert_reduce_fusion = f32[3,1024]{1,0:T(4,128)S(1)} fusion(f32[3,1024]{1,0:T(4,128)S(1)} %get-tuple-element.11, f32[3,1024,1024]{1,2,0:T(8,128)S(1)} %get-tuple-element.12), kind=kLoop, calls=%fused_computation | loop fusion | flops 15725568 | bytes 12607488 | tf_op jit(solution)/shard_map/reduce_sum | solution.py:23
  52.7 0.6 pad_maximum_fusion.stats_ref
  53.3 38.7 %shard_map.47 = bf16[16,5120]{1,0:T(8,128)(2,1)} custom-call(bf16[3,8,128,128]{3,2,1,0:T(8,128)(2,1)} %bitcast.15, f32[2,3,8,128]{3,2,1,0:T(8,128)} %pad_maximum_fusion.stats_ref, bf16[384,5120]{1,0:T(8,128)(2,1)} %w_ref.1), custom_call_target="tpu_custom_call" | custom-call | tf_op jit(solution)/shard_map/pallas_call | solution.py:259
  92.0 1.6 %copy.12 = bf16[16,5120]{1,0:T(8,128)(2,1)} copy(bf16[16,5120]{1,0:T(8,128)(2,1)} %shard_map.47) | data formatting | bytes 327680
  (1 shorter events, 0.0 us)
Async XLA Ops:
  43.4 3.3 %copy-start = (bf16[3,8,128,128]{3,2,1,0:T(8,128)(2,1)S(1)}, bf16[3,8,128,128]{3,2,1,0:T(8,128)(2,1)}, u32[]{:S(2)}) copy-start(bf16[3,8,128,128]{3,2,1,0:T(8,128)(2,1)} %get-tuple-element.10) | copy-start | bytes 2359300

commit v15 on v14

--- a/solution.py
+++ b/solution.py
@@ -258,7 +258,7 @@
     vmem = pl.BlockSpec(memory_space=pltpu.VMEM)
     return pl.pallas_call(
         functools.partial(project_kernel, na, n_hi),
-        out_shape=jax.ShapeDtypeStruct((rows, cols), jnp.bfloat16),
+        out_shape=jax.ShapeDtypeStruct((rows, cols), jnp.float32),
         in_specs=[vmem, vmem, vmem],
         out_specs=vmem,
         scratch_shapes=[
@@ -298,7 +298,7 @@
         value_heads.reshape(own_heads, -1, HD), score_scale)
     stats = jnp.stack([row_peak, row_total], axis=0).reshape(2, own_heads, ca_count, block_rows)
     parts = weighted.astype(jnp.bfloat16).reshape(own_heads, ca_count, block_rows, HD)
-    return project(parts, stats, out_weight, tp_count)
+    return project(parts, stats, out_weight, tp_count).astype(jnp.bfloat16)
 
 
 def solution(mesh):

time: 93.8 us -> 93.9 us (level)
  other arithmetic: 2.67 us -> 4.33 us
  local copies, waits for them, and re-layouts: 1.6 us -> 0.01 us
    convert_element_type x0 -> x1, other arithmetic: none -> 1.66 us  [local(): return project(parts, stats, out_weight, tp_count).astype(jnp.bfloat16)]
    unnamed x3 -> x2, local copies, waits for them, and re-layouts: 1.6 us -> 0.01 us
where the time goes in v15:
time: 93.9 us; the launch traced here: 93.7 us
  Pallas kernels  82.1 us (87%)
  matrix products  7.23 us (8%)
  other arithmetic  4.33 us (5%)
    pallas_call x1, Pallas kernels, exchange(): pl.pallas_call(functools.partial(exchange_kernel, na, nz, nt), out_shape=...  43.4 us
    pallas_call x1, Pallas kernels, project(): pl.pallas_call(functools.partial(project_kernel, na, n_hi), out_shape=jax...  38.7 us
    dot_general x1, matrix products, attend_local(): jnp.einsum('hij,hjd->hid', weights_low, value_heads, preferred_element_ty...  3.98 us
    dot_general x1, matrix products, attend_local(): jnp.einsum('hid,hjd->hij', query_heads, key_heads, preferred_element_type...  3.25 us
    reduce_sum x1, other arithmetic, attend_local(): row_total = jnp.sum(weights_low.astype(jnp.float32), axis=-1)  2.06 us

profile of v15, /device:TPU:1, one launch (start us, length us, event | category | flops | bytes accessed | tf_op | source)
XLA Modules:
  0.0 93.7 jit_solution(658525330120911001)
XLA Ops:
  0.0 43.4 %shard_map.46 = (bf16[3,8,128,128]{3,2,1,0:T(8,128)(2,1)}, bf16[3,8,128,128]{3,2,1,0:T(8,128)(2,1)}, bf16[3,8,128,128]{3,2,1,0:T(8,128)(2,1)}) custom-call(bf16[16,3072]{1,0:T(8,128)(2,1)} %q_ref.1, bf16[16,3072]{1,0:T(8,128)(2,1)} %k_ref.1, bf16[16,3072]{1,0:T(8,128)(2,1)} %v_ref.1), custom_call_target="tpu_custom_call" | custom-call | tf_op jit(solution)/shard_map/pallas_call | solution.py:142
  43.4 0.0 copy-start
  43.4 3.3 %multiply_reduce_fusion = (f32[3,1024]{1,0:T(4,128)S(1)}, f32[3,1024,1024]{1,2,0:T(8,128)S(1)}) fusion(bf16[3,1024,128]{2,1,0:T(8,128)(2,1)} %bitcast.16, bf16[3,1024,128]{2,1,0:T(8,128)(2,1)} %bitcast.17), kind=kOutput, calls=%fused_computation.2 | convolution fusion | flops 811594752 | bytes 14168064 | tf_op jit(solution)/shard_map/hid,hjd->hij/dot_general | solution.py:18
  46.6 0.0 copy-done
  46.6 4.0 %convolution_convert_fusion = bf16[3,1024,128]{2,1,0:T(8,128)(2,1)} fusion(bf16[3,1024,128]{2,1,0:T(8,128)(2,1)S(1)} %bitcast.18, f32[3,1024,1024]{1,2,0:T(8,128)S(1)} %get-tuple-element.12, f32[3,1024]{1,0:T(4,128)S(1)} %get-tuple-element.11), kind=kOutput, calls=%fused_computation.3 | convolution fusion | flops 815136768 | bytes 14168064 | tf_op jit(solution)/shard_map/hij,hjd->hid/dot_general | solution.py:24
  50.6 2.1 %convert_reduce_fusion = f32[3,1024]{1,0:T(4,128)S(1)} fusion(f32[3,1024]{1,0:T(4,128)S(1)} %get-tuple-element.11, f32[3,1024,1024]{1,2,0:T(8,128)S(1)} %get-tuple-element.12), kind=kLoop, calls=%fused_computation | loop fusion | flops 15725568 | bytes 12607488 | tf_op jit(solution)/shard_map/reduce_sum | solution.py:23
  52.7 0.6 pad_maximum_fusion.stats_ref
  53.3 38.7 %shard_map.47 = f32[16,5120]{1,0:T(8,128)} custom-call(bf16[3,8,128,128]{3,2,1,0:T(8,128)(2,1)} %bitcast.15, f32[2,3,8,128]{3,2,1,0:T(8,128)} %pad_maximum_fusion.stats_ref, bf16[384,5120]{1,0:T(8,128)(2,1)} %w_ref.1), custom_call_target="tpu_custom_call" | custom-call | tf_op jit(solution)/shard_map/pallas_call | solution.py:259
  92.0 1.7 %convert_element_type.15 = bf16[16,5120]{1,0:T(8,128)(2,1)} convert(f32[16,5120]{1,0:T(8,128)} %shard_map.47) | non-fusion elementwise | flops 81920 | bytes 491520 | tf_op jit(solution)/shard_map/convert_element_type | solution.py:301
  (1 shorter events, 0.0 us)
Async XLA Ops:
  43.4 3.3 %copy-start = (bf16[3,8,128,128]{3,2,1,0:T(8,128)(2,1)S(1)}, bf16[3,8,128,128]{3,2,1,0:T(8,128)(2,1)}, u32[]{:S(2)}) copy-start(bf16[3,8,128,128]{3,2,1,0:T(8,128)(2,1)} %get-tuple-element.10) | copy-start | bytes 2359300

commit v16 on v14

--- a/solution.py
+++ b/solution.py
@@ -73,21 +73,20 @@
                 sources[i].at[:, columns(t, h)], target(i, h), own_sems.at[i, h])
             copy.start()
             own.append(copy)
-    spread = []
+    spread = [[], [], []]
     for off in range(1, nt):
         dest = lax.rem(t + off, nt)
         for i in range(3):
             for h in range(heads):
-                spread.append(pltpu.make_async_remote_copy(
+                spread[i].append(pltpu.make_async_remote_copy(
                     src_ref=sources[i].at[:, columns(dest, h)], dst_ref=target(i, h),
                     send_sem=spread_sems.at[0, i, h, off - 1],
                     recv_sem=spread_sems.at[1, i, h, off - 1],
                     device_id=(a, z, dest), device_id_type=mesh_ids))
-    for copy in spread:
-        copy.start()
-    for copy in spread:
-        copy.wait()
-    for copy in own:
+    for group in spread:
+        for copy in group:
+            copy.start()
+    for copy in spread[0] + own[:heads]:
         copy.wait()
 
     q_copies = []
@@ -107,6 +106,8 @@
             return (chain,)
         return (0, 1)
 
+    for copy in spread[1] + own[heads:2 * heads]:
+        copy.wait()
     sent = []
     for step in range(n_steps):
         for part in range(2):
@@ -116,6 +117,9 @@
                 slot = lax.rem(z + sign * step + nz, nz)
                 if step > 0:
                     copies.pop((step - 1, part)).wait_recv()
+                elif part == 1 and chain == 0:
+                    for copy in spread[2] + own[2 * heads:]:
+                        copy.wait()
                 buf = (k_out, v_out)[part]
                 copy = pltpu.make_async_remote_copy(
                     src_ref=buf.at[:, slot], dst_ref=buf.at[:, slot],
@@ -220,27 +224,37 @@
         mine = pl.multiple_of((j * 2 + core) * rows, rows)
         pick[0, pl.ds(j * rows, rows), :] = att_buf[pl.ds(their, rows), :]
         pick[1, pl.ds(j * rows, rows), :] = att_buf[pl.ds(mine, rows), :]
-    send1[...] = jnp.dot(pick[0], w_ref[...], preferred_element_type=jnp.float32).astype(
-        jnp.bfloat16)
-    first = pltpu.make_async_remote_copy(
-        src_ref=send1, dst_ref=recv1, send_sem=sems1.at[0], recv_sem=sems1.at[1],
-        device_id=partner, device_id_type=mesh_ids)
-    first.start()
+    cols = send1.shape[1]
+    half = cols // 2
+    firsts = []
+    for k in range(2):
+        window = pl.ds(k * half, half)
+        send1[:, window] = jnp.dot(
+            pick[0], w_ref[:, window], preferred_element_type=jnp.float32).astype(jnp.bfloat16)
+        copy = pltpu.make_async_remote_copy(
+            src_ref=send1.at[:, window], dst_ref=recv1.at[:, window], send_sem=sems1.at[0, k],
+            recv_sem=sems1.at[1, k], device_id=partner, device_id_type=mesh_ids)
+        copy.start()
+        firsts.append(copy)
     total[...] = jnp.dot(pick[1], w_ref[...], preferred_element_type=jnp.float32).astype(
         jnp.bfloat16).astype(jnp.float32)
-    first.wait()
-    for j in range(n_hi):
-        block = pl.ds(j * rows, rows)
-        send2[j] = (total[block, :] + recv1[block, :].astype(jnp.float32)).astype(jnp.bfloat16)
     second = []
-    for off in range(1, n_hi):
-        dest = lax.rem(hi + off, n_hi)
-        copy = pltpu.make_async_remote_copy(
-            src_ref=send2.at[dest], dst_ref=recv2.at[off - 1], send_sem=send_sems2.at[off - 1],
-            recv_sem=recv_sems2.at[off - 1], device_id=(a, z, dest * 2 + core),
-            device_id_type=mesh_ids)
-        copy.start()
-        second.append(copy)
+    for k in range(2):
+        window = pl.ds(k * half, half)
+        firsts[k].wait()
+        for j in range(n_hi):
+            block = pl.ds(j * rows, rows)
+            send2[j, :, window] = (
+                total[block, window] + recv1[block, window].astype(jnp.float32)
+            ).astype(jnp.bfloat16)
+        for off in range(1, n_hi):
+            dest = lax.rem(hi + off, n_hi)
+            copy = pltpu.make_async_remote_copy(
+                src_ref=send2.at[dest, :, window], dst_ref=recv2.at[off - 1, :, window],
+                send_sem=send_sems2.at[0, k, off - 1], recv_sem=send_sems2.at[1, k, off - 1],
+                device_id=(a, z, dest * 2 + core), device_id_type=mesh_ids)
+            copy.start()
+            second.append(copy)
     own_rows = pl.ds(pl.multiple_of(hi * rows, rows), rows)
     own = total[own_rows, :] + recv1[own_rows, :].astype(jnp.float32)
     for copy in second:
@@ -273,9 +287,9 @@
             pltpu.VMEM((n_hi - 1, rows, cols), jnp.bfloat16),
             pltpu.SemaphoreType.DMA((2, na - 1)),
             pltpu.SemaphoreType.DMA((2, na - 1)),
-            pltpu.SemaphoreType.DMA((2,)),
-            pltpu.SemaphoreType.DMA((n_hi - 1,)),
-            pltpu.SemaphoreType.DMA((n_hi - 1,)),
+            pltpu.SemaphoreType.DMA((2, 2)),
+            pltpu.SemaphoreType.DMA((2, 2, n_hi - 1)),
+            pltpu.SemaphoreType.DMA((1,)),
             pltpu.SemaphoreType.DMA(()),
         ],
         compiler_params=pltpu.CompilerParams(collective_id=1, has_side_effects=True),

time: 93.8 us -> 91.4 us (0.974)
  Pallas kernels: 82 us -> 79.6 us
    pallas_call x1, Pallas kernels: 38.7 us -> 36.7 us  [project(): pl.pallas_call(functools.partial(project_kernel, na, n_hi), out_shape=jax...]
where the time goes in v16:
time: 91.4 us; the launch traced here: 91.2 us
  Pallas kernels  79.6 us (87%)
  matrix products  7.24 us (8%)
  other arithmetic  2.67 us (3%)
  local copies, waits for them, and re-layouts  1.6 us (2%)
    pallas_call x1, Pallas kernels, exchange(): pl.pallas_call(functools.partial(exchange_kernel, na, nz, nt), out_shape=...  42.9 us
    pallas_call x1, Pallas kernels, project(): pl.pallas_call(functools.partial(project_kernel, na, n_hi), out_shape=jax...  36.7 us
    dot_general x1, matrix products, attend_local(): jnp.einsum('hij,hjd->hid', weights_low, value_heads, preferred_element_ty...  3.99 us
    dot_general x1, matrix products, attend_local(): jnp.einsum('hid,hjd->hij', query_heads, key_heads, preferred_element_type...  3.25 us
    reduce_sum x1, other arithmetic, attend_local(): row_total = jnp.sum(weights_low.astype(jnp.float32), axis=-1)  2.06 us

profile of v16, /device:TPU:1, one launch (start us, length us, event | category | flops | bytes accessed | tf_op | source)
XLA Modules:
  0.0 91.2 jit_solution(7237538966743940383)
XLA Ops:
  0.0 42.9 %shard_map.46 = (bf16[3,8,128,128]{3,2,1,0:T(8,128)(2,1)}, bf16[3,8,128,128]{3,2,1,0:T(8,128)(2,1)}, bf16[3,8,128,128]{3,2,1,0:T(8,128)(2,1)}) custom-call(bf16[16,3072]{1,0:T(8,128)(2,1)} %q_ref.1, bf16[16,3072]{1,0:T(8,128)(2,1)} %k_ref.1, bf16[16,3072]{1,0:T(8,128)(2,1)} %v_ref.1), custom_call_target="tpu_custom_call" | custom-call | tf_op jit(solution)/shard_map/pallas_call | solution.py:146
  42.9 0.0 copy-start
  42.9 3.3 %multiply_reduce_fusion = (f32[3,1024]{1,0:T(4,128)S(1)}, f32[3,1024,1024]{1,2,0:T(8,128)S(1)}) fusion(bf16[3,1024,128]{2,1,0:T(8,128)(2,1)} %bitcast.16, bf16[3,1024,128]{2,1,0:T(8,128)(2,1)} %bitcast.17), kind=kOutput, calls=%fused_computation.2 | convolution fusion | flops 811594752 | bytes 14168064 | tf_op jit(solution)/shard_map/hid,hjd->hij/dot_general | solution.py:18
  46.2 0.0 copy-done
  46.2 4.0 %convolution_convert_fusion = bf16[3,1024,128]{2,1,0:T(8,128)(2,1)} fusion(bf16[3,1024,128]{2,1,0:T(8,128)(2,1)S(1)} %bitcast.18, f32[3,1024,1024]{1,2,0:T(8,128)S(1)} %get-tuple-element.12, f32[3,1024]{1,0:T(4,128)S(1)} %get-tuple-element.11), kind=kOutput, calls=%fused_computation.3 | convolution fusion | flops 815136768 | bytes 14168064 | tf_op jit(solution)/shard_map/hij,hjd->hid/dot_general | solution.py:24
  50.2 2.1 %convert_reduce_fusion = f32[3,1024]{1,0:T(4,128)S(1)} fusion(f32[3,1024]{1,0:T(4,128)S(1)} %get-tuple-element.11, f32[3,1024,1024]{1,2,0:T(8,128)S(1)} %get-tuple-element.12), kind=kLoop, calls=%fused_computation | loop fusion | flops 15725568 | bytes 12607488 | tf_op jit(solution)/shard_map/reduce_sum | solution.py:23
  52.2 0.6 pad_maximum_fusion.stats_ref
  52.9 36.7 %shard_map.47 = bf16[16,5120]{1,0:T(8,128)(2,1)} custom-call(bf16[3,8,128,128]{3,2,1,0:T(8,128)(2,1)} %bitcast.15, f32[2,3,8,128]{3,2,1,0:T(8,128)} %pad_maximum_fusion.stats_ref, bf16[384,5120]{1,0:T(8,128)(2,1)} %w_ref.1), custom_call_target="tpu_custom_call" | custom-call | tf_op jit(solution)/shard_map/pallas_call | solution.py:273
  89.6 1.6 %copy.12 = bf16[16,5120]{1,0:T(8,128)(2,1)} copy(bf16[16,5120]{1,0:T(8,128)(2,1)} %shard_map.47) | data formatting | bytes 327680
  (1 shorter events, 0.0 us)
Async XLA Ops:
  42.9 3.3 %copy-start = (bf16[3,8,128,128]{3,2,1,0:T(8,128)(2,1)S(1)}, bf16[3,8,128,128]{3,2,1,0:T(8,128)(2,1)}, u32[]{:S(2)}) copy-start(bf16[3,8,128,128]{3,2,1,0:T(8,128)(2,1)} %get-tuple-element.10) | copy-start | bytes 2359300

commit v17 on v16

--- a/solution.py
+++ b/solution.py
@@ -11,6 +11,7 @@
 
 HD = 128
 KEY_SPLIT = 8
+STAGE_CHUNKS = 4
 
 
 def attend_local(query_heads, key_heads, value_heads, score_scale):
@@ -225,10 +226,10 @@
         pick[0, pl.ds(j * rows, rows), :] = att_buf[pl.ds(their, rows), :]
         pick[1, pl.ds(j * rows, rows), :] = att_buf[pl.ds(mine, rows), :]
     cols = send1.shape[1]
-    half = cols // 2
+    chunk = cols // STAGE_CHUNKS
     firsts = []
-    for k in range(2):
-        window = pl.ds(k * half, half)
+    for k in range(STAGE_CHUNKS):
+        window = pl.ds(k * chunk, chunk)
         send1[:, window] = jnp.dot(
             pick[0], w_ref[:, window], preferred_element_type=jnp.float32).astype(jnp.bfloat16)
         copy = pltpu.make_async_remote_copy(
@@ -239,8 +240,8 @@
     total[...] = jnp.dot(pick[1], w_ref[...], preferred_element_type=jnp.float32).astype(
         jnp.bfloat16).astype(jnp.float32)
     second = []
-    for k in range(2):
-        window = pl.ds(k * half, half)
+    for k in range(STAGE_CHUNKS):
+        window = pl.ds(k * chunk, chunk)
         firsts[k].wait()
         for j in range(n_hi):
             block = pl.ds(j * rows, rows)
@@ -287,8 +288,8 @@
             pltpu.VMEM((n_hi - 1, rows, cols), jnp.bfloat16),
             pltpu.SemaphoreType.DMA((2, na - 1)),
             pltpu.SemaphoreType.DMA((2, na - 1)),
-            pltpu.SemaphoreType.DMA((2, 2)),
-            pltpu.SemaphoreType.DMA((2, 2, n_hi - 1)),
+            pltpu.SemaphoreType.DMA((2, STAGE_CHUNKS)),
+            pltpu.SemaphoreType.DMA((2, STAGE_CHUNKS, n_hi - 1)),
             pltpu.SemaphoreType.DMA((1,)),
             pltpu.SemaphoreType.DMA(()),
         ],

time: 91.4 us -> 91.3 us (level); the launches traced: 91.2 us -> 90.1 us
  Pallas kernels: 79.6 us -> 78.6 us
    pallas_call x1, Pallas kernels: 36.7 us -> 35.7 us  [project(): pl.pallas_call(functools.partial(project_kernel, na, n_hi), out_shape=jax...]
where the time goes in v17:
time: 91.3 us; the launch traced here: 90.1 us
  Pallas kernels  78.6 us (86%)
  matrix products  7.24 us (8%)
  other arithmetic  2.67 us (3%)
  local copies, waits for them, and re-layouts  1.6 us (2%)
    pallas_call x1, Pallas kernels, exchange(): pl.pallas_call(functools.partial(exchange_kernel, na, nz, nt), out_shape=...  42.9 us
    pallas_call x1, Pallas kernels, project(): pl.pallas_call(functools.partial(project_kernel, na, n_hi), out_shape=jax...  35.7 us
    dot_general x1, matrix products, attend_local(): jnp.einsum('hij,hjd->hid', weights_low, value_heads, preferred_element_ty...  3.99 us
    dot_general x1, matrix products, attend_local(): jnp.einsum('hid,hjd->hij', query_heads, key_heads, preferred_element_type...  3.25 us
    reduce_sum x1, other arithmetic, attend_local(): row_total = jnp.sum(weights_low.astype(jnp.float32), axis=-1)  2.06 us

profile of v17, /device:TPU:1, one launch (start us, length us, event | category | flops | bytes accessed | tf_op | source)
XLA Modules:
  0.0 90.1 jit_solution(3737302908611717267)
XLA Ops:
  0.0 42.9 %shard_map.46 = (bf16[3,8,128,128]{3,2,1,0:T(8,128)(2,1)}, bf16[3,8,128,128]{3,2,1,0:T(8,128)(2,1)}, bf16[3,8,128,128]{3,2,1,0:T(8,128)(2,1)}) custom-call(bf16[16,3072]{1,0:T(8,128)(2,1)} %q_ref.1, bf16[16,3072]{1,0:T(8,128)(2,1)} %k_ref.1, bf16[16,3072]{1,0:T(8,128)(2,1)} %v_ref.1), custom_call_target="tpu_custom_call" | custom-call | tf_op jit(solution)/shard_map/pallas_call | solution.py:147
  42.9 0.0 copy-start
  42.9 3.3 %multiply_reduce_fusion = (f32[3,1024]{1,0:T(4,128)S(1)}, f32[3,1024,1024]{1,2,0:T(8,128)S(1)}) fusion(bf16[3,1024,128]{2,1,0:T(8,128)(2,1)} %bitcast.16, bf16[3,1024,128]{2,1,0:T(8,128)(2,1)} %bitcast.17), kind=kOutput, calls=%fused_computation.2 | convolution fusion | flops 811594752 | bytes 14168064 | tf_op jit(solution)/shard_map/hid,hjd->hij/dot_general | solution.py:19
  46.2 0.0 copy-done
  46.2 4.0 %convolution_convert_fusion = bf16[3,1024,128]{2,1,0:T(8,128)(2,1)} fusion(bf16[3,1024,128]{2,1,0:T(8,128)(2,1)S(1)} %bitcast.18, f32[3,1024,1024]{1,2,0:T(8,128)S(1)} %get-tuple-element.12, f32[3,1024]{1,0:T(4,128)S(1)} %get-tuple-element.11), kind=kOutput, calls=%fused_computation.3 | convolution fusion | flops 815136768 | bytes 14168064 | tf_op jit(solution)/shard_map/hij,hjd->hid/dot_general | solution.py:25
  50.2 2.1 %convert_reduce_fusion = f32[3,1024]{1,0:T(4,128)S(1)} fusion(f32[3,1024]{1,0:T(4,128)S(1)} %get-tuple-element.11, f32[3,1024,1024]{1,2,0:T(8,128)S(1)} %get-tuple-element.12), kind=kLoop, calls=%fused_computation | loop fusion | flops 15725568 | bytes 12607488 | tf_op jit(solution)/shard_map/reduce_sum | solution.py:24
  52.2 0.6 pad_maximum_fusion.stats_ref
  52.9 35.7 %shard_map.47 = bf16[16,5120]{1,0:T(8,128)(2,1)} custom-call(bf16[3,8,128,128]{3,2,1,0:T(8,128)(2,1)} %bitcast.15, f32[2,3,8,128]{3,2,1,0:T(8,128)} %pad_maximum_fusion.stats_ref, bf16[384,5120]{1,0:T(8,128)(2,1)} %w_ref.1), custom_call_target="tpu_custom_call" | custom-call | tf_op jit(solution)/shard_map/pallas_call | solution.py:274
  88.5 1.6 %copy.12 = bf16[16,5120]{1,0:T(8,128)(2,1)} copy(bf16[16,5120]{1,0:T(8,128)(2,1)} %shard_map.47) | data formatting | bytes 327680
  (1 shorter events, 0.0 us)
Async XLA Ops:
  42.9 3.3 %copy-start = (bf16[3,8,128,128]{3,2,1,0:T(8,128)(2,1)S(1)}, bf16[3,8,128,128]{3,2,1,0:T(8,128)(2,1)}, u32[]{:S(2)}) copy-start(bf16[3,8,128,128]{3,2,1,0:T(8,128)(2,1)} %get-tuple-element.10) | copy-start | bytes 2359300

commit v18 on v17

--- a/solution.py
+++ b/solution.py
@@ -189,17 +189,28 @@
 
     own_stats = pltpu.make_async_copy(stats_ref.at[:, :, a], got_stats.at[na - 1], own_stat_sem)
     own_stats.start()
-    gathered = []
+    stat_copies = []
     for off in range(1, na):
         dest = lax.rem(a + off, na)
-        for src, dst, sems in ((parts_ref.at[:, dest], got_parts, part_sems),
-                               (stats_ref.at[:, :, dest], got_stats, stat_sems)):
+        copy = pltpu.make_async_remote_copy(
+            src_ref=stats_ref.at[:, :, dest], dst_ref=got_stats.at[off - 1],
+            send_sem=stat_sems.at[0, off - 1], recv_sem=stat_sems.at[1, off - 1],
+            device_id=(dest, z, t), device_id_type=mesh_ids)
+        copy.start()
+        stat_copies.append(copy)
+    part_copies = []
+    for h in range(heads):
+        per_head = []
+        for off in range(1, na):
+            dest = lax.rem(a + off, na)
             copy = pltpu.make_async_remote_copy(
-                src_ref=src, dst_ref=dst.at[off - 1], send_sem=sems.at[0, off - 1],
-                recv_sem=sems.at[1, off - 1], device_id=(dest, z, t), device_id_type=mesh_ids)
+                src_ref=parts_ref.at[h, dest], dst_ref=got_parts.at[off - 1, h],
+                send_sem=part_sems.at[0, h, off - 1], recv_sem=part_sems.at[1, h, off - 1],
+                device_id=(dest, z, t), device_id_type=mesh_ids)
             copy.start()
-            gathered.append(copy)
-    for copy in gathered:
+            per_head.append(copy)
+        part_copies.append(per_head)
+    for copy in stat_copies:
         copy.wait()
     own_stats.wait()
 
@@ -213,6 +224,8 @@
     for factor, part_sum in zip(factors[1:], sums[1:]):
         totals = totals + factor * part_sum
     for h in range(heads):
+        for copy in part_copies[h]:
+            copy.wait()
         numerator = parts_ref[h, a].astype(jnp.float32) * factors[0][h][:, None]
         for off in range(1, na):
             numerator = numerator + (
@@ -286,7 +299,7 @@
             pltpu.VMEM((n_hi * rows, cols), jnp.float32),
             pltpu.VMEM((n_hi, rows, cols), jnp.bfloat16),
             pltpu.VMEM((n_hi - 1, rows, cols), jnp.bfloat16),
-            pltpu.SemaphoreType.DMA((2, na - 1)),
+            pltpu.SemaphoreType.DMA((2, heads, na - 1)),
             pltpu.SemaphoreType.DMA((2, na - 1)),
             pltpu.SemaphoreType.DMA((2, STAGE_CHUNKS)),
             pltpu.SemaphoreType.DMA((2, STAGE_CHUNKS, n_hi - 1)),

time: 91.3 us -> 91.2 us (level)
  the two profiles are of different devices: /device:TPU:1 before, /device:TPU:9 now
where the time goes in v18:
time: 91.2 us; the launch traced here: 91 us
  Pallas kernels  79.4 us (87%)
  matrix products  7.24 us (8%)
  other arithmetic  2.67 us (3%)
  local copies, waits for them, and re-layouts  1.6 us (2%)
    pallas_call x1, Pallas kernels, exchange(): pl.pallas_call(functools.partial(exchange_kernel, na, nz, nt), out_shape=...  40.5 us
    pallas_call x1, Pallas kernels, project(): pl.pallas_call(functools.partial(project_kernel, na, n_hi), out_shape=jax...  39 us
    dot_general x1, matrix products, attend_local(): jnp.einsum('hij,hjd->hid', weights_low, value_heads, preferred_element_ty...  3.99 us
    dot_general x1, matrix products, attend_local(): jnp.einsum('hid,hjd->hij', query_heads, key_heads, preferred_element_type...  3.25 us
    reduce_sum x1, other arithmetic, attend_local(): row_total = jnp.sum(weights_low.astype(jnp.float32), axis=-1)  2.06 us

profile of v18, /device:TPU:9, one launch (start us, length us, event | category | flops | bytes accessed | tf_op | source)
XLA Modules:
  0.0 91.0 jit_solution(3711807923064555530)
XLA Ops:
  0.0 40.5 %shard_map.46 = (bf16[3,8,128,128]{3,2,1,0:T(8,128)(2,1)}, bf16[3,8,128,128]{3,2,1,0:T(8,128)(2,1)}, bf16[3,8,128,128]{3,2,1,0:T(8,128)(2,1)}) custom-call(bf16[16,3072]{1,0:T(8,128)(2,1)} %q_ref.1, bf16[16,3072]{1,0:T(8,128)(2,1)} %k_ref.1, bf16[16,3072]{1,0:T(8,128)(2,1)} %v_ref.1), custom_call_target="tpu_custom_call" | custom-call | tf_op jit(solution)/shard_map/pallas_call | solution.py:147
  40.5 0.0 copy-start
  40.5 3.3 %multiply_reduce_fusion = (f32[3,1024]{1,0:T(4,128)S(1)}, f32[3,1024,1024]{1,2,0:T(8,128)S(1)}) fusion(bf16[3,1024,128]{2,1,0:T(8,128)(2,1)} %bitcast.16, bf16[3,1024,128]{2,1,0:T(8,128)(2,1)} %bitcast.17), kind=kOutput, calls=%fused_computation.2 | convolution fusion | flops 811594752 | bytes 14168064 | tf_op jit(solution)/shard_map/hid,hjd->hij/dot_general | solution.py:19
  43.7 0.0 copy-done
  43.7 4.0 %convolution_convert_fusion = bf16[3,1024,128]{2,1,0:T(8,128)(2,1)} fusion(bf16[3,1024,128]{2,1,0:T(8,128)(2,1)S(1)} %bitcast.18, f32[3,1024,1024]{1,2,0:T(8,128)S(1)} %get-tuple-element.12, f32[3,1024]{1,0:T(4,128)S(1)} %get-tuple-element.11), kind=kOutput, calls=%fused_computation.3 | convolution fusion | flops 815136768 | bytes 14168064 | tf_op jit(solution)/shard_map/hij,hjd->hid/dot_general | solution.py:25
  47.7 2.1 %convert_reduce_fusion = f32[3,1024]{1,0:T(4,128)S(1)} fusion(f32[3,1024]{1,0:T(4,128)S(1)} %get-tuple-element.11, f32[3,1024,1024]{1,2,0:T(8,128)S(1)} %get-tuple-element.12), kind=kLoop, calls=%fused_computation | loop fusion | flops 15725568 | bytes 12607488 | tf_op jit(solution)/shard_map/reduce_sum | solution.py:24
  49.8 0.6 pad_maximum_fusion.stats_ref
  50.4 39.0 %shard_map.47 = bf16[16,5120]{1,0:T(8,128)(2,1)} custom-call(bf16[3,8,128,128]{3,2,1,0:T(8,128)(2,1)} %bitcast.15, f32[2,3,8,128]{3,2,1,0:T(8,128)} %pad_maximum_fusion.stats_ref, bf16[384,5120]{1,0:T(8,128)(2,1)} %w_ref.1), custom_call_target="tpu_custom_call" | custom-call | tf_op jit(solution)/shard_map/pallas_call | solution.py:287
  89.4 1.6 %copy.12 = bf16[16,5120]{1,0:T(8,128)(2,1)} copy(bf16[16,5120]{1,0:T(8,128)(2,1)} %shard_map.47) | data formatting | bytes 327680
  (1 shorter events, 0.0 us)
Async XLA Ops:
  40.5 3.3 %copy-start = (bf16[3,8,128,128]{3,2,1,0:T(8,128)(2,1)S(1)}, bf16[3,8,128,128]{3,2,1,0:T(8,128)(2,1)}, u32[]{:S(2)}) copy-start(bf16[3,8,128,128]{3,2,1,0:T(8,128)(2,1)} %get-tuple-element.10) | copy-start | bytes 2359300

commit v19 on v18

--- a/solution.py
+++ b/solution.py
@@ -21,11 +21,11 @@
     )
     row_peak = jnp.max(scores, axis=-1)
     weights_low = jnp.exp(scores - row_peak[..., None]).astype(jnp.bfloat16)
-    row_total = jnp.sum(weights_low.astype(jnp.float32), axis=-1)
+    with_ones = jnp.concatenate([value_heads, jnp.ones_like(value_heads)], axis=-1)
     weighted = jnp.einsum(
-        "hij,hjd->hid", weights_low, value_heads, preferred_element_type=jnp.float32
+        "hij,hjd->hid", weights_low, with_ones, preferred_element_type=jnp.float32
     )
-    return row_peak, row_total, weighted
+    return row_peak, weighted[..., HD], weighted[..., :HD]
 
 
 def gather_by_exchange(block, axis_name):

time: 91.2 us -> 95.1 us (1.043)
  local copies, waits for them, and re-layouts: 1.6 us -> 5.88 us
  other arithmetic: 2.67 us -> 0.61 us
  matrix products: 7.24 us -> 8.93 us
    slice x0 -> x2, local copies, waits for them, and re-layouts: none -> 4.28 us  [attend_local(): return (row_peak, weighted[..., HD], weighted[..., :HD])]
    reduce_sum x1 -> x0, other arithmetic: 2.06 us -> none  [attend_local(): row_total = jnp.sum(weights_low.astype(jnp.float32), axis=-1)]
    dot_general x1, matrix products: 3.99 us -> 5.75 us  [attend_local(): jnp.einsum('hij,hjd->hid', weights_low, with_ones, preferred_element_type...]
where the time goes in v19:
time: 95.1 us; the launch traced here: 94.8 us
  Pallas kernels  79.4 us (83%)
  matrix products  8.93 us (9%)
  local copies, waits for them, and re-layouts  5.88 us (6%)
    pallas_call x1, Pallas kernels, exchange(): pl.pallas_call(functools.partial(exchange_kernel, na, nz, nt), out_shape=...  40.5 us
    pallas_call x1, Pallas kernels, project(): pl.pallas_call(functools.partial(project_kernel, na, n_hi), out_shape=jax...  38.9 us
    dot_general x1, matrix products, attend_local(): jnp.einsum('hij,hjd->hid', weights_low, with_ones, preferred_element_type...  5.75 us
    slice x2, local copies, waits for them, and re-layouts, attend_local(): return (row_peak, weighted[..., HD], weighted[..., :HD])  4.28 us
    dot_general x1, matrix products, attend_local(): jnp.einsum('hid,hjd->hij', query_heads, key_heads, preferred_element_type...  3.18 us

profile of v19, /device:TPU:9, one launch (start us, length us, event | category | flops | bytes accessed | tf_op | source)
XLA Modules:
  0.0 94.8 jit_solution(15250294696773047423)
XLA Ops:
  0.0 40.5 %shard_map.46 = (bf16[3,8,128,128]{3,2,1,0:T(8,128)(2,1)}, bf16[3,8,128,128]{3,2,1,0:T(8,128)(2,1)}, bf16[3,8,128,128]{3,2,1,0:T(8,128)(2,1)}) custom-call(bf16[16,3072]{1,0:T(8,128)(2,1)} %q_ref.1, bf16[16,3072]{1,0:T(8,128)(2,1)} %k_ref.1, bf16[16,3072]{1,0:T(8,128)(2,1)} %v_ref.1), custom_call_target="tpu_custom_call" | custom-call | tf_op jit(solution)/shard_map/pallas_call | solution.py:147
  40.5 3.2 %multiply_reduce_fusion = (f32[3,1024]{1,0:T(4,128)S(1)}, f32[3,1024,1024]{1,2,0:T(8,128)S(1)}) fusion(bf16[3,1024,128]{2,1,0:T(8,128)(2,1)} %bitcast.18, bf16[3,1024,128]{2,1,0:T(8,128)(2,1)} %bitcast.19), kind=kOutput, calls=%fused_computation.1 | convolution fusion | flops 811594752 | bytes 14168064 | tf_op jit(solution)/shard_map/hid,hjd->hij/dot_general | solution.py:19
  43.6 5.7 %fusion = f32[3,1024,256]{2,1,0:T(8,128)} fusion(f32[3,1024,1024]{1,2,0:T(8,128)S(1)} %get-tuple-element.12, f32[3,1024]{1,0:T(4,128)S(1)} %get-tuple-element.11, bf16[3,1024,128]{2,1,0:T(8,128)(2,1)} %bitcast.22), kind=kOutput, calls=%fused_computation.2 | convolution fusion | flops 1620049920 | bytes 16527360 | tf_op jit(solution)/shard_map/hij,hjd->hid/dot_general | solution.py:25
  49.4 1.9 %slice_reduce_fusion = f32[3,1024]{1,0:T(4,128)S(1)} fusion(f32[3,1024,256]{2,1,0:T(8,128)} %fusion), kind=kLoop, calls=%fused_computation.5 | loop fusion | bytes 24576 | tf_op jit(solution)/shard_map/slice | solution.py:28
  51.3 2.4 %slice.13 = bf16[3,1024,128]{2,1,0:T(8,128)(2,1)} slice(f32[3,1024,256]{2,1,0:T(8,128)} %fusion), slice={[0:3], [0:1024], [0:128]} | slice | bytes 1572864 | tf_op jit(solution)/shard_map/slice | solution.py:28
  53.7 0.6 pad_maximum_fusion.stats_ref
  54.3 38.9 %shard_map.47 = bf16[16,5120]{1,0:T(8,128)(2,1)} custom-call(bf16[3,8,128,128]{3,2,1,0:T(8,128)(2,1)} %bitcast.17, f32[2,3,8,128]{3,2,1,0:T(8,128)} %pad_maximum_fusion.stats_ref, bf16[384,5120]{1,0:T(8,128)(2,1)} %w_ref.1), custom_call_target="tpu_custom_call" | custom-call | tf_op jit(solution)/shard_map/pallas_call | solution.py:287
  93.2 1.6 %copy.14 = bf16[16,5120]{1,0:T(8,128)(2,1)} copy(bf16[16,5120]{1,0:T(8,128)(2,1)} %shard_map.47) | data formatting | bytes 327680
  (1 shorter events, 0.0 us)

commit v20 on v18

--- a/solution.py
+++ b/solution.py
@@ -87,17 +87,18 @@
     for group in spread:
         for copy in group:
             copy.start()
-    for copy in spread[0] + own[:heads]:
-        copy.wait()
-
     q_copies = []
-    for off in range(1, na):
-        copy = pltpu.make_async_remote_copy(
-            src_ref=q_out.at[:, a], dst_ref=q_out.at[:, a], send_sem=q_sems.at[0, off - 1],
-            recv_sem=q_sems.at[1, off - 1], device_id=(lax.rem(a + off, na), z, t),
-            device_id_type=mesh_ids)
-        copy.start()
-        q_copies.append(copy)
+
+    def push_queries():
+        for copy in spread[0] + own[:heads]:
+            copy.wait()
+        for off in range(1, na):
+            copy = pltpu.make_async_remote_copy(
+                src_ref=q_out.at[:, a], dst_ref=q_out.at[:, a], send_sem=q_sems.at[0, off - 1],
+                recv_sem=q_sems.at[1, off - 1], device_id=(lax.rem(a + off, na), z, t),
+                device_id_type=mesh_ids)
+            copy.start()
+            q_copies.append(copy)
 
     n_steps = nz // 2
     chains = ((right, r_sems, -1, {}), (left, l_sems, 1, {}))
@@ -119,6 +120,7 @@
                 if step > 0:
                     copies.pop((step - 1, part)).wait_recv()
                 elif part == 1 and chain == 0:
+                    push_queries()
                     for copy in spread[2] + own[2 * heads:]:
                         copy.wait()
                 buf = (k_out, v_out)[part]

time: 91.2 us -> 91.1 us (level)
  the two profiles are of different devices: /device:TPU:9 before, /device:TPU:1 now
where the time goes in v20:
time: 91.1 us; the launch traced here: 89.5 us
  Pallas kernels  77.9 us (86%)
  matrix products  7.24 us (8%)
  other arithmetic  2.67 us (3%)
  local copies, waits for them, and re-layouts  1.6 us (2%)
    pallas_call x1, Pallas kernels, exchange(): pl.pallas_call(functools.partial(exchange_kernel, na, nz, nt), out_shape=...  42.9 us
    pallas_call x1, Pallas kernels, project(): pl.pallas_call(functools.partial(project_kernel, na, n_hi), out_shape=jax...  35 us
    dot_general x1, matrix products, attend_local(): jnp.einsum('hij,hjd->hid', weights_low, value_heads, preferred_element_ty...  3.99 us
    dot_general x1, matrix products, attend_local(): jnp.einsum('hid,hjd->hij', query_heads, key_heads, preferred_element_type...  3.25 us
    reduce_sum x1, other arithmetic, attend_local(): row_total = jnp.sum(weights_low.astype(jnp.float32), axis=-1)  2.06 us

profile of v20, /device:TPU:1, one launch (start us, length us, event | category | flops | bytes accessed | tf_op | source)
XLA Modules:
  0.0 89.5 jit_solution(17266498917640781056)
XLA Ops:
  0.0 42.9 %shard_map.46 = (bf16[3,8,128,128]{3,2,1,0:T(8,128)(2,1)}, bf16[3,8,128,128]{3,2,1,0:T(8,128)(2,1)}, bf16[3,8,128,128]{3,2,1,0:T(8,128)(2,1)}) custom-call(bf16[16,3072]{1,0:T(8,128)(2,1)} %q_ref.1, bf16[16,3072]{1,0:T(8,128)(2,1)} %k_ref.1, bf16[16,3072]{1,0:T(8,128)(2,1)} %v_ref.1), custom_call_target="tpu_custom_call" | custom-call | tf_op jit(solution)/shard_map/pallas_call | solution.py:149
  42.9 0.0 copy-start
  42.9 3.3 %multiply_reduce_fusion = (f32[3,1024]{1,0:T(4,128)S(1)}, f32[3,1024,1024]{1,2,0:T(8,128)S(1)}) fusion(bf16[3,1024,128]{2,1,0:T(8,128)(2,1)} %bitcast.16, bf16[3,1024,128]{2,1,0:T(8,128)(2,1)} %bitcast.17), kind=kOutput, calls=%fused_computation.2 | convolution fusion | flops 811594752 | bytes 14168064 | tf_op jit(solution)/shard_map/hid,hjd->hij/dot_general | solution.py:19
  46.2 0.0 copy-done
  46.2 4.0 %convolution_convert_fusion = bf16[3,1024,128]{2,1,0:T(8,128)(2,1)} fusion(bf16[3,1024,128]{2,1,0:T(8,128)(2,1)S(1)} %bitcast.18, f32[3,1024,1024]{1,2,0:T(8,128)S(1)} %get-tuple-element.12, f32[3,1024]{1,0:T(4,128)S(1)} %get-tuple-element.11), kind=kOutput, calls=%fused_computation.3 | convolution fusion | flops 815136768 | bytes 14168064 | tf_op jit(solution)/shard_map/hij,hjd->hid/dot_general | solution.py:25
  50.2 2.1 %convert_reduce_fusion = f32[3,1024]{1,0:T(4,128)S(1)} fusion(f32[3,1024]{1,0:T(4,128)S(1)} %get-tuple-element.11, f32[3,1024,1024]{1,2,0:T(8,128)S(1)} %get-tuple-element.12), kind=kLoop, calls=%fused_computation | loop fusion | flops 15725568 | bytes 12607488 | tf_op jit(solution)/shard_map/reduce_sum | solution.py:24
  52.2 0.6 pad_maximum_fusion.stats_ref
  52.9 35.0 %shard_map.47 = bf16[16,5120]{1,0:T(8,128)(2,1)} custom-call(bf16[3,8,128,128]{3,2,1,0:T(8,128)(2,1)} %bitcast.15, f32[2,3,8,128]{3,2,1,0:T(8,128)} %pad_maximum_fusion.stats_ref, bf16[384,5120]{1,0:T(8,128)(2,1)} %w_ref.1), custom_call_target="tpu_custom_call" | custom-call | tf_op jit(solution)/shard_map/pallas_call | solution.py:289
  87.9 1.6 %copy.12 = bf16[16,5120]{1,0:T(8,128)(2,1)} copy(bf16[16,5120]{1,0:T(8,128)(2,1)} %shard_map.47) | data formatting | bytes 327680
  (1 shorter events, 0.0 us)
Async XLA Ops:
  42.9 3.3 %copy-start = (bf16[3,8,128,128]{3,2,1,0:T(8,128)(2,1)S(1)}, bf16[3,8,128,128]{3,2,1,0:T(8,128)(2,1)}, u32[]{:S(2)}) copy-start(bf16[3,8,128,128]{3,2,1,0:T(8,128)(2,1)} %get-tuple-element.10) | copy-start | bytes 2359300

commit v21 on v20

--- a/solution.py
+++ b/solution.py
@@ -166,7 +166,7 @@
     )(query_vectors, key_vectors, value_vectors)
 
 
-def project_kernel(na, n_hi, parts_ref, stats_ref, w_ref, out_ref, got_parts, got_stats, att_buf,
+def project_kernel(na, n_hi, parts_ref, peak_ref, sum_ref, w_ref, out_ref, got_parts, got_stats, att_buf,
                    pick, send1, recv1, total, send2, recv2, part_sems, stat_sems, sems1, send_sems2,
                    recv_sems2, own_stat_sem):
     mesh_ids = pl.DeviceIdType.MESH
@@ -189,17 +189,23 @@
                             device_id_type=mesh_ids)
     pl.semaphore_wait(barrier, na - 1 + n_hi)
 
-    own_stats = pltpu.make_async_copy(stats_ref.at[:, :, a], got_stats.at[na - 1], own_stat_sem)
-    own_stats.start()
+    stat_refs = (peak_ref, sum_ref)
+    own_stats = []
+    for k in range(2):
+        copy = pltpu.make_async_copy(
+            stat_refs[k].at[:, a], got_stats.at[na - 1, k], own_stat_sem.at[k])
+        copy.start()
+        own_stats.append(copy)
     stat_copies = []
     for off in range(1, na):
         dest = lax.rem(a + off, na)
-        copy = pltpu.make_async_remote_copy(
-            src_ref=stats_ref.at[:, :, dest], dst_ref=got_stats.at[off - 1],
-            send_sem=stat_sems.at[0, off - 1], recv_sem=stat_sems.at[1, off - 1],
-            device_id=(dest, z, t), device_id_type=mesh_ids)
-        copy.start()
-        stat_copies.append(copy)
+        for k in range(2):
+            copy = pltpu.make_async_remote_copy(
+                src_ref=stat_refs[k].at[:, dest], dst_ref=got_stats.at[off - 1, k],
+                send_sem=stat_sems.at[0, k, off - 1], recv_sem=stat_sems.at[1, k, off - 1],
+                device_id=(dest, z, t), device_id_type=mesh_ids)
+            copy.start()
+            stat_copies.append(copy)
     part_copies = []
     for h in range(heads):
         per_head = []
@@ -212,9 +218,8 @@
             copy.start()
             per_head.append(copy)
         part_copies.append(per_head)
-    for copy in stat_copies:
+    for copy in stat_copies + own_stats:
         copy.wait()
-    own_stats.wait()
 
     peaks = [got_stats[na - 1, 0]] + [got_stats[off - 1, 0] for off in range(1, na)]
     sums = [got_stats[na - 1, 1]] + [got_stats[off - 1, 1] for off in range(1, na)]
@@ -280,7 +285,7 @@
     out_ref[...] = own.astype(out_ref.dtype)
 
 
-def project(parts, stats, out_weight, tp_count):
+def project(parts, peak, row_sum, out_weight, tp_count):
     heads, na, block_rows, _ = parts.shape
     n_hi = tp_count // 2
     rows = block_rows // tp_count
@@ -289,11 +294,11 @@
     return pl.pallas_call(
         functools.partial(project_kernel, na, n_hi),
         out_shape=jax.ShapeDtypeStruct((rows, cols), jnp.bfloat16),
-        in_specs=[vmem, vmem, vmem],
+        in_specs=[vmem, vmem, vmem, vmem],
         out_specs=vmem,
         scratch_shapes=[
             pltpu.VMEM((na - 1, heads, block_rows, HD), parts.dtype),
-            pltpu.VMEM((na, 2, heads, block_rows), stats.dtype),
+            pltpu.VMEM((na, 2, heads, block_rows), peak.dtype),
             pltpu.VMEM((block_rows, heads * HD), jnp.bfloat16),
             pltpu.VMEM((2, n_hi * rows, heads * HD), jnp.bfloat16),
             pltpu.VMEM((n_hi * rows, cols), jnp.bfloat16),
@@ -302,14 +307,14 @@
             pltpu.VMEM((n_hi, rows, cols), jnp.bfloat16),
             pltpu.VMEM((n_hi - 1, rows, cols), jnp.bfloat16),
             pltpu.SemaphoreType.DMA((2, heads, na - 1)),
-            pltpu.SemaphoreType.DMA((2, na - 1)),
+            pltpu.SemaphoreType.DMA((2, 2, na - 1)),
             pltpu.SemaphoreType.DMA((2, STAGE_CHUNKS)),
             pltpu.SemaphoreType.DMA((2, STAGE_CHUNKS, n_hi - 1)),
             pltpu.SemaphoreType.DMA((1,)),
-            pltpu.SemaphoreType.DMA(()),
+            pltpu.SemaphoreType.DMA((2,)),
         ],
         compiler_params=pltpu.CompilerParams(collective_id=1, has_side_effects=True),
-    )(parts, stats, out_weight)
+    )(parts, peak, row_sum, out_weight)
 
 
 def local(query_vectors, key_vectors, value_vectors, out_weight):
@@ -326,9 +331,10 @@
     row_peak, row_total, weighted = attend_local(
         query_heads.reshape(own_heads, -1, HD), key_heads.reshape(own_heads, -1, HD),
         value_heads.reshape(own_heads, -1, HD), score_scale)
-    stats = jnp.stack([row_peak, row_total], axis=0).reshape(2, own_heads, ca_count, block_rows)
+    peak = row_peak.reshape(own_heads, ca_count, block_rows)
+    row_sum = row_total.reshape(own_heads, ca_count, block_rows)
     parts = weighted.astype(jnp.bfloat16).reshape(own_heads, ca_count, block_rows, HD)
-    return project(parts, stats, out_weight, tp_count)
+    return project(parts, peak, row_sum, out_weight, tp_count)
 
 
 def solution(mesh):

time: 91.1 us -> 91.3 us (level)
  no operation moved by 1% of the time
where the time goes in v21:
time: 91.3 us; the launch traced here: 89.6 us
  Pallas kernels  78.1 us (86%)
  matrix products  7.24 us (8%)
  local copies, waits for them, and re-layouts  2.2 us (2%)
  other arithmetic  2.06 us (2%)
    pallas_call x1, Pallas kernels, exchange(): pl.pallas_call(functools.partial(exchange_kernel, na, nz, nt), out_shape=...  42.9 us
    pallas_call x1, Pallas kernels, project(): pl.pallas_call(functools.partial(project_kernel, na, n_hi), out_shape=jax...  35.2 us
    dot_general x1, matrix products, attend_local(): jnp.einsum('hij,hjd->hid', weights_low, value_heads, preferred_element_ty...  3.99 us
    dot_general x1, matrix products, attend_local(): jnp.einsum('hid,hjd->hij', query_heads, key_heads, preferred_element_type...  3.25 us
    reduce_sum x1, other arithmetic, attend_local(): row_total = jnp.sum(weights_low.astype(jnp.float32), axis=-1)  2.06 us

profile of v21, /device:TPU:1, one launch (start us, length us, event | category | flops | bytes accessed | tf_op | source)
XLA Modules:
  0.0 89.6 jit_solution(8458773648753866631)
XLA Ops:
  0.0 42.9 %shard_map.46 = (bf16[3,8,128,128]{3,2,1,0:T(8,128)(2,1)}, bf16[3,8,128,128]{3,2,1,0:T(8,128)(2,1)}, bf16[3,8,128,128]{3,2,1,0:T(8,128)(2,1)}) custom-call(bf16[16,3072]{1,0:T(8,128)(2,1)} %q_ref.1, bf16[16,3072]{1,0:T(8,128)(2,1)} %k_ref.1, bf16[16,3072]{1,0:T(8,128)(2,1)} %v_ref.1), custom_call_target="tpu_custom_call" | custom-call | tf_op jit(solution)/shard_map/pallas_call | solution.py:149
  42.9 0.0 copy-start
  42.9 3.3 %multiply_reduce_fusion = (f32[3,1024]{1,0:T(4,128)S(1)}, f32[3,1024,1024]{1,2,0:T(8,128)S(1)}) fusion(bf16[3,1024,128]{2,1,0:T(8,128)(2,1)} %bitcast.14, bf16[3,1024,128]{2,1,0:T(8,128)(2,1)} %bitcast.15), kind=kOutput, calls=%fused_computation.2 | convolution fusion | flops 811594752 | bytes 14168064 | tf_op jit(solution)/shard_map/hid,hjd->hij/dot_general | solution.py:19
  46.2 0.0 copy-done
  46.2 4.0 %convolution_convert_fusion = bf16[3,1024,128]{2,1,0:T(8,128)(2,1)} fusion(bf16[3,1024,128]{2,1,0:T(8,128)(2,1)S(1)} %bitcast.16, f32[3,1024,1024]{1,2,0:T(8,128)S(1)} %get-tuple-element.12, f32[3,1024]{1,0:T(4,128)S(1)} %get-tuple-element.11), kind=kOutput, calls=%fused_computation.3 | convolution fusion | flops 815136768 | bytes 14168064 | tf_op jit(solution)/shard_map/hij,hjd->hid/dot_general | solution.py:25
  50.2 2.1 %convert_reduce_fusion = f32[3,1024]{1,0:T(4,128)S(1)} fusion(f32[3,1024]{1,0:T(4,128)S(1)} %get-tuple-element.11, f32[3,1024,1024]{1,2,0:T(8,128)S(1)} %get-tuple-element.12), kind=kLoop, calls=%fused_computation | loop fusion | flops 15725568 | bytes 12607488 | tf_op jit(solution)/shard_map/reduce_sum | solution.py:24
  52.2 0.6 copy_bitcast_fusion
  52.8 35.2 %shard_map.47 = bf16[16,5120]{1,0:T(8,128)(2,1)} custom-call(bf16[3,8,128,128]{3,2,1,0:T(8,128)(2,1)} %bitcast.13, f32[3,8,128]{2,1,0:T(8,128)} %get-tuple-element.14.peak_ref, f32[3,8,128]{2,1,0:T(8,128)} %get-tuple-element.13.sum_ref, bf16[384,5120]{1,0:T(8,128)(2,1)} %w_ref.1), custom_call_target="tpu_custom_call" | custom-call | tf_op jit(solution)/shard_map/pallas_call | solution.py:294
  88.0 1.6 %copy.12 = bf16[16,5120]{1,0:T(8,128)(2,1)} copy(bf16[16,5120]{1,0:T(8,128)(2,1)} %shard_map.47) | data formatting | bytes 327680
Async XLA Ops:
  42.9 3.3 %copy-start = (bf16[3,8,128,128]{3,2,1,0:T(8,128)(2,1)S(1)}, bf16[3,8,128,128]{3,2,1,0:T(8,128)(2,1)}, u32[]{:S(2)}) copy-start(bf16[3,8,128,128]{3,2,1,0:T(8,128)(2,1)} %get-tuple-element.10) | copy-start | bytes 2359300

commit v22 on v20

--- a/solution.py
+++ b/solution.py
@@ -154,7 +154,7 @@
             jax.ShapeDtypeStruct((heads, nz, nt * rows, HD), dtype),
         ),
         in_specs=[pl.BlockSpec(memory_space=pl.ANY)] * 3,
-        out_specs=tuple(pl.BlockSpec(memory_space=pl.ANY) for _ in range(3)),
+        out_specs=tuple(pl.BlockSpec(memory_space=pltpu.VMEM) for _ in range(3)),
         scratch_shapes=[
             pltpu.SemaphoreType.DMA((2, 3, heads, nt - 1)),
             pltpu.SemaphoreType.DMA((3, heads)),

time: 91.1 us -> 92 us (level)
  no operation moved by 1% of the time
where the time goes in v22:
time: 92 us; the launch traced here: 90.3 us
  Pallas kernels  78.7 us (86%)
  matrix products  7.24 us (8%)
  other arithmetic  2.67 us (3%)
  local copies, waits for them, and re-layouts  1.6 us (2%)
    pallas_call x1, Pallas kernels, exchange(): pl.pallas_call(functools.partial(exchange_kernel, na, nz, nt), out_shape=...  43.7 us
    pallas_call x1, Pallas kernels, project(): pl.pallas_call(functools.partial(project_kernel, na, n_hi), out_shape=jax...  35.1 us
    dot_general x1, matrix products, attend_local(): jnp.einsum('hij,hjd->hid', weights_low, value_heads, preferred_element_ty...  3.99 us
    dot_general x1, matrix products, attend_local(): jnp.einsum('hid,hjd->hij', query_heads, key_heads, preferred_element_type...  3.25 us
    reduce_sum x1, other arithmetic, attend_local(): row_total = jnp.sum(weights_low.astype(jnp.float32), axis=-1)  2.06 us

profile of v22, /device:TPU:1, one launch (start us, length us, event | category | flops | bytes accessed | tf_op | source)
XLA Modules:
  0.0 90.3 jit_solution(7419804132802952728)
XLA Ops:
  0.0 43.7 %shard_map.46 = (bf16[3,8,128,128]{3,2,1,0:T(8,128)(2,1)}, bf16[3,8,128,128]{3,2,1,0:T(8,128)(2,1)}, bf16[3,8,128,128]{3,2,1,0:T(8,128)(2,1)}) custom-call(bf16[16,3072]{1,0:T(8,128)(2,1)} %q_ref.1, bf16[16,3072]{1,0:T(8,128)(2,1)} %k_ref.1, bf16[16,3072]{1,0:T(8,128)(2,1)} %v_ref.1), custom_call_target="tpu_custom_call" | custom-call | tf_op jit(solution)/shard_map/pallas_call | solution.py:149
  43.7 0.0 copy-start
  43.7 3.3 %multiply_reduce_fusion = (f32[3,1024]{1,0:T(4,128)S(1)}, f32[3,1024,1024]{1,2,0:T(8,128)S(1)}) fusion(bf16[3,1024,128]{2,1,0:T(8,128)(2,1)} %bitcast.16, bf16[3,1024,128]{2,1,0:T(8,128)(2,1)} %bitcast.17), kind=kOutput, calls=%fused_computation.2 | convolution fusion | flops 811594752 | bytes 14168064 | tf_op jit(solution)/shard_map/hid,hjd->hij/dot_general | solution.py:19
  46.9 0.0 copy-done
  47.0 4.0 %convolution_convert_fusion = bf16[3,1024,128]{2,1,0:T(8,128)(2,1)} fusion(bf16[3,1024,128]{2,1,0:T(8,128)(2,1)S(1)} %bitcast.18, f32[3,1024,1024]{1,2,0:T(8,128)S(1)} %get-tuple-element.12, f32[3,1024]{1,0:T(4,128)S(1)} %get-tuple-element.11), kind=kOutput, calls=%fused_computation.3 | convolution fusion | flops 815136768 | bytes 14168064 | tf_op jit(solution)/shard_map/hij,hjd->hid/dot_general | solution.py:25
  50.9 2.1 %convert_reduce_fusion = f32[3,1024]{1,0:T(4,128)S(1)} fusion(f32[3,1024]{1,0:T(4,128)S(1)} %get-tuple-element.11, f32[3,1024,1024]{1,2,0:T(8,128)S(1)} %get-tuple-element.12), kind=kLoop, calls=%fused_computation | loop fusion | flops 15725568 | bytes 12607488 | tf_op jit(solution)/shard_map/reduce_sum | solution.py:24
  53.0 0.6 pad_maximum_fusion.stats_ref
  53.6 35.1 %shard_map.47 = bf16[16,5120]{1,0:T(8,128)(2,1)} custom-call(bf16[3,8,128,128]{3,2,1,0:T(8,128)(2,1)} %bitcast.15, f32[2,3,8,128]{3,2,1,0:T(8,128)} %pad_maximum_fusion.stats_ref, bf16[384,5120]{1,0:T(8,128)(2,1)} %w_ref.1), custom_call_target="tpu_custom_call" | custom-call | tf_op jit(solution)/shard_map/pallas_call | solution.py:289
  88.7 1.6 %copy.12 = bf16[16,5120]{1,0:T(8,128)(2,1)} copy(bf16[16,5120]{1,0:T(8,128)(2,1)} %shard_map.47) | data formatting | bytes 327680
  (1 shorter events, 0.0 us)
Async XLA Ops:
  43.7 3.3 %copy-start = (bf16[3,8,128,128]{3,2,1,0:T(8,128)(2,1)S(1)}, bf16[3,8,128,128]{3,2,1,0:T(8,128)(2,1)}, u32[]{:S(2)}) copy-start(bf16[3,8,128,128]{3,2,1,0:T(8,128)(2,1)} %get-tuple-element.10) | copy-start | bytes 2359300

commit v23 on v20

--- a/solution.py
+++ b/solution.py
@@ -84,7 +84,7 @@
                     send_sem=spread_sems.at[0, i, h, off - 1],
                     recv_sem=spread_sems.at[1, i, h, off - 1],
                     device_id=(a, z, dest), device_id_type=mesh_ids))
-    for group in spread:
+    for group in (spread[1], spread[2], spread[0]):
         for copy in group:
             copy.start()
     q_copies = []

time: 91.1 us -> 92.3 us (1.013); the launches traced: 89.5 us -> 92.1 us
  Pallas kernels: 77.9 us -> 80.5 us
    pallas_call x1, Pallas kernels: 35 us -> 39.6 us  [project(): pl.pallas_call(functools.partial(project_kernel, na, n_hi), out_shape=jax...]
    pallas_call x1, Pallas kernels: 42.9 us -> 40.9 us  [exchange(): pl.pallas_call(functools.partial(exchange_kernel, na, nz, nt), out_shape=...]
where the time goes in v23:
time: 92.3 us; the launch traced here: 92.1 us
  Pallas kernels  80.5 us (87%)
  matrix products  7.24 us (8%)
  other arithmetic  2.67 us (3%)
  local copies, waits for them, and re-layouts  1.6 us (2%)
    pallas_call x1, Pallas kernels, exchange(): pl.pallas_call(functools.partial(exchange_kernel, na, nz, nt), out_shape=...  40.9 us
    pallas_call x1, Pallas kernels, project(): pl.pallas_call(functools.partial(project_kernel, na, n_hi), out_shape=jax...  39.6 us
    dot_general x1, matrix products, attend_local(): jnp.einsum('hij,hjd->hid', weights_low, value_heads, preferred_element_ty...  3.99 us
    dot_general x1, matrix products, attend_local(): jnp.einsum('hid,hjd->hij', query_heads, key_heads, preferred_element_type...  3.25 us
    reduce_sum x1, other arithmetic, attend_local(): row_total = jnp.sum(weights_low.astype(jnp.float32), axis=-1)  2.06 us

profile of v23, /device:TPU:1, one launch (start us, length us, event | category | flops | bytes accessed | tf_op | source)
XLA Modules:
  0.0 92.1 jit_solution(14928719944462803533)
XLA Ops:
  0.0 40.9 %shard_map.46 = (bf16[3,8,128,128]{3,2,1,0:T(8,128)(2,1)}, bf16[3,8,128,128]{3,2,1,0:T(8,128)(2,1)}, bf16[3,8,128,128]{3,2,1,0:T(8,128)(2,1)}) custom-call(bf16[16,3072]{1,0:T(8,128)(2,1)} %q_ref.1, bf16[16,3072]{1,0:T(8,128)(2,1)} %k_ref.1, bf16[16,3072]{1,0:T(8,128)(2,1)} %v_ref.1), custom_call_target="tpu_custom_call" | custom-call | tf_op jit(solution)/shard_map/pallas_call | solution.py:149
  40.9 0.0 copy-start
  40.9 3.3 %multiply_reduce_fusion = (f32[3,1024]{1,0:T(4,128)S(1)}, f32[3,1024,1024]{1,2,0:T(8,128)S(1)}) fusion(bf16[3,1024,128]{2,1,0:T(8,128)(2,1)} %bitcast.16, bf16[3,1024,128]{2,1,0:T(8,128)(2,1)} %bitcast.17), kind=kOutput, calls=%fused_computation.2 | convolution fusion | flops 811594752 | bytes 14168064 | tf_op jit(solution)/shard_map/hid,hjd->hij/dot_general | solution.py:19
  44.2 0.0 copy-done
  44.2 4.0 %convolution_convert_fusion = bf16[3,1024,128]{2,1,0:T(8,128)(2,1)} fusion(bf16[3,1024,128]{2,1,0:T(8,128)(2,1)S(1)} %bitcast.18, f32[3,1024,1024]{1,2,0:T(8,128)S(1)} %get-tuple-element.12, f32[3,1024]{1,0:T(4,128)S(1)} %get-tuple-element.11), kind=kOutput, calls=%fused_computation.3 | convolution fusion | flops 815136768 | bytes 14168064 | tf_op jit(solution)/shard_map/hij,hjd->hid/dot_general | solution.py:25
  48.2 2.1 %convert_reduce_fusion = f32[3,1024]{1,0:T(4,128)S(1)} fusion(f32[3,1024]{1,0:T(4,128)S(1)} %get-tuple-element.11, f32[3,1024,1024]{1,2,0:T(8,128)S(1)} %get-tuple-element.12), kind=kLoop, calls=%fused_computation | loop fusion | flops 15725568 | bytes 12607488 | tf_op jit(solution)/shard_map/reduce_sum | solution.py:24
  50.2 0.6 pad_maximum_fusion.stats_ref
  50.8 39.6 %shard_map.47 = bf16[16,5120]{1,0:T(8,128)(2,1)} custom-call(bf16[3,8,128,128]{3,2,1,0:T(8,128)(2,1)} %bitcast.15, f32[2,3,8,128]{3,2,1,0:T(8,128)} %pad_maximum_fusion.stats_ref, bf16[384,5120]{1,0:T(8,128)(2,1)} %w_ref.1), custom_call_target="tpu_custom_call" | custom-call | tf_op jit(solution)/shard_map/pallas_call | solution.py:289
  90.5 1.6 %copy.12 = bf16[16,5120]{1,0:T(8,128)(2,1)} copy(bf16[16,5120]{1,0:T(8,128)(2,1)} %shard_map.47) | data formatting | bytes 327680
  (1 shorter events, 0.0 us)
Async XLA Ops:
  40.9 3.3 %copy-start = (bf16[3,8,128,128]{3,2,1,0:T(8,128)(2,1)S(1)}, bf16[3,8,128,128]{3,2,1,0:T(8,128)(2,1)}, u32[]{:S(2)}) copy-start(bf16[3,8,128,128]{3,2,1,0:T(8,128)(2,1)} %get-tuple-element.10) | copy-start | bytes 2359300

commit v24 on v20

--- a/solution.py
+++ b/solution.py
@@ -263,7 +263,7 @@
             send2[j, :, window] = (
                 total[block, window] + recv1[block, window].astype(jnp.float32)
             ).astype(jnp.bfloat16)
-        for off in range(1, n_hi):
+        for off in sorted(range(1, n_hi), key=lambda o: -min(o, n_hi - o)):
             dest = lax.rem(hi + off, n_hi)
             copy = pltpu.make_async_remote_copy(
                 src_ref=send2.at[dest, :, window], dst_ref=recv2.at[off - 1, :, window],

time: 91.1 us -> 91.1 us (level)
  no operation moved by 1% of the time
where the time goes in v24:
time: 91.1 us; the launch traced here: 89.7 us
  Pallas kernels  78.1 us (86%)
  matrix products  7.24 us (8%)
  other arithmetic  2.67 us (3%)
  local copies, waits for them, and re-layouts  1.6 us (2%)
    pallas_call x1, Pallas kernels, exchange(): pl.pallas_call(functools.partial(exchange_kernel, na, nz, nt), out_shape=...  42.9 us
    pallas_call x1, Pallas kernels, project(): pl.pallas_call(functools.partial(project_kernel, na, n_hi), out_shape=jax...  35.2 us
    dot_general x1, matrix products, attend_local(): jnp.einsum('hij,hjd->hid', weights_low, value_heads, preferred_element_ty...  3.99 us
    dot_general x1, matrix products, attend_local(): jnp.einsum('hid,hjd->hij', query_heads, key_heads, preferred_element_type...  3.25 us
    reduce_sum x1, other arithmetic, attend_local(): row_total = jnp.sum(weights_low.astype(jnp.float32), axis=-1)  2.06 us

profile of v24, /device:TPU:1, one launch (start us, length us, event | category | flops | bytes accessed | tf_op | source)
XLA Modules:
  0.0 89.7 jit_solution(2612740151647750367)
XLA Ops:
  0.0 42.9 %shard_map.46 = (bf16[3,8,128,128]{3,2,1,0:T(8,128)(2,1)}, bf16[3,8,128,128]{3,2,1,0:T(8,128)(2,1)}, bf16[3,8,128,128]{3,2,1,0:T(8,128)(2,1)}) custom-call(bf16[16,3072]{1,0:T(8,128)(2,1)} %q_ref.1, bf16[16,3072]{1,0:T(8,128)(2,1)} %k_ref.1, bf16[16,3072]{1,0:T(8,128)(2,1)} %v_ref.1), custom_call_target="tpu_custom_call" | custom-call | tf_op jit(solution)/shard_map/pallas_call | solution.py:149
  42.9 0.0 copy-start
  42.9 3.3 %multiply_reduce_fusion = (f32[3,1024]{1,0:T(4,128)S(1)}, f32[3,1024,1024]{1,2,0:T(8,128)S(1)}) fusion(bf16[3,1024,128]{2,1,0:T(8,128)(2,1)} %bitcast.16, bf16[3,1024,128]{2,1,0:T(8,128)(2,1)} %bitcast.17), kind=kOutput, calls=%fused_computation.2 | convolution fusion | flops 811594752 | bytes 14168064 | tf_op jit(solution)/shard_map/hid,hjd->hij/dot_general | solution.py:19
  46.2 0.0 copy-done
  46.2 4.0 %convolution_convert_fusion = bf16[3,1024,128]{2,1,0:T(8,128)(2,1)} fusion(bf16[3,1024,128]{2,1,0:T(8,128)(2,1)S(1)} %bitcast.18, f32[3,1024,1024]{1,2,0:T(8,128)S(1)} %get-tuple-element.12, f32[3,1024]{1,0:T(4,128)S(1)} %get-tuple-element.11), kind=kOutput, calls=%fused_computation.3 | convolution fusion | flops 815136768 | bytes 14168064 | tf_op jit(solution)/shard_map/hij,hjd->hid/dot_general | solution.py:25
  50.2 2.1 %convert_reduce_fusion = f32[3,1024]{1,0:T(4,128)S(1)} fusion(f32[3,1024]{1,0:T(4,128)S(1)} %get-tuple-element.11, f32[3,1024,1024]{1,2,0:T(8,128)S(1)} %get-tuple-element.12), kind=kLoop, calls=%fused_computation | loop fusion | flops 15725568 | bytes 12607488 | tf_op jit(solution)/shard_map/reduce_sum | solution.py:24
  52.2 0.6 pad_maximum_fusion.stats_ref
  52.9 35.2 %shard_map.47 = bf16[16,5120]{1,0:T(8,128)(2,1)} custom-call(bf16[3,8,128,128]{3,2,1,0:T(8,128)(2,1)} %bitcast.15, f32[2,3,8,128]{3,2,1,0:T(8,128)} %pad_maximum_fusion.stats_ref, bf16[384,5120]{1,0:T(8,128)(2,1)} %w_ref.1), custom_call_target="tpu_custom_call" | custom-call | tf_op jit(solution)/shard_map/pallas_call | solution.py:289
  88.1 1.6 %copy.12 = bf16[16,5120]{1,0:T(8,128)(2,1)} copy(bf16[16,5120]{1,0:T(8,128)(2,1)} %shard_map.47) | data formatting | bytes 327680
  (1 shorter events, 0.0 us)
Async XLA Ops:
  42.9 3.3 %copy-start = (bf16[3,8,128,128]{3,2,1,0:T(8,128)(2,1)S(1)}, bf16[3,8,128,128]{3,2,1,0:T(8,128)(2,1)}, u32[]{:S(2)}) copy-start(bf16[3,8,128,128]{3,2,1,0:T(8,128)(2,1)} %get-tuple-element.10) | copy-start | bytes 2359300
